TPU v7x, 1024 devices: a whole 8x8x8 slice. The times are simulated.
1024 devices in a mesh: plan: 128 (over z, y, core), height: 8 (over x).
Axes of the slice: x: 8, y: 8, z: 8, core: 2. Of those that a mesh axis runs over, the one named last changes fastest.
Arguments:
- right_side: float32 [128, 8, 64, 128], P('plan', 'height'), may hold values from -6 to 6
- couplings: bfloat16 [128, 8, 3, 64, 64, 128], P('plan', 'height'), may hold values from -0.3125 to 0.3125
- neighbours: int32 [128, 8, 3, 128], P('plan', 'height'), may hold values from 0 to 639
- aggregates: int32 [128, 8, 128], P('plan', 'height'), may hold values from 0 to 15
- coarse_ops: bfloat16 [64, 64, 160], replicated, may hold values from -0.5 to 2
- coarse_smooth: bfloat16 [64, 64, 176], replicated, may hold values from -0.5 to 2
Outputs:
- solution: float32 [128, 8, 64, 128], P('plan', 'height')
All inputs are finite; a program needn't handle non-finite values.
Results may differ from a plain program's by a relative error of at most 0.0003.
Values sent between devices are 32-bit elements; how exact they have to be, the bound alone decides.
No kernel may reach another device: no remote copies, remote signals or barrier semaphores. Data moves between devices by JAX's collectives and lax.ppermute only.
A program may use at most 128 MiB of HBM per device.

v0:
```python
import functools
import math

import jax
import jax.numpy as jnp
from jax import lax
from jax.experimental import pallas as pl
from jax.experimental.pallas import tpu as pltpu
from jax.sharding import PartitionSpec as P

BS = 64
NB = 128
NC = 16
LEVELS = 10
SUB = 8
GROUPS = BS // SUB
F32 = jnp.float32
MIB = 1 << 20


def whole(count):
    return [pl.BlockSpec(memory_space=pltpu.VMEM)] * count


def call(body, out_shape, inputs, limit, scratch=()):
    several = isinstance(out_shape, (tuple, list))
    return pl.pallas_call(
        body,
        out_shape=out_shape,
        in_specs=whole(len(inputs)),
        out_specs=whole(len(out_shape)) if several else whole(1)[0],
        scratch_shapes=scratch,
        compiler_params=pltpu.CompilerParams(vmem_limit_bytes=limit),
    )(*inputs)


def iota(shape, axis):
    return lax.broadcasted_iota(jnp.int32, shape, axis)


def fold(rows):
    sub = iota((SUB, NB), 0)
    step = 1
    while len(rows) > 1:
        keep = (sub & step) == 0
        rows = [
            jnp.where(keep, a, b) + pltpu.roll(jnp.where(keep, b, a), step, 0)
            for a, b in zip(rows[0::2], rows[1::2])
        ]
        step *= 2
    return rows[0]


def take_lanes(value, index):
    return jnp.take_along_axis(value, index, axis=1, mode="promise_in_bounds")


def pick(fields, links_ref):
    picked = []
    for which in range(3):
        link = jnp.broadcast_to(links_ref[which : which + 1, :], (BS, NB))
        lane, part = link & (NB - 1), link >> 7
        value = take_lanes(fields[0], lane)
        for number in range(1, 5):
            value = jnp.where(part == number, take_lanes(fields[number], lane), value)
        picked.append(value)
    return picked


def coupled(weights_ref, picked, tile):
    rows = []
    for row in range(SUB):
        total = None
        for which in range(3):
            product = weights_ref[which, tile * SUB + row].astype(F32) * picked[which]
            for part in range(GROUPS):
                piece = product[part * SUB : (part + 1) * SUB]
                total = piece if total is None else total + piece
        rows.append(total)
    return fold(rows)


def tiles(step):
    def body(tile, carry):
        step(tile, pl.ds(pl.multiple_of(tile * SUB, SUB), SUB))
        return carry

    lax.fori_loop(0, GROUPS, body, 0)


def first_body(source, below, above, before, after, weights, links, second):
    fields = [ref[...] for ref in (source, below, above, before, after)]
    picked = pick(fields, links)

    def step(tile, rows):
        mine = source[rows, :]
        applied = 0.5 * (mine + coupled(weights, picked, tile))
        second[rows, :] = 0.5 * mine + 0.5 * (mine - applied)

    tiles(step)


def second_body(field, below, above, before, after, weights, links, source, owners, sent, left):
    fields = [ref[...] for ref in (field, below, above, before, after)]
    picked = pick(fields, links)

    def step(tile, rows):
        left[rows, :] = source[rows, :] - (field[rows, :] + coupled(weights, picked, tile))

    tiles(step)
    member = ((iota((NB, NB), 0) & (NC - 1)) == owners[...]).astype(F32)
    spread = lax.dot_general(
        left[...],
        member,
        (((1,), (1,)), ((), ())),
        precision=lax.Precision.HIGHEST,
        preferred_element_type=F32,
    )
    lane_group = iota((SUB, NB), 1) // NC
    packed = spread[0:SUB]
    for group in range(1, GROUPS):
        packed = jnp.where(lane_group == group, spread[group * SUB : (group + 1) * SUB], packed)
    packed = packed * math.sqrt(NC / NB)
    for copy in range(sent.shape[0]):
        sent[copy] = packed


def last_body(field, below, above, before, after, weights, links, source, out):
    fields = [ref[...] for ref in (field, below, above, before, after)]
    picked = pick(fields, links)

    def step(tile, rows):
        mine = field[rows, :]
        applied = mine + coupled(weights, picked, tile)
        out[rows, :] = mine + 0.5 * (source[rows, :] - applied)

    tiles(step)


def swap_blocks(values):
    group = iota((SUB, NB), 1) // NC
    values = list(values)
    for bit in (1, 2, 4):
        keep = (group & bit) == 0
        for low in range(8):
            if low & bit:
                continue
            a, b = values[low], values[low | bit]
            values[low] = jnp.where(keep, a, pltpu.roll(b, NC * bit, 1))
            values[low | bit] = jnp.where(keep, pltpu.roll(a, NB - NC * bit, 1), b)
    return values


def pack_body(ops, smooth, packed, ops_high, smooth_high):
    lane = iota((SUB, NB), 1)

    def body(number, carry):
        inner = number
        low_ops, low_smooth, high = [], [], []
        for part in range(GROUPS):
            row = part * SUB + inner
            low_ops.append(ops[row, :, 0:NB].astype(F32))
            low_smooth.append(smooth[row, :, 0:NB].astype(F32))
            ops_high[part, :, 0 : 2 * NC] = ops[row, :, NB:].astype(F32)
            smooth_high[part, :, 0 : 3 * NC] = smooth[row, :, NB:].astype(F32)
        for column in range(GROUPS):
            rows = slice(column * SUB, (column + 1) * SUB)
            place = column * SUB + inner
            for level, value in enumerate(swap_blocks([v[rows] for v in low_ops])):
                packed[level, place] = value
            for level, value in enumerate(swap_blocks([v[rows] for v in low_smooth])):
                packed[LEVELS + level, place] = value
            high = [
                jnp.where(
                    lane < 2 * NC,
                    ops_high[part, rows, :],
                    pltpu.roll(smooth_high[part, rows, :], 2 * NC, 1),
                )
                for part in range(GROUPS)
            ]
            high = swap_blocks(high)
            for level, place_of in enumerate((8, 9, LEVELS + 8, LEVELS + 9, LEVELS + 10)):
                packed[place_of, place] = high[level]
        return carry

    lax.fori_loop(0, SUB, body, 0)


def block_product(packed, number, vectors):
    lane = iota((SUB, NB), 1) & (NC - 1)
    totals = [[None] * SUB for _ in vectors]
    for column in range(GROUPS):
        spread = [take_lanes(v, lane + column * NC) for v in vectors]
        for row in range(SUB):
            weight = packed[number, column * SUB + row]
            for total, value in zip(totals, spread):
                piece = weight * value
                total[row] = piece if total[row] is None else total[row] + piece
    return [fold(total) for total in totals]


def climb(packed, first_level, received, me, kept, sent):
    count = received.shape[0].bit_length() - 1
    columns = [received[me]]
    for bits in range(1, count + 1):
        start = (me >> bits) << bits
        total = received[start]
        for other in range(1, 2**bits):
            total = total + received[start + other]
        columns.append(total * 2.0 ** (-bits / 2))
    for step in range(count):
        level = first_level + step
        smoothed = block_product(packed, LEVELS + level, columns)
        kept[2 * step] = columns[0]
        kept[2 * step + 1] = smoothed[0]
        removed = block_product(packed, level, smoothed[1:])
        columns = [a - b for a, b in zip(columns[1:], removed)]
    return columns[0]


def climb_body(first_level, axis, shift, packed, received, sent, kept):
    me = (lax.axis_index(axis) >> shift) & (received.shape[0] - 1)
    top = climb(packed, first_level, received, me, kept, sent)
    for copy in range(sent.shape[0]):
        sent[copy] = top


def turn_body(axis, packed, received, low, middle, field, owners, third, kept):
    first_level = LEVELS - (received.shape[0].bit_length() - 1)
    top = climb(packed, first_level, received, lax.axis_index(axis), kept, None)
    (error,) = block_product(packed, 2 * LEVELS, [top])
    low_levels = low.shape[0] // 2
    for level in reversed(range(LEVELS)):
        if level >= first_level:
            saved, place = kept, level - first_level
        elif level >= low_levels:
            saved, place = middle, level - low_levels
        else:
            saved, place = low, level
        error = saved[2 * place + 1] + error
        (applied,) = block_product(packed, level, [error])
        (fixed,) = block_product(packed, LEVELS + level, [saved[2 * place] - applied])
        error = error + fixed
    owner = jnp.broadcast_to(owners[...], (SUB, NB))
    for group in range(GROUPS):
        rows = slice(group * SUB, (group + 1) * SUB)
        third[rows, :] = field[rows, :] + take_lanes(error, owner + group * NC)


def shifted(value, axis, step):
    count = lax.axis_size(axis)
    pairs = [(i, i + step) for i in range(count) if 0 <= i + step < count]
    return lax.ppermute(value, axis, pairs)


def halo(value):
    return (
        shifted(value, "height", 1),
        shifted(value, "height", -1),
        shifted(value, "plan", 1),
        shifted(value, "plan", -1),
    )


def exchange(value, axis, groups=None):
    return lax.all_to_all(value, axis, 0, 0, axis_index_groups=groups, tiled=True)


def shards(right_side, couplings, neighbours, aggregates, coarse_ops, coarse_smooth):
    source = right_side[0, 0]
    weights = couplings[0, 0]
    links = neighbours[0, 0]
    owners = aggregates[0]
    plan = lax.axis_size("plan")
    height = lax.axis_size("height")
    height_bits = height.bit_length() - 1
    plan_bits = plan.bit_length() - 1
    low_bits = (plan_bits + 1) // 2
    near = 2**low_bits
    far = plan // near
    field_shape = jax.ShapeDtypeStruct((BS, NB), F32)

    def vectors(count):
        return jax.ShapeDtypeStruct((count, SUB, NB), F32)

    packed = call(
        pack_body,
        jax.ShapeDtypeStruct((2 * LEVELS + 1, BS, SUB, NB), F32),
        (coarse_ops, coarse_smooth),
        24 * MIB,
        [pltpu.VMEM((GROUPS, BS, NB), F32)] * 2,
    )
    second = call(
        first_body, field_shape, (source, *halo(source), weights, links), 12 * MIB
    )
    sent = call(
        second_body,
        vectors(near),
        (second, *halo(second), weights, links, source, owners),
        12 * MIB,
        [pltpu.VMEM((BS, NB), F32)],
    )
    near_groups = [[a * near + b for b in range(near)] for a in range(far)]
    far_groups = [[a * near + b for a in range(far)] for b in range(near)]
    received = exchange(sent, "plan", near_groups)
    sent, low = call(
        functools.partial(climb_body, 0, "plan", 0),
        (vectors(far), vectors(2 * low_bits)),
        (packed, received),
        16 * MIB,
    )
    received = exchange(sent, "plan", far_groups)
    sent, middle = call(
        functools.partial(climb_body, low_bits, "plan", low_bits),
        (vectors(height), vectors(2 * (plan_bits - low_bits))),
        (packed, received),
        16 * MIB,
    )
    received = exchange(sent, "height")
    third = call(
        functools.partial(turn_body, "height"),
        field_shape,
        (packed, received, low, middle, second, owners),
        16 * MIB,
        [pltpu.VMEM((2 * height_bits, SUB, NB), F32)],
    )
    out = call(
        last_body, field_shape, (third, *halo(third), weights, links, source), 12 * MIB
    )
    return out[None, None]


def solution(mesh):
    in_specs = (
        P("plan", "height", None, None),
        P("plan", "height", None, None, None, None),
        P("plan", "height", None, None),
        P("plan", "height", None),
        P(),
        P(),
    )
    out_specs = P("plan", "height", None, None)
    return jax.shard_map(shards, mesh=mesh, in_specs=in_specs, out_specs=out_specs, check_vma=False)
```

profile of v0, /device:TPU:51, one launch (start us, length us, event | category | flops | bytes accessed | tf_op | source)
XLA Modules:
  0.0 127.7 jit_solution(6907715485778107269)
XLA Ops:
  0.0 0.0 copy-start.8
  0.0 2.7 %collective-permute-start.3 = (f32[64,128]{1,0:T(8,128)}, f32[64,128]{1,0:T(8,128)S(1)}, u32[]{:S(2)}, u32[]{:S(2)}) collective-permute-start(f32[64,128]{1,0:T(8,128)} %bitcast.10), channel_id=1, source_target_pairs={{8,0},{16,8},{24,16},{32,24},{40,32},{48,40},{56,48},{64,56},{72,6... | collective-permute-start | bytes 98312 | tf_op jit(solution)/shard_map/ppermute | solution.py:253
  2.7 4.4 %collective-permute-start.2 = (f32[64,128]{1,0:T(8,128)}, f32[64,128]{1,0:T(8,128)S(1)}, u32[]{:S(2)}, u32[]{:S(2)}) collective-permute-start(f32[64,128]{1,0:T(8,128)} %bitcast.11), channel_id=1, source_target_pairs={{0,8},{8,16},{16,24},{24,32},{32,40},{40,48},{48,56},{56,64},{64,7... | collective-permute-start | bytes 98312 | tf_op jit(solution)/shard_map/ppermute | solution.py:253
  7.2 2.2 %collective-permute-start.1 = (f32[64,128]{1,0:T(8,128)}, f32[64,128]{1,0:T(8,128)S(1)}, u32[]{:S(2)}, u32[]{:S(2)}) collective-permute-start(f32[64,128]{1,0:T(8,128)} %bitcast.12), channel_id=1, source_target_pairs={{1,0},{2,1},{3,2},{4,3},{5,4},{6,5},{7,6},{9,8},{10,9},{11,10},{12... | collective-permute-start | bytes 98312 | tf_op jit(solution)/shard_map/ppermute | solution.py:253
  9.3 3.1 %collective-permute-start = (f32[64,128]{1,0:T(8,128)}, f32[64,128]{1,0:T(8,128)S(1)}, u32[]{:S(2)}, u32[]{:S(2)}) collective-permute-start(f32[64,128]{1,0:T(8,128)} %bitcast.13), channel_id=1, source_target_pairs={{0,1},{1,2},{2,3},{3,4},{4,5},{5,6},{6,7},{8,9},{9,10},{10,11},{11... | collective-permute-start | bytes 98312 | tf_op jit(solution)/shard_map/ppermute | solution.py:253
  12.5 0.7 copy.9
  13.1 0.0 collective-permute-done.3.after
  13.1 0.0 collective-permute-done.2.before
  13.1 0.0 collective-permute-done.1.above
  13.2 1.0 collective-permute-done.below
  14.2 1.9 %copy-done.2 = bf16[1,1,3,64,64,128]{5,4,3,2,1,0:T(8,128)(2,1)S(1)} copy-done((bf16[1,1,3,64,64,128]{5,4,3,2,1,0:T(8,128)(2,1)S(1)}, bf16[1,1,3,64,64,128]{5,4,3,2,1,0:T(8,128)(2,1)}, u32[]{:S(2)}) %copy-start.2) | copy-done | bytes 3145752
  16.1 0.8 copy-done.6
  16.8 1.0 shard_map.65.field
  17.8 1.9 %collective-permute-start.7 = (f32[64,128]{1,0:T(8,128)S(1)}, f32[64,128]{1,0:T(8,128)S(1)}, u32[]{:S(2)}, u32[]{:S(2)}) collective-permute-start(f32[64,128]{1,0:T(8,128)S(1)} %shard_map.65.field), channel_id=1, source_target_pairs={{8,0},{16,8},{24,16},{32,24},{40,32},{48,40},{56,48},{64,56},{72,6... | collective-permute-start | bytes 98312 | tf_op jit(solution)/shard_map/ppermute | solution.py:253
  19.7 4.9 %collective-permute-start.6 = (f32[64,128]{1,0:T(8,128)S(1)}, f32[64,128]{1,0:T(8,128)S(1)}, u32[]{:S(2)}, u32[]{:S(2)}) collective-permute-start(f32[64,128]{1,0:T(8,128)S(1)} %shard_map.65.field), channel_id=1, source_target_pairs={{0,8},{8,16},{16,24},{24,32},{32,40},{40,48},{48,56},{56,64},{64,7... | collective-permute-start | bytes 98312 | tf_op jit(solution)/shard_map/ppermute | solution.py:253
  24.6 1.9 %collective-permute-start.5 = (f32[64,128]{1,0:T(8,128)S(1)}, f32[64,128]{1,0:T(8,128)S(1)}, u32[]{:S(2)}, u32[]{:S(2)}) collective-permute-start(f32[64,128]{1,0:T(8,128)S(1)} %shard_map.65.field), channel_id=1, source_target_pairs={{1,0},{2,1},{3,2},{4,3},{5,4},{6,5},{7,6},{9,8},{10,9},{11,10},{12... | collective-permute-start | bytes 98312 | tf_op jit(solution)/shard_map/ppermute | solution.py:253
  26.5 3.4 %collective-permute-start.4 = (f32[64,128]{1,0:T(8,128)S(1)}, f32[64,128]{1,0:T(8,128)S(1)}, u32[]{:S(2)}, u32[]{:S(2)}) collective-permute-start(f32[64,128]{1,0:T(8,128)S(1)} %shard_map.65.field), channel_id=1, source_target_pairs={{0,1},{1,2},{2,3},{3,4},{4,5},{5,6},{6,7},{8,9},{9,10},{10,11},{11... | collective-permute-start | bytes 98312 | tf_op jit(solution)/shard_map/ppermute | solution.py:253
  29.9 0.0 collective-permute-done.7.after
  29.9 0.0 collective-permute-done.6.before
  29.9 0.0 collective-permute-done.5.above
  29.9 1.3 collective-permute-done.4.below
  31.2 0.0 copy-done.8
  31.2 0.0 copy-done.3
  31.2 1.8 %shard_map.66 = f32[16,8,128]{2,1,0:T(8,128)} custom-call(f32[64,128]{1,0:T(8,128)S(1)} %shard_map.65.field, f32[64,128]{1,0:T(8,128)S(1)} %collective-permute-done.4.below, f32[64,128]{1,0:T(8,128)S(1)} %collective-permute-done.5.above, f32[64,128]{1,0:T(8,128)S(1)} %collective-permute-done.6.before, f32[64,128]{1,0:T(8,128)S(1)} %collective-permute-done.7.after, ...), custom_call_target="tpu_custom_call" | custom-call | tf_op jit(solution)/shard_map/pallas_call | solution.py:27
  33.0 13.6 %all-to-all-start = ((f32[16,8,128]{2,1,0:T(8,128)}), f32[16,8,128]{2,1,0:T(8,128)S(1)}, u32[]{:S(2)}, u32[]{:S(2)}) async-start(f32[16,8,128]{2,1,0:T(8,128)} %shard_map.66), calls=%async_computation | async-start | bytes 131072 | tf_op jit(solution)/shard_map/all_to_all | solution.py:266
  46.6 1.6 %copy-done.4 = bf16[64,64,160]{2,1,0:T(8,128)(2,1)S(1)} copy-done((bf16[64,64,160]{2,1,0:T(8,128)(2,1)S(1)}, bf16[64,64,160]{2,1,0:T(8,128)(2,1)}, u32[]{:S(2)}) %copy-start.4) | copy-done | bytes 1310744
  48.2 1.6 %copy-done.5 = bf16[64,64,176]{2,1,0:T(8,128)(2,1)S(1)} copy-done((bf16[64,64,176]{2,1,0:T(8,128)(2,1)S(1)}, bf16[64,64,176]{2,1,0:T(8,128)(2,1)}, u32[]{:S(2)}) %copy-start.5) | copy-done | bytes 1441816
  49.8 19.6 %shard_map.64.packed = f32[21,64,8,128]{3,2,1,0:T(8,128)S(1)} custom-call(bf16[64,64,160]{2,1,0:T(8,128)(2,1)S(1)} %copy-done.4, bf16[64,64,176]{2,1,0:T(8,128)(2,1)S(1)} %copy-done.5), custom_call_target="tpu_custom_call" | custom-call | tf_op jit(solution)/shard_map/pallas_call | solution.py:27
  69.4 0.0 copy-start
  69.4 2.4 %copy-done = f32[21,64,8,128]{3,2,1,0:T(8,128)} copy-done((f32[21,64,8,128]{3,2,1,0:T(8,128)}, f32[21,64,8,128]{3,2,1,0:T(8,128)S(1)}, u32[]{:S(2)}) %copy-start) | copy-done | bytes 5505048
  71.8 0.0 all-to-all-done.received
  71.8 2.6 %copy-done.1 = f32[21,64,8,128]{3,2,1,0:T(8,128)S(1)} copy-done((f32[21,64,8,128]{3,2,1,0:T(8,128)S(1)}, f32[21,64,8,128]{3,2,1,0:T(8,128)}, u32[]{:S(2)}) %copy-start.1) | copy-done | bytes 5505048
  74.3 1.0 shard_map.67
  75.3 15.5 %all_to_all.15.received = f32[8,8,128]{2,1,0:T(8,128)S(1)} all-to-all(f32[8,8,128]{2,1,0:T(8,128)S(1)} %get-tuple-element.9), channel_id=1, replica_groups={{0,128,256,384,512,640,768,896},{8,136,264,392,520,648,776,904},{16,144..., dimensions={0} | all-to-all | bytes 65536 | tf_op jit(solution)/shard_map/all_to_all | solution.py:266
  90.8 0.7 shard_map.68
  91.5 0.0 copy-start.7
  91.5 14.6 %all_to_all.16.received = f32[8,8,128]{2,1,0:T(8,128)S(1)} all-to-all(f32[8,8,128]{2,1,0:T(8,128)S(1)} %get-tuple-element.10), channel_id=1, replica_groups=mesh['plan'=128,'height'=8] {'height'}, dimensions={0} | all-to-all | bytes 65536 | tf_op jit(solution)/shard_map/all_to_all | solution.py:266
  106.2 2.9 %shard_map.69.field = f32[64,128]{1,0:T(8,128)S(1)} custom-call(f32[21,64,8,128]{3,2,1,0:T(8,128)S(1)} %copy-done.1, f32[8,8,128]{2,1,0:T(8,128)S(1)} %all_to_all.16.received, f32[8,8,128]{2,1,0:T(8,128)S(1)} %get-tuple-element.11.low, f32[6,8,128]{2,1,0:T(8,128)S(1)} %get-tuple-element.12.middle, f32[64,128]{1,0:T(8,128)S(1)} %shard_map.65.field, ...), custom_call_target="tpu_custom_call" | custom-call | tf_op jit(solution)/shard_map/pallas_call | solution.py:27
  109.1 5.1 %collective-permute-start.11 = (f32[64,128]{1,0:T(8,128)S(1)}, f32[64,128]{1,0:T(8,128)S(1)}, u32[]{:S(2)}, u32[]{:S(2)}) collective-permute-start(f32[64,128]{1,0:T(8,128)S(1)} %shard_map.69.field), channel_id=1, source_target_pairs={{8,0},{16,8},{24,16},{32,24},{40,32},{48,40},{56,48},{64,56},{72,6... | collective-permute-start | bytes 98312 | tf_op jit(solution)/shard_map/ppermute | solution.py:253
  114.1 4.2 %collective-permute-start.10 = (f32[64,128]{1,0:T(8,128)S(1)}, f32[64,128]{1,0:T(8,128)S(1)}, u32[]{:S(2)}, u32[]{:S(2)}) collective-permute-start(f32[64,128]{1,0:T(8,128)S(1)} %shard_map.69.field), channel_id=1, source_target_pairs={{0,8},{8,16},{16,24},{24,32},{32,40},{40,48},{48,56},{56,64},{64,7... | collective-permute-start | bytes 98312 | tf_op jit(solution)/shard_map/ppermute | solution.py:253
  118.3 3.1 %collective-permute-start.9 = (f32[64,128]{1,0:T(8,128)S(1)}, f32[64,128]{1,0:T(8,128)S(1)}, u32[]{:S(2)}, u32[]{:S(2)}) collective-permute-start(f32[64,128]{1,0:T(8,128)S(1)} %shard_map.69.field), channel_id=1, source_target_pairs={{1,0},{2,1},{3,2},{4,3},{5,4},{6,5},{7,6},{9,8},{10,9},{11,10},{12... | collective-permute-start | bytes 98312 | tf_op jit(solution)/shard_map/ppermute | solution.py:253
  121.4 2.2 %collective-permute-start.8 = (f32[64,128]{1,0:T(8,128)S(1)}, f32[64,128]{1,0:T(8,128)S(1)}, u32[]{:S(2)}, u32[]{:S(2)}) collective-permute-start(f32[64,128]{1,0:T(8,128)S(1)} %shard_map.69.field), channel_id=1, source_target_pairs={{0,1},{1,2},{2,3},{3,4},{4,5},{5,6},{6,7},{8,9},{9,10},{10,11},{11... | collective-permute-start | bytes 98312 | tf_op jit(solution)/shard_map/ppermute | solution.py:253
  123.6 0.0 collective-permute-done.11.after
  123.7 0.0 collective-permute-done.10.before
  123.7 0.0 collective-permute-done.9.above
  123.7 2.4 %collective-permute-done.8.below = f32[64,128]{1,0:T(8,128)S(1)} collective-permute-done((f32[64,128]{1,0:T(8,128)S(1)}, f32[64,128]{1,0:T(8,128)S(1)}, u32[]{:S(2)}, u32[]{:S(2)}) %collective-permute-start.8) | collective-permute-done | bytes 32800 | tf_op jit(solution)/shard_map/ppermute | solution.py:253
  126.1 0.0 copy-done.7
  126.1 1.6 %shard_map.70 = f32[64,128]{1,0:T(8,128)} custom-call(f32[64,128]{1,0:T(8,128)S(1)} %shard_map.69.field, f32[64,128]{1,0:T(8,128)S(1)} %collective-permute-done.8.below, f32[64,128]{1,0:T(8,128)S(1)} %collective-permute-done.9.above, f32[64,128]{1,0:T(8,128)S(1)} %collective-permute-done.10.before, f32[64,128]{1,0:T(8,128)S(1)} %collective-permute-done.11.after, ...), custom_call_target="tpu_custom_call" | custom-call | tf_op jit(solution)/shard_map/pallas_call | solution.py:27
  (6 shorter events, 0.0 us)
Async XLA Ops:
  0.0 31.2 %copy-start.8 = (s32[1,1,128]{2,1,0:T(1,128)S(1)}, s32[1,1,128]{2,1,0:T(1,128)}, u32[]{:S(2)}) copy-start(s32[1,1,128]{2,1,0:T(1,128)} %param.9) | copy-start | bytes 1540
  0.0 13.1 %collective-permute-start.3 = (f32[64,128]{1,0:T(8,128)}, f32[64,128]{1,0:T(8,128)S(1)}, u32[]{:S(2)}, u32[]{:S(2)}) collective-permute-start(f32[64,128]{1,0:T(8,128)} %bitcast.10), channel_id=1, source_target_pairs={{8,0},{16,8},{24,16},{32,24},{40,32},{48,40},{56,48},{64,56},{72,6... | collective-permute-start | bytes 98312 | tf_op jit(solution)/shard_map/ppermute | solution.py:253
  2.7 10.4 %collective-permute-start.2 = (f32[64,128]{1,0:T(8,128)}, f32[64,128]{1,0:T(8,128)S(1)}, u32[]{:S(2)}, u32[]{:S(2)}) collective-permute-start(f32[64,128]{1,0:T(8,128)} %bitcast.11), channel_id=1, source_target_pairs={{0,8},{8,16},{16,24},{24,32},{32,40},{40,48},{48,56},{56,64},{64,7... | collective-permute-start | bytes 98312 | tf_op jit(solution)/shard_map/ppermute | solution.py:253
  7.2 6.0 %collective-permute-start.1 = (f32[64,128]{1,0:T(8,128)}, f32[64,128]{1,0:T(8,128)S(1)}, u32[]{:S(2)}, u32[]{:S(2)}) collective-permute-start(f32[64,128]{1,0:T(8,128)} %bitcast.12), channel_id=1, source_target_pairs={{1,0},{2,1},{3,2},{4,3},{5,4},{6,5},{7,6},{9,8},{10,9},{11,10},{12... | collective-permute-start | bytes 98312 | tf_op jit(solution)/shard_map/ppermute | solution.py:253
  9.3 4.9 %collective-permute-start = (f32[64,128]{1,0:T(8,128)}, f32[64,128]{1,0:T(8,128)S(1)}, u32[]{:S(2)}, u32[]{:S(2)}) collective-permute-start(f32[64,128]{1,0:T(8,128)} %bitcast.13), channel_id=1, source_target_pairs={{0,1},{1,2},{2,3},{3,4},{4,5},{5,6},{6,7},{8,9},{9,10},{10,11},{11... | collective-permute-start | bytes 98312 | tf_op jit(solution)/shard_map/ppermute | solution.py:253
  14.2 1.9 %copy-start.2 = (bf16[1,1,3,64,64,128]{5,4,3,2,1,0:T(8,128)(2,1)S(1)}, bf16[1,1,3,64,64,128]{5,4,3,2,1,0:T(8,128)(2,1)}, u32[]{:S(2)}) copy-start(bf16[1,1,3,64,64,128]{5,4,3,2,1,0:T(8,128)(2,1)} %param.7) | copy-start | bytes 9437188
  16.1 0.8 copy-start.6
  16.8 14.4 %copy-start.3 = (bf16[1,1,3,64,64,128]{5,4,3,2,1,0:T(8,128)(2,1)S(1)}, bf16[1,1,3,64,64,128]{5,4,3,2,1,0:T(8,128)(2,1)}, u32[]{:S(2)}) copy-start(bf16[1,1,3,64,64,128]{5,4,3,2,1,0:T(8,128)(2,1)} %param.7) | copy-start | bytes 9437188
  17.8 12.1 %collective-permute-start.7 = (f32[64,128]{1,0:T(8,128)S(1)}, f32[64,128]{1,0:T(8,128)S(1)}, u32[]{:S(2)}, u32[]{:S(2)}) collective-permute-start(f32[64,128]{1,0:T(8,128)S(1)} %shard_map.65.field), channel_id=1, source_target_pairs={{8,0},{16,8},{24,16},{32,24},{40,32},{48,40},{56,48},{64,56},{72,6... | collective-permute-start | bytes 98312 | tf_op jit(solution)/shard_map/ppermute | solution.py:253
  19.7 10.2 %collective-permute-start.6 = (f32[64,128]{1,0:T(8,128)S(1)}, f32[64,128]{1,0:T(8,128)S(1)}, u32[]{:S(2)}, u32[]{:S(2)}) collective-permute-start(f32[64,128]{1,0:T(8,128)S(1)} %shard_map.65.field), channel_id=1, source_target_pairs={{0,8},{8,16},{16,24},{24,32},{32,40},{40,48},{48,56},{56,64},{64,7... | collective-permute-start | bytes 98312 | tf_op jit(solution)/shard_map/ppermute | solution.py:253
  24.6 5.3 %collective-permute-start.5 = (f32[64,128]{1,0:T(8,128)S(1)}, f32[64,128]{1,0:T(8,128)S(1)}, u32[]{:S(2)}, u32[]{:S(2)}) collective-permute-start(f32[64,128]{1,0:T(8,128)S(1)} %shard_map.65.field), channel_id=1, source_target_pairs={{1,0},{2,1},{3,2},{4,3},{5,4},{6,5},{7,6},{9,8},{10,9},{11,10},{12... | collective-permute-start | bytes 98312 | tf_op jit(solution)/shard_map/ppermute | solution.py:253
  26.5 4.7 %collective-permute-start.4 = (f32[64,128]{1,0:T(8,128)S(1)}, f32[64,128]{1,0:T(8,128)S(1)}, u32[]{:S(2)}, u32[]{:S(2)}) collective-permute-start(f32[64,128]{1,0:T(8,128)S(1)} %shard_map.65.field), channel_id=1, source_target_pairs={{0,1},{1,2},{2,3},{3,4},{4,5},{5,6},{6,7},{8,9},{9,10},{10,11},{11... | collective-permute-start | bytes 98312 | tf_op jit(solution)/shard_map/ppermute | solution.py:253
  33.0 38.8 %all-to-all-start = ((f32[16,8,128]{2,1,0:T(8,128)}), f32[16,8,128]{2,1,0:T(8,128)S(1)}, u32[]{:S(2)}, u32[]{:S(2)}) async-start(f32[16,8,128]{2,1,0:T(8,128)} %shard_map.66), calls=%async_computation | async-start | bytes 131072 | tf_op jit(solution)/shard_map/all_to_all | solution.py:266
  46.6 1.6 %copy-start.4 = (bf16[64,64,160]{2,1,0:T(8,128)(2,1)S(1)}, bf16[64,64,160]{2,1,0:T(8,128)(2,1)}, u32[]{:S(2)}) copy-start(bf16[64,64,160]{2,1,0:T(8,128)(2,1)} %ops.1) | copy-start | bytes 3932164
  48.2 1.6 %copy-start.5 = (bf16[64,64,176]{2,1,0:T(8,128)(2,1)S(1)}, bf16[64,64,176]{2,1,0:T(8,128)(2,1)}, u32[]{:S(2)}) copy-start(bf16[64,64,176]{2,1,0:T(8,128)(2,1)} %smooth.1) | copy-start | bytes 4325380
  69.4 2.4 %copy-start = (f32[21,64,8,128]{3,2,1,0:T(8,128)}, f32[21,64,8,128]{3,2,1,0:T(8,128)S(1)}, u32[]{:S(2)}) copy-start(f32[21,64,8,128]{3,2,1,0:T(8,128)S(1)} %shard_map.64.packed) | copy-start | bytes 16515076
  71.8 2.6 %copy-start.1 = (f32[21,64,8,128]{3,2,1,0:T(8,128)S(1)}, f32[21,64,8,128]{3,2,1,0:T(8,128)}, u32[]{:S(2)}) copy-start(f32[21,64,8,128]{3,2,1,0:T(8,128)} %copy-done) | copy-start | bytes 16515076
  91.5 34.6 %copy-start.7 = (f32[1,1,64,128]{3,2,1,0:T(8,128)S(1)}, f32[1,1,64,128]{3,2,1,0:T(8,128)}, u32[]{:S(2)}) copy-start(f32[1,1,64,128]{3,2,1,0:T(8,128)} %param.6) | copy-start | bytes 98308
  109.1 14.6 %collective-permute-start.11 = (f32[64,128]{1,0:T(8,128)S(1)}, f32[64,128]{1,0:T(8,128)S(1)}, u32[]{:S(2)}, u32[]{:S(2)}) collective-permute-start(f32[64,128]{1,0:T(8,128)S(1)} %shard_map.69.field), channel_id=1, source_target_pairs={{8,0},{16,8},{24,16},{32,24},{40,32},{48,40},{56,48},{64,56},{72,6... | collective-permute-start | bytes 98312 | tf_op jit(solution)/shard_map/ppermute | solution.py:253
  114.1 9.5 %collective-permute-start.10 = (f32[64,128]{1,0:T(8,128)S(1)}, f32[64,128]{1,0:T(8,128)S(1)}, u32[]{:S(2)}, u32[]{:S(2)}) collective-permute-start(f32[64,128]{1,0:T(8,128)S(1)} %shard_map.69.field), channel_id=1, source_target_pairs={{0,8},{8,16},{16,24},{24,32},{32,40},{40,48},{48,56},{56,64},{64,7... | collective-permute-start | bytes 98312 | tf_op jit(solution)/shard_map/ppermute | solution.py:253
  118.3 5.3 %collective-permute-start.9 = (f32[64,128]{1,0:T(8,128)S(1)}, f32[64,128]{1,0:T(8,128)S(1)}, u32[]{:S(2)}, u32[]{:S(2)}) collective-permute-start(f32[64,128]{1,0:T(8,128)S(1)} %shard_map.69.field), channel_id=1, source_target_pairs={{1,0},{2,1},{3,2},{4,3},{5,4},{6,5},{7,6},{9,8},{10,9},{11,10},{12... | collective-permute-start | bytes 98312 | tf_op jit(solution)/shard_map/ppermute | solution.py:253
  121.4 4.7 %collective-permute-start.8 = (f32[64,128]{1,0:T(8,128)S(1)}, f32[64,128]{1,0:T(8,128)S(1)}, u32[]{:S(2)}, u32[]{:S(2)}) collective-permute-start(f32[64,128]{1,0:T(8,128)S(1)} %shard_map.69.field), channel_id=1, source_target_pairs={{0,1},{1,2},{2,3},{3,4},{4,5},{5,6},{6,7},{8,9},{9,10},{10,11},{11... | collective-permute-start | bytes 98312 | tf_op jit(solution)/shard_map/ppermute | solution.py:253
where the time goes:
time: 128 us
  starting transfers between devices  52.6 us (41%)
  blocking collectives  30.1 us (24%)
  Pallas kernels  28.5 us (22%)
  local copies, waits for them, and re-layouts  11.5 us (9%)
  waiting for transfers between devices  4.76 us (4%)
    ppermute x12, starting transfers between devices, shifted(): return lax.ppermute(value, axis, pairs)  39 us
    all_to_all x2, blocking collectives, exchange(): lax.all_to_all(value, axis, 0, 0, axis_index_groups=groups, tiled=True)  30.1 us
    pallas_call x7, Pallas kernels, call(): pl.pallas_call(body, out_shape=out_shape, in_specs=whole(len(inputs)), ou...  28.5 us
    all_to_all x1, starting transfers between devices, exchange(): lax.all_to_all(value, axis, 0, 0, axis_index_groups=groups, tiled=True)  13.6 us
    unnamed x19, local copies, waits for them, and re-layouts  11.5 us
    ppermute x12, waiting for transfers between devices, shifted(): return lax.ppermute(value, axis, pairs)  4.76 us
  transfers between devices with their start and end apart: 13, of which 3 were waited for; matrix products, arithmetic and copies ran while one was open for 1% of the time, Pallas kernels for 15%

commit v1 on v0

--- a/solution.py
+++ b/solution.py
@@ -1,4 +1,3 @@
-import functools
 import math
 
 import jax
@@ -58,7 +57,7 @@
 def pick(fields, links_ref):
     picked = []
     for which in range(3):
-        link = jnp.broadcast_to(links_ref[which : which + 1, :], (BS, NB))
+        link = jnp.broadcast_to(links_ref[which], (BS, NB))
         lane, part = link & (NB - 1), link >> 7
         value = take_lanes(fields[0], lane)
         for number in range(1, 5):
@@ -137,60 +136,52 @@
     tiles(step)
 
 
-def swap_blocks(values):
+def skew(values, count):
     group = iota((SUB, NB), 1) // NC
-    values = list(values)
-    for bit in (1, 2, 4):
-        keep = (group & bit) == 0
-        for low in range(8):
-            if low & bit:
-                continue
-            a, b = values[low], values[low | bit]
-            values[low] = jnp.where(keep, a, pltpu.roll(b, NC * bit, 1))
-            values[low | bit] = jnp.where(keep, pltpu.roll(a, NB - NC * bit, 1), b)
-    return values
+    values = [v if g == 0 else pltpu.roll(v, NC * g, 1) for g, v in enumerate(values)]
+    wanted = [(GROUPS - level) % GROUPS for level in range(count)]
+    needed = [set(wanted)]
+    for bit in (4, 2):
+        needed.append({v for v in needed[-1]} | {(v + bit) % GROUPS for v in needed[-1]})
+    for bit, places in zip((1, 2, 4), reversed(needed)):
+        second = (group & bit) != 0
+        values = [
+            jnp.where(second, values[(v + bit) % GROUPS], values[v]) if v in places else None
+            for v in range(GROUPS)
+        ]
+    return [values[v] for v in wanted]
 
 
 def pack_body(ops, smooth, packed, ops_high, smooth_high):
-    lane = iota((SUB, NB), 1)
-
-    def body(number, carry):
-        inner = number
-        low_ops, low_smooth, high = [], [], []
+    def body(inner, carry):
         for part in range(GROUPS):
             row = part * SUB + inner
-            low_ops.append(ops[row, :, 0:NB].astype(F32))
-            low_smooth.append(smooth[row, :, 0:NB].astype(F32))
             ops_high[part, :, 0 : 2 * NC] = ops[row, :, NB:].astype(F32)
             smooth_high[part, :, 0 : 3 * NC] = smooth[row, :, NB:].astype(F32)
         for column in range(GROUPS):
             rows = slice(column * SUB, (column + 1) * SUB)
             place = column * SUB + inner
-            for level, value in enumerate(swap_blocks([v[rows] for v in low_ops])):
-                packed[level, place] = value
-            for level, value in enumerate(swap_blocks([v[rows] for v in low_smooth])):
-                packed[LEVELS + level, place] = value
-            high = [
-                jnp.where(
-                    lane < 2 * NC,
-                    ops_high[part, rows, :],
-                    pltpu.roll(smooth_high[part, rows, :], 2 * NC, 1),
-                )
-                for part in range(GROUPS)
-            ]
-            high = swap_blocks(high)
-            for level, place_of in enumerate((8, 9, LEVELS + 8, LEVELS + 9, LEVELS + 10)):
-                packed[place_of, place] = high[level]
+            for base, low, high, count in (
+                (0, ops, ops_high, 2),
+                (LEVELS, smooth, smooth_high, 3),
+            ):
+                values = [low[part * SUB + inner, rows, 0:NB].astype(F32) for part in range(GROUPS)]
+                for level, value in enumerate(skew(values, GROUPS)):
+                    packed[base + level, place] = value
+                values = [high[part, rows, :] for part in range(GROUPS)]
+                for level, value in enumerate(skew(values, count)):
+                    packed[base + GROUPS + level, place] = value
         return carry
 
     lax.fori_loop(0, SUB, body, 0)
 
 
-def block_product(packed, number, vectors):
+def block_product(packed, number, vectors, turned):
     lane = iota((SUB, NB), 1) & (NC - 1)
     totals = [[None] * SUB for _ in vectors]
     for column in range(GROUPS):
-        spread = [take_lanes(v, lane + column * NC) for v in vectors]
+        place = lane + ((column + turned) % GROUPS) * NC
+        spread = [take_lanes(v, place) for v in vectors]
         for row in range(SUB):
             weight = packed[number, column * SUB + row]
             for total, value in zip(totals, spread):
@@ -199,7 +190,7 @@
     return [fold(total) for total in totals]
 
 
-def climb(packed, first_level, received, me, kept, sent):
+def climb(packed, first_level, received, me, kept):
     count = received.shape[0].bit_length() - 1
     columns = [received[me]]
     for bits in range(1, count + 1):
@@ -210,37 +201,36 @@
         columns.append(total * 2.0 ** (-bits / 2))
     for step in range(count):
         level = first_level + step
-        smoothed = block_product(packed, LEVELS + level, columns)
+        smoothed = block_product(packed, LEVELS + level, columns, max(level - 1, 0))
+        if level > 0:
+            columns = [pltpu.roll(v, NC, 1) for v in columns]
         kept[2 * step] = columns[0]
         kept[2 * step + 1] = smoothed[0]
-        removed = block_product(packed, level, smoothed[1:])
+        removed = block_product(packed, level, smoothed[1:], level)
         columns = [a - b for a, b in zip(columns[1:], removed)]
     return columns[0]
 
 
-def climb_body(first_level, axis, shift, packed, received, sent, kept):
-    me = (lax.axis_index(axis) >> shift) & (received.shape[0] - 1)
-    top = climb(packed, first_level, received, me, kept, sent)
+def climb_body(packed, received, sent, kept):
+    me = lax.axis_index("plan") & (received.shape[0] - 1)
+    top = climb(packed, 0, received, me, kept)
     for copy in range(sent.shape[0]):
         sent[copy] = top
 
 
-def turn_body(axis, packed, received, low, middle, field, owners, third, kept):
-    first_level = LEVELS - (received.shape[0].bit_length() - 1)
-    top = climb(packed, first_level, received, lax.axis_index(axis), kept, None)
-    (error,) = block_product(packed, 2 * LEVELS, [top])
+def turn_body(packed, received, low, field, owners, third, kept):
     low_levels = low.shape[0] // 2
+    near = 2**low_levels
+    far = lax.axis_size("plan") // near
+    me = lax.axis_index("height") * far + lax.axis_index("plan") // near
+    top = climb(packed, low_levels, received, me, kept)
+    (error,) = block_product(packed, 2 * LEVELS, [top], LEVELS - 1)
     for level in reversed(range(LEVELS)):
-        if level >= first_level:
-            saved, place = kept, level - first_level
-        elif level >= low_levels:
-            saved, place = middle, level - low_levels
-        else:
-            saved, place = low, level
-        error = saved[2 * place + 1] + error
-        (applied,) = block_product(packed, level, [error])
-        (fixed,) = block_product(packed, LEVELS + level, [saved[2 * place] - applied])
-        error = error + fixed
+        saved, place = (low, level) if level < low_levels else (kept, level - low_levels)
+        error = pltpu.roll(saved[2 * place + 1], NC, 1) + error
+        (applied,) = block_product(packed, level, [error], level + 1)
+        (fixed,) = block_product(packed, LEVELS + level, [saved[2 * place] - applied], level)
+        error = pltpu.roll(error, NB - NC, 1) + fixed
     owner = jnp.broadcast_to(owners[...], (SUB, NB))
     for group in range(GROUPS):
         rows = slice(group * SUB, (group + 1) * SUB)
@@ -269,11 +259,10 @@
 def shards(right_side, couplings, neighbours, aggregates, coarse_ops, coarse_smooth):
     source = right_side[0, 0]
     weights = couplings[0, 0]
-    links = neighbours[0, 0]
+    links = neighbours[0, 0][:, None, :]
     owners = aggregates[0]
     plan = lax.axis_size("plan")
     height = lax.axis_size("height")
-    height_bits = height.bit_length() - 1
     plan_bits = plan.bit_length() - 1
     low_bits = (plan_bits + 1) // 2
     near = 2**low_bits
@@ -290,9 +279,9 @@
         24 * MIB,
         [pltpu.VMEM((GROUPS, BS, NB), F32)] * 2,
     )
-    second = call(
-        first_body, field_shape, (source, *halo(source), weights, links), 12 * MIB
-    )
+    around = halo(source)
+    packed, source = lax.optimization_barrier((packed, source))
+    second = call(first_body, field_shape, (source, *around, weights, links), 12 * MIB)
     sent = call(
         second_body,
         vectors(near),
@@ -301,28 +290,21 @@
         [pltpu.VMEM((BS, NB), F32)],
     )
     near_groups = [[a * near + b for b in range(near)] for a in range(far)]
-    far_groups = [[a * near + b for a in range(far)] for b in range(near)]
     received = exchange(sent, "plan", near_groups)
     sent, low = call(
-        functools.partial(climb_body, 0, "plan", 0),
-        (vectors(far), vectors(2 * low_bits)),
-        (packed, received),
+        climb_body, (vectors(far * height), vectors(2 * low_bits)), (packed, received), 16 * MIB
+    )
+    far_groups = [
+        [(a * near + b) * height + h for h in range(height) for a in range(far)]
+        for b in range(near)
+    ]
+    received = exchange(sent, ("plan", "height"), far_groups)
+    third = call(
+        turn_body,
+        field_shape,
+        (packed, received, low, second, owners),
         16 * MIB,
-    )
-    received = exchange(sent, "plan", far_groups)
-    sent, middle = call(
-        functools.partial(climb_body, low_bits, "plan", low_bits),
-        (vectors(height), vectors(2 * (plan_bits - low_bits))),
-        (packed, received),
-        16 * MIB,
-    )
-    received = exchange(sent, "height")
-    third = call(
-        functools.partial(turn_body, "height"),
-        field_shape,
-        (packed, received, low, middle, second, owners),
-        16 * MIB,
-        [pltpu.VMEM((2 * height_bits, SUB, NB), F32)],
+        [pltpu.VMEM((2 * (LEVELS - low_bits), SUB, NB), F32)],
     )
     out = call(
         last_body, field_shape, (third, *halo(third), weights, links, source), 12 * MIB

time: 128 us -> 107 us (0.84)
  the two profiles are of different devices: /device:TPU:51 before, /device:TPU:2 now
where the time goes in v1:
time: 107 us
  blocking collectives  43.5 us (41%)
  starting transfers between devices  41.9 us (39%)
  Pallas kernels  10.9 us (10%)
  waiting for transfers between devices  7.02 us (7%)
  local copies, waits for them, and re-layouts  3.19 us (3%)
    all_to_all x2, blocking collectives, exchange(): lax.all_to_all(value, axis, 0, 0, axis_index_groups=groups, tiled=True)  43.5 us
    ppermute x12, starting transfers between devices, shifted(): return lax.ppermute(value, axis, pairs)  41.9 us
    pallas_call x6, Pallas kernels, call(): pl.pallas_call(body, out_shape=out_shape, in_specs=whole(len(inputs)), ou...  10.9 us
    ppermute x12, waiting for transfers between devices, shifted(): return lax.ppermute(value, axis, pairs)  7.02 us
    unnamed x12, local copies, waits for them, and re-layouts  3.19 us
  transfers between devices with their start and end apart: 12, of which 3 were waited for; matrix products, arithmetic and copies ran while one was open for 0% of the time, Pallas kernels for 2%

profile of v1, /device:TPU:2, one launch (start us, length us, event | category | flops | bytes accessed | tf_op | source)
XLA Modules:
  0.0 106.8 jit_solution(6469071911139635807)
XLA Ops:
  0.0 0.0 copy-start.4
  0.0 0.0 copy-start
  0.0 1.5 %collective-permute-start.3 = (f32[64,128]{1,0:T(8,128)}, f32[64,128]{1,0:T(8,128)S(1)}, u32[]{:S(2)}, u32[]{:S(2)}) collective-permute-start(f32[64,128]{1,0:T(8,128)} %bitcast.8), channel_id=1, source_target_pairs={{8,0},{16,8},{24,16},{32,24},{40,32},{48,40},{56,48},{64,56},{72,6... | collective-permute-start | bytes 98312 | tf_op jit(solution)/shard_map/ppermute | solution.py:243
  1.6 3.0 %collective-permute-start.2 = (f32[64,128]{1,0:T(8,128)}, f32[64,128]{1,0:T(8,128)S(1)}, u32[]{:S(2)}, u32[]{:S(2)}) collective-permute-start(f32[64,128]{1,0:T(8,128)} %bitcast.9), channel_id=1, source_target_pairs={{0,8},{8,16},{16,24},{24,32},{32,40},{40,48},{48,56},{56,64},{64,7... | collective-permute-start | bytes 98312 | tf_op jit(solution)/shard_map/ppermute | solution.py:243
  4.6 15.1 %collective-permute-start.1 = (f32[64,128]{1,0:T(8,128)}, f32[64,128]{1,0:T(8,128)S(1)}, u32[]{:S(2)}, u32[]{:S(2)}) collective-permute-start(f32[64,128]{1,0:T(8,128)} %bitcast.10), channel_id=1, source_target_pairs={{1,0},{2,1},{3,2},{4,3},{5,4},{6,5},{7,6},{9,8},{10,9},{11,10},{12... | collective-permute-start | bytes 98312 | tf_op jit(solution)/shard_map/ppermute | solution.py:243
  19.7 1.9 %collective-permute-start = (f32[64,128]{1,0:T(8,128)}, f32[64,128]{1,0:T(8,128)S(1)}, u32[]{:S(2)}, u32[]{:S(2)}) collective-permute-start(f32[64,128]{1,0:T(8,128)} %bitcast.11), channel_id=1, source_target_pairs={{0,1},{1,2},{2,3},{3,4},{4,5},{5,6},{6,7},{8,9},{9,10},{10,11},{11... | collective-permute-start | bytes 98312 | tf_op jit(solution)/shard_map/ppermute | solution.py:243
  21.6 0.0 copy-start.1
  21.6 1.6 %copy-done.1 = bf16[64,64,160]{2,1,0:T(8,128)(2,1)S(1)} copy-done((bf16[64,64,160]{2,1,0:T(8,128)(2,1)S(1)}, bf16[64,64,160]{2,1,0:T(8,128)(2,1)}, u32[]{:S(2)}) %copy-start.1) | copy-done | bytes 1310744
  23.2 0.0 copy-start.2
  23.2 1.6 %copy-done.2 = bf16[64,64,176]{2,1,0:T(8,128)(2,1)S(1)} copy-done((bf16[64,64,176]{2,1,0:T(8,128)(2,1)S(1)}, bf16[64,64,176]{2,1,0:T(8,128)(2,1)}, u32[]{:S(2)}) %copy-start.2) | copy-done | bytes 1441816
  24.8 0.0 copy-start.3
  24.8 2.3 %shard_map.64.packed = f32[21,64,8,128]{3,2,1,0:T(8,128)S(1)} custom-call(bf16[64,64,160]{2,1,0:T(8,128)(2,1)S(1)} %copy-done.1, bf16[64,64,176]{2,1,0:T(8,128)(2,1)S(1)} %copy-done.2), custom_call_target="tpu_custom_call" | custom-call | tf_op jit(solution)/shard_map/pallas_call | solution.py:26
  27.1 0.0 copy-start.5
  27.1 0.0 collective-permute-done.3.after
  27.1 0.0 collective-permute-done.2.before
  27.1 0.0 collective-permute-done.1.above
  27.2 0.0 collective-permute-done.below
  27.2 0.0 copy-done.4
  27.2 0.0 copy-done
  27.2 0.0 copy-done.3
  27.2 1.0 shard_map.65.field
  28.2 1.3 %collective-permute-start.7 = (f32[64,128]{1,0:T(8,128)S(1)}, f32[64,128]{1,0:T(8,128)S(1)}, u32[]{:S(2)}, u32[]{:S(2)}) collective-permute-start(f32[64,128]{1,0:T(8,128)S(1)} %shard_map.65.field), channel_id=1, source_target_pairs={{8,0},{16,8},{24,16},{32,24},{40,32},{48,40},{56,48},{64,56},{72,6... | collective-permute-start | bytes 98312 | tf_op jit(solution)/shard_map/ppermute | solution.py:243
  29.5 3.0 %collective-permute-start.6 = (f32[64,128]{1,0:T(8,128)S(1)}, f32[64,128]{1,0:T(8,128)S(1)}, u32[]{:S(2)}, u32[]{:S(2)}) collective-permute-start(f32[64,128]{1,0:T(8,128)S(1)} %shard_map.65.field), channel_id=1, source_target_pairs={{0,8},{8,16},{16,24},{24,32},{32,40},{40,48},{48,56},{56,64},{64,7... | collective-permute-start | bytes 98312 | tf_op jit(solution)/shard_map/ppermute | solution.py:243
  32.5 3.9 %collective-permute-start.5 = (f32[64,128]{1,0:T(8,128)S(1)}, f32[64,128]{1,0:T(8,128)S(1)}, u32[]{:S(2)}, u32[]{:S(2)}) collective-permute-start(f32[64,128]{1,0:T(8,128)S(1)} %shard_map.65.field), channel_id=1, source_target_pairs={{1,0},{2,1},{3,2},{4,3},{5,4},{6,5},{7,6},{9,8},{10,9},{11,10},{12... | collective-permute-start | bytes 98312 | tf_op jit(solution)/shard_map/ppermute | solution.py:243
  36.4 1.9 %collective-permute-start.4 = (f32[64,128]{1,0:T(8,128)S(1)}, f32[64,128]{1,0:T(8,128)S(1)}, u32[]{:S(2)}, u32[]{:S(2)}) collective-permute-start(f32[64,128]{1,0:T(8,128)S(1)} %shard_map.65.field), channel_id=1, source_target_pairs={{0,1},{1,2},{2,3},{3,4},{4,5},{5,6},{6,7},{8,9},{9,10},{10,11},{11... | collective-permute-start | bytes 98312 | tf_op jit(solution)/shard_map/ppermute | solution.py:243
  38.4 0.0 collective-permute-done.7.after
  38.4 0.0 collective-permute-done.6.before
  38.4 0.3 collective-permute-done.5.above
  38.7 3.6 %collective-permute-done.4.below = f32[64,128]{1,0:T(8,128)S(1)} collective-permute-done((f32[64,128]{1,0:T(8,128)S(1)}, f32[64,128]{1,0:T(8,128)S(1)}, u32[]{:S(2)}, u32[]{:S(2)}) %collective-permute-start.4) | collective-permute-done | bytes 32800 | tf_op jit(solution)/shard_map/ppermute | solution.py:243
  42.2 0.0 copy-done.5
  42.3 1.2 %shard_map.66 = f32[16,8,128]{2,1,0:T(8,128)S(1)} custom-call(f32[64,128]{1,0:T(8,128)S(1)} %shard_map.65.field, f32[64,128]{1,0:T(8,128)S(1)} %collective-permute-done.4.below, f32[64,128]{1,0:T(8,128)S(1)} %collective-permute-done.5.above, f32[64,128]{1,0:T(8,128)S(1)} %collective-permute-done.6.before, f32[64,128]{1,0:T(8,128)S(1)} %collective-permute-done.7.after, ...), custom_call_target="tpu_custom_call" | custom-call | tf_op jit(solution)/shard_map/pallas_call | solution.py:26
  43.4 10.4 %all_to_all.10.received = f32[16,8,128]{2,1,0:T(8,128)S(1)} all-to-all(f32[16,8,128]{2,1,0:T(8,128)S(1)} %shard_map.66), channel_id=1, replica_groups={{0,8,16,24,32,40,48,56,64,72,80,88,96,104,112,120},{128,136,144,152,160..., dimensions={0} | all-to-all | bytes 131072 | tf_op jit(solution)/shard_map/all_to_all | solution.py:256
  53.8 1.0 shard_map.67
  54.9 33.1 %all_to_all.11.received = f32[64,8,128]{2,1,0:T(8,128)S(1)} all-to-all(f32[64,8,128]{2,1,0:T(8,128)S(1)} %get-tuple-element.11), channel_id=1, replica_groups={{0,128,256,384,512,640,768,896,1,129,257,385,513,641,769,897,2,130,258,..., dimensions={0} | all-to-all | bytes 524288 | tf_op jit(solution)/shard_map/all_to_all | solution.py:256
  87.9 3.9 %shard_map.68.field = f32[64,128]{1,0:T(8,128)S(1)} custom-call(f32[21,64,8,128]{3,2,1,0:T(8,128)S(1)} %shard_map.64.packed, f32[64,8,128]{2,1,0:T(8,128)S(1)} %all_to_all.11.received, f32[8,8,128]{2,1,0:T(8,128)S(1)} %get-tuple-element.12.low, f32[64,128]{1,0:T(8,128)S(1)} %shard_map.65.field, s32[1,128]{1,0:T(1,128)S(1)} %bitcast.19), custom_call_target="tpu_custom_call" | custom-call | tf_op jit(solution)/shard_map/pallas_call | solution.py:26
  91.8 1.3 %collective-permute-start.11 = (f32[64,128]{1,0:T(8,128)S(1)}, f32[64,128]{1,0:T(8,128)S(1)}, u32[]{:S(2)}, u32[]{:S(2)}) collective-permute-start(f32[64,128]{1,0:T(8,128)S(1)} %shard_map.68.field), channel_id=1, source_target_pairs={{8,0},{16,8},{24,16},{32,24},{40,32},{48,40},{56,48},{64,56},{72,6... | collective-permute-start | bytes 98312 | tf_op jit(solution)/shard_map/ppermute | solution.py:243
  93.1 3.0 %collective-permute-start.10 = (f32[64,128]{1,0:T(8,128)S(1)}, f32[64,128]{1,0:T(8,128)S(1)}, u32[]{:S(2)}, u32[]{:S(2)}) collective-permute-start(f32[64,128]{1,0:T(8,128)S(1)} %shard_map.68.field), channel_id=1, source_target_pairs={{0,8},{8,16},{16,24},{24,32},{32,40},{40,48},{48,56},{56,64},{64,7... | collective-permute-start | bytes 98312 | tf_op jit(solution)/shard_map/ppermute | solution.py:243
  96.2 3.2 %collective-permute-start.9 = (f32[64,128]{1,0:T(8,128)S(1)}, f32[64,128]{1,0:T(8,128)S(1)}, u32[]{:S(2)}, u32[]{:S(2)}) collective-permute-start(f32[64,128]{1,0:T(8,128)S(1)} %shard_map.68.field), channel_id=1, source_target_pairs={{1,0},{2,1},{3,2},{4,3},{5,4},{6,5},{7,6},{9,8},{10,9},{11,10},{12... | collective-permute-start | bytes 98312 | tf_op jit(solution)/shard_map/ppermute | solution.py:243
  99.4 2.6 %collective-permute-start.8 = (f32[64,128]{1,0:T(8,128)S(1)}, f32[64,128]{1,0:T(8,128)S(1)}, u32[]{:S(2)}, u32[]{:S(2)}) collective-permute-start(f32[64,128]{1,0:T(8,128)S(1)} %shard_map.68.field), channel_id=1, source_target_pairs={{0,1},{1,2},{2,3},{3,4},{4,5},{5,6},{6,7},{8,9},{9,10},{10,11},{11... | collective-permute-start | bytes 98312 | tf_op jit(solution)/shard_map/ppermute | solution.py:243
  102.0 0.0 collective-permute-done.11.after
  102.0 0.0 collective-permute-done.10.before
  102.0 0.0 collective-permute-done.9.above
  102.0 3.1 %collective-permute-done.8.below = f32[64,128]{1,0:T(8,128)S(1)} collective-permute-done((f32[64,128]{1,0:T(8,128)S(1)}, f32[64,128]{1,0:T(8,128)S(1)}, u32[]{:S(2)}, u32[]{:S(2)}) %collective-permute-start.8) | collective-permute-done | bytes 32800 | tf_op jit(solution)/shard_map/ppermute | solution.py:243
  105.2 1.6 %shard_map.69 = f32[64,128]{1,0:T(8,128)} custom-call(f32[64,128]{1,0:T(8,128)S(1)} %shard_map.68.field, f32[64,128]{1,0:T(8,128)S(1)} %collective-permute-done.8.below, f32[64,128]{1,0:T(8,128)S(1)} %collective-permute-done.9.above, f32[64,128]{1,0:T(8,128)S(1)} %collective-permute-done.10.before, f32[64,128]{1,0:T(8,128)S(1)} %collective-permute-done.11.after, ...), custom_call_target="tpu_custom_call" | custom-call | tf_op jit(solution)/shard_map/pallas_call | solution.py:26
Async XLA Ops:
  0.0 27.2 %copy-start.4 = (s32[1,1,3,128]{3,1,2,0:T(1,128)S(1)}, s32[1,1,3,128]{3,1,2,0:T(1,128)}, u32[]{:S(2)}) copy-start(s32[1,1,3,128]{3,1,2,0:T(1,128)} %param.8) | copy-start | bytes 4612
  0.0 27.2 %copy-start = (bf16[1,1,3,64,64,128]{5,4,3,2,1,0:T(8,128)(2,1)S(1)}, bf16[1,1,3,64,64,128]{5,4,3,2,1,0:T(8,128)(2,1)}, u32[]{:S(2)}) copy-start(bf16[1,1,3,64,64,128]{5,4,3,2,1,0:T(8,128)(2,1)} %param.7) | copy-start | bytes 9437188
  0.0 27.1 %collective-permute-start.3 = (f32[64,128]{1,0:T(8,128)}, f32[64,128]{1,0:T(8,128)S(1)}, u32[]{:S(2)}, u32[]{:S(2)}) collective-permute-start(f32[64,128]{1,0:T(8,128)} %bitcast.8), channel_id=1, source_target_pairs={{8,0},{16,8},{24,16},{32,24},{40,32},{48,40},{56,48},{64,56},{72,6... | collective-permute-start | bytes 98312 | tf_op jit(solution)/shard_map/ppermute | solution.py:243
  1.6 25.6 %collective-permute-start.2 = (f32[64,128]{1,0:T(8,128)}, f32[64,128]{1,0:T(8,128)S(1)}, u32[]{:S(2)}, u32[]{:S(2)}) collective-permute-start(f32[64,128]{1,0:T(8,128)} %bitcast.9), channel_id=1, source_target_pairs={{0,8},{8,16},{16,24},{24,32},{32,40},{40,48},{48,56},{56,64},{64,7... | collective-permute-start | bytes 98312 | tf_op jit(solution)/shard_map/ppermute | solution.py:243
  4.6 22.6 %collective-permute-start.1 = (f32[64,128]{1,0:T(8,128)}, f32[64,128]{1,0:T(8,128)S(1)}, u32[]{:S(2)}, u32[]{:S(2)}) collective-permute-start(f32[64,128]{1,0:T(8,128)} %bitcast.10), channel_id=1, source_target_pairs={{1,0},{2,1},{3,2},{4,3},{5,4},{6,5},{7,6},{9,8},{10,9},{11,10},{12... | collective-permute-start | bytes 98312 | tf_op jit(solution)/shard_map/ppermute | solution.py:243
  19.7 7.5 %collective-permute-start = (f32[64,128]{1,0:T(8,128)}, f32[64,128]{1,0:T(8,128)S(1)}, u32[]{:S(2)}, u32[]{:S(2)}) collective-permute-start(f32[64,128]{1,0:T(8,128)} %bitcast.11), channel_id=1, source_target_pairs={{0,1},{1,2},{2,3},{3,4},{4,5},{5,6},{6,7},{8,9},{9,10},{10,11},{11... | collective-permute-start | bytes 98312 | tf_op jit(solution)/shard_map/ppermute | solution.py:243
  21.6 1.6 %copy-start.1 = (bf16[64,64,160]{2,1,0:T(8,128)(2,1)S(1)}, bf16[64,64,160]{2,1,0:T(8,128)(2,1)}, u32[]{:S(2)}) copy-start(bf16[64,64,160]{2,1,0:T(8,128)(2,1)} %ops.1) | copy-start | bytes 3932164
  23.2 1.6 %copy-start.2 = (bf16[64,64,176]{2,1,0:T(8,128)(2,1)S(1)}, bf16[64,64,176]{2,1,0:T(8,128)(2,1)}, u32[]{:S(2)}) copy-start(bf16[64,64,176]{2,1,0:T(8,128)(2,1)} %smooth.1) | copy-start | bytes 4325380
  24.8 2.4 %copy-start.3 = (f32[1,1,64,128]{3,2,1,0:T(8,128)S(1)}, f32[1,1,64,128]{3,2,1,0:T(8,128)}, u32[]{:S(2)}) copy-start(f32[1,1,64,128]{3,2,1,0:T(8,128)} %param.6) | copy-start | bytes 98308
  27.1 15.1 %copy-start.5 = (s32[1,1,128]{2,1,0:T(1,128)S(1)}, s32[1,1,128]{2,1,0:T(1,128)}, u32[]{:S(2)}) copy-start(s32[1,1,128]{2,1,0:T(1,128)} %param.9) | copy-start | bytes 1540
  28.2 10.2 %collective-permute-start.7 = (f32[64,128]{1,0:T(8,128)S(1)}, f32[64,128]{1,0:T(8,128)S(1)}, u32[]{:S(2)}, u32[]{:S(2)}) collective-permute-start(f32[64,128]{1,0:T(8,128)S(1)} %shard_map.65.field), channel_id=1, source_target_pairs={{8,0},{16,8},{24,16},{32,24},{40,32},{48,40},{56,48},{64,56},{72,6... | collective-permute-start | bytes 98312 | tf_op jit(solution)/shard_map/ppermute | solution.py:243
  29.5 8.9 %collective-permute-start.6 = (f32[64,128]{1,0:T(8,128)S(1)}, f32[64,128]{1,0:T(8,128)S(1)}, u32[]{:S(2)}, u32[]{:S(2)}) collective-permute-start(f32[64,128]{1,0:T(8,128)S(1)} %shard_map.65.field), channel_id=1, source_target_pairs={{0,8},{8,16},{16,24},{24,32},{32,40},{40,48},{48,56},{56,64},{64,7... | collective-permute-start | bytes 98312 | tf_op jit(solution)/shard_map/ppermute | solution.py:243
  32.5 6.2 %collective-permute-start.5 = (f32[64,128]{1,0:T(8,128)S(1)}, f32[64,128]{1,0:T(8,128)S(1)}, u32[]{:S(2)}, u32[]{:S(2)}) collective-permute-start(f32[64,128]{1,0:T(8,128)S(1)} %shard_map.65.field), channel_id=1, source_target_pairs={{1,0},{2,1},{3,2},{4,3},{5,4},{6,5},{7,6},{9,8},{10,9},{11,10},{12... | collective-permute-start | bytes 98312 | tf_op jit(solution)/shard_map/ppermute | solution.py:243
  36.4 5.8 %collective-permute-start.4 = (f32[64,128]{1,0:T(8,128)S(1)}, f32[64,128]{1,0:T(8,128)S(1)}, u32[]{:S(2)}, u32[]{:S(2)}) collective-permute-start(f32[64,128]{1,0:T(8,128)S(1)} %shard_map.65.field), channel_id=1, source_target_pairs={{0,1},{1,2},{2,3},{3,4},{4,5},{5,6},{6,7},{8,9},{9,10},{10,11},{11... | collective-permute-start | bytes 98312 | tf_op jit(solution)/shard_map/ppermute | solution.py:243
  91.8 10.2 %collective-permute-start.11 = (f32[64,128]{1,0:T(8,128)S(1)}, f32[64,128]{1,0:T(8,128)S(1)}, u32[]{:S(2)}, u32[]{:S(2)}) collective-permute-start(f32[64,128]{1,0:T(8,128)S(1)} %shard_map.68.field), channel_id=1, source_target_pairs={{8,0},{16,8},{24,16},{32,24},{40,32},{48,40},{56,48},{64,56},{72,6... | collective-permute-start | bytes 98312 | tf_op jit(solution)/shard_map/ppermute | solution.py:243
  93.1 8.9 %collective-permute-start.10 = (f32[64,128]{1,0:T(8,128)S(1)}, f32[64,128]{1,0:T(8,128)S(1)}, u32[]{:S(2)}, u32[]{:S(2)}) collective-permute-start(f32[64,128]{1,0:T(8,128)S(1)} %shard_map.68.field), channel_id=1, source_target_pairs={{0,8},{8,16},{16,24},{24,32},{32,40},{40,48},{48,56},{56,64},{64,7... | collective-permute-start | bytes 98312 | tf_op jit(solution)/shard_map/ppermute | solution.py:243
  96.2 5.9 %collective-permute-start.9 = (f32[64,128]{1,0:T(8,128)S(1)}, f32[64,128]{1,0:T(8,128)S(1)}, u32[]{:S(2)}, u32[]{:S(2)}) collective-permute-start(f32[64,128]{1,0:T(8,128)S(1)} %shard_map.68.field), channel_id=1, source_target_pairs={{1,0},{2,1},{3,2},{4,3},{5,4},{6,5},{7,6},{9,8},{10,9},{11,10},{12... | collective-permute-start | bytes 98312 | tf_op jit(solution)/shard_map/ppermute | solution.py:243
  99.4 5.8 %collective-permute-start.8 = (f32[64,128]{1,0:T(8,128)S(1)}, f32[64,128]{1,0:T(8,128)S(1)}, u32[]{:S(2)}, u32[]{:S(2)}) collective-permute-start(f32[64,128]{1,0:T(8,128)S(1)} %shard_map.68.field), channel_id=1, source_target_pairs={{0,1},{1,2},{2,3},{3,4},{4,5},{5,6},{6,7},{8,9},{9,10},{10,11},{11... | collective-permute-start | bytes 98312 | tf_op jit(solution)/shard_map/ppermute | solution.py:243

commit v2 on v1

--- a/solution.py
+++ b/solution.py
@@ -1,3 +1,4 @@
+import functools
 import math
 
 import jax
@@ -55,13 +56,15 @@
 
 
 def pick(fields, links_ref):
+    odd = lax.axis_index("plan") & 1
+    numbers = (0, 4 - odd, 3 + odd, 2, 1)
     picked = []
     for which in range(3):
         link = jnp.broadcast_to(links_ref[which], (BS, NB))
         lane, part = link & (NB - 1), link >> 7
         value = take_lanes(fields[0], lane)
-        for number in range(1, 5):
-            value = jnp.where(part == number, take_lanes(fields[number], lane), value)
+        for number, field in zip(numbers[1:], fields[1:]):
+            value = jnp.where(part == number, take_lanes(field, lane), value)
         picked.append(value)
     return picked
 
@@ -87,8 +90,8 @@
     lax.fori_loop(0, GROUPS, body, 0)
 
 
-def first_body(source, below, above, before, after, weights, links, second):
-    fields = [ref[...] for ref in (source, below, above, before, after)]
+def first_body(source, inner, outer, above, below, weights, links, second):
+    fields = [ref[...] for ref in (source, inner, outer, above, below)]
     picked = pick(fields, links)
 
     def step(tile, rows):
@@ -99,8 +102,8 @@
     tiles(step)
 
 
-def second_body(field, below, above, before, after, weights, links, source, owners, sent, left):
-    fields = [ref[...] for ref in (field, below, above, before, after)]
+def second_body(field, inner, outer, above, below, weights, links, source, owners, sent, left):
+    fields = [ref[...] for ref in (field, inner, outer, above, below)]
     picked = pick(fields, links)
 
     def step(tile, rows):
@@ -124,8 +127,8 @@
         sent[copy] = packed
 
 
-def last_body(field, below, above, before, after, weights, links, source, out):
-    fields = [ref[...] for ref in (field, below, above, before, after)]
+def last_body(field, inner, outer, above, below, weights, links, source, out):
+    fields = [ref[...] for ref in (field, inner, outer, above, below)]
     picked = pick(fields, links)
 
     def step(tile, rows):
@@ -152,45 +155,53 @@
     return [values[v] for v in wanted]
 
 
-def pack_body(ops, smooth, packed, ops_high, smooth_high):
+def pack_body(source, packed, high):
+    count = packed.shape[0]
+    rest = (count - GROUPS) * NC
+
     def body(inner, carry):
         for part in range(GROUPS):
-            row = part * SUB + inner
-            ops_high[part, :, 0 : 2 * NC] = ops[row, :, NB:].astype(F32)
-            smooth_high[part, :, 0 : 3 * NC] = smooth[row, :, NB:].astype(F32)
+            high[part, :, 0:rest] = source[part, inner, :, NB:].astype(F32)
         for column in range(GROUPS):
             rows = slice(column * SUB, (column + 1) * SUB)
             place = column * SUB + inner
-            for base, low, high, count in (
-                (0, ops, ops_high, 2),
-                (LEVELS, smooth, smooth_high, 3),
-            ):
-                values = [low[part * SUB + inner, rows, 0:NB].astype(F32) for part in range(GROUPS)]
-                for level, value in enumerate(skew(values, GROUPS)):
-                    packed[base + level, place] = value
-                values = [high[part, rows, :] for part in range(GROUPS)]
-                for level, value in enumerate(skew(values, count)):
-                    packed[base + GROUPS + level, place] = value
+            values = [source[part, inner, rows, 0:NB].astype(F32) for part in range(GROUPS)]
+            for level, value in enumerate(skew(values, GROUPS)):
+                packed[level, place] = value
+            values = [high[part, rows, :] for part in range(GROUPS)]
+            for level, value in enumerate(skew(values, count - GROUPS)):
+                packed[GROUPS + level, place] = value
         return carry
 
     lax.fori_loop(0, SUB, body, 0)
 
 
-def block_product(packed, number, vectors, turned):
+def pack(blocks):
+    width = blocks.shape[2]
+    return call(
+        pack_body,
+        jax.ShapeDtypeStruct((width // NC, BS, SUB, NB), F32),
+        (blocks.reshape(GROUPS, SUB, BS, width),),
+        12 * MIB,
+        [pltpu.VMEM((GROUPS, BS, NB), F32)],
+    )
+
+
+def block_product(packed, level, vectors, turned):
     lane = iota((SUB, NB), 1) & (NC - 1)
     totals = [[None] * SUB for _ in vectors]
     for column in range(GROUPS):
         place = lane + ((column + turned) % GROUPS) * NC
         spread = [take_lanes(v, place) for v in vectors]
         for row in range(SUB):
-            weight = packed[number, column * SUB + row]
+            weight = packed[level, column * SUB + row]
             for total, value in zip(totals, spread):
                 piece = weight * value
                 total[row] = piece if total[row] is None else total[row] + piece
     return [fold(total) for total in totals]
 
 
-def climb(packed, first_level, received, me, kept):
+def climb(ops, smooth, first_level, received, me, kept):
     count = received.shape[0].bit_length() - 1
     columns = [received[me]]
     for bits in range(1, count + 1):
@@ -201,35 +212,36 @@
         columns.append(total * 2.0 ** (-bits / 2))
     for step in range(count):
         level = first_level + step
-        smoothed = block_product(packed, LEVELS + level, columns, max(level - 1, 0))
+        smoothed = block_product(smooth, level, columns, max(level - 1, 0))
         if level > 0:
             columns = [pltpu.roll(v, NC, 1) for v in columns]
         kept[2 * step] = columns[0]
         kept[2 * step + 1] = smoothed[0]
-        removed = block_product(packed, level, smoothed[1:], level)
+        removed = block_product(ops, level, smoothed[1:], level)
         columns = [a - b for a, b in zip(columns[1:], removed)]
     return columns[0]
 
 
-def climb_body(packed, received, sent, kept):
-    me = lax.axis_index("plan") & (received.shape[0] - 1)
-    top = climb(packed, 0, received, me, kept)
+def climb_body(first_level, ops, smooth, received, sent, kept):
+    me = (lax.axis_index("plan") >> first_level) & (received.shape[0] - 1)
+    top = climb(ops, smooth, first_level, received, me, kept)
     for copy in range(sent.shape[0]):
         sent[copy] = top
 
 
-def turn_body(packed, received, low, field, owners, third, kept):
-    low_levels = low.shape[0] // 2
-    near = 2**low_levels
-    far = lax.axis_size("plan") // near
-    me = lax.axis_index("height") * far + lax.axis_index("plan") // near
-    top = climb(packed, low_levels, received, me, kept)
-    (error,) = block_product(packed, 2 * LEVELS, [top], LEVELS - 1)
+def turn_body(ops, smooth, received, low, middle, field, owners, third, high):
+    levels = [
+        (saved, 2 * place)
+        for saved in (low, middle, high)
+        for place in range(saved.shape[0] // 2)
+    ]
+    top = climb(ops, smooth, (low.shape[0] + middle.shape[0]) // 2, received, lax.axis_index("height"), high)
+    (error,) = block_product(smooth, LEVELS, [top], LEVELS - 1)
     for level in reversed(range(LEVELS)):
-        saved, place = (low, level) if level < low_levels else (kept, level - low_levels)
-        error = pltpu.roll(saved[2 * place + 1], NC, 1) + error
-        (applied,) = block_product(packed, level, [error], level + 1)
-        (fixed,) = block_product(packed, LEVELS + level, [saved[2 * place] - applied], level)
+        saved, place = levels[level]
+        error = pltpu.roll(saved[place + 1], NC, 1) + error
+        (applied,) = block_product(ops, level, [error], level + 1)
+        (fixed,) = block_product(smooth, level, [saved[place] - applied], level)
         error = pltpu.roll(error, NB - NC, 1) + fixed
     owner = jnp.broadcast_to(owners[...], (SUB, NB))
     for group in range(GROUPS):
@@ -237,19 +249,23 @@
         third[rows, :] = field[rows, :] + take_lanes(error, owner + group * NC)
 
 
-def shifted(value, axis, step):
-    count = lax.axis_size(axis)
+def shifted(value, step):
+    count = lax.axis_size("height")
     pairs = [(i, i + step) for i in range(count) if 0 <= i + step < count]
-    return lax.ppermute(value, axis, pairs)
+    return lax.ppermute(value, "height", pairs)
+
+
+def swapped(value, first):
+    pairs = []
+    for low in range(first, lax.axis_size("plan") - 1, 2):
+        pairs += [(low, low + 1), (low + 1, low)]
+    return lax.ppermute(value, "plan", pairs)
 
 
 def halo(value):
-    return (
-        shifted(value, "height", 1),
-        shifted(value, "height", -1),
-        shifted(value, "plan", 1),
-        shifted(value, "plan", -1),
-    )
+    inner, outer = swapped(value, 0), swapped(value, 1)
+    above, below = shifted(value, -1), shifted(value, 1)
+    return inner, outer, above, below
 
 
 def exchange(value, axis, groups=None):
@@ -272,39 +288,44 @@
     def vectors(count):
         return jax.ShapeDtypeStruct((count, SUB, NB), F32)
 
-    packed = call(
-        pack_body,
-        jax.ShapeDtypeStruct((2 * LEVELS + 1, BS, SUB, NB), F32),
-        (coarse_ops, coarse_smooth),
-        24 * MIB,
-        [pltpu.VMEM((GROUPS, BS, NB), F32)] * 2,
-    )
+    smooth = pack(coarse_smooth)
     around = halo(source)
-    packed, source = lax.optimization_barrier((packed, source))
+    smooth, source = lax.optimization_barrier((smooth, source))
     second = call(first_body, field_shape, (source, *around, weights, links), 12 * MIB)
+    around = halo(second)
+    second, coarse_ops = lax.optimization_barrier((second, coarse_ops))
+    ops = pack(coarse_ops)
+    ops, source = lax.optimization_barrier((ops, source))
     sent = call(
         second_body,
         vectors(near),
-        (second, *halo(second), weights, links, source, owners),
+        (second, *around, weights, links, source, owners),
         12 * MIB,
         [pltpu.VMEM((BS, NB), F32)],
     )
     near_groups = [[a * near + b for b in range(near)] for a in range(far)]
+    far_groups = [[a * near + b for a in range(far)] for b in range(near)]
     received = exchange(sent, "plan", near_groups)
     sent, low = call(
-        climb_body, (vectors(far * height), vectors(2 * low_bits)), (packed, received), 16 * MIB
-    )
-    far_groups = [
-        [(a * near + b) * height + h for h in range(height) for a in range(far)]
-        for b in range(near)
-    ]
-    received = exchange(sent, ("plan", "height"), far_groups)
+        functools.partial(climb_body, 0),
+        (vectors(far), vectors(2 * low_bits)),
+        (ops, smooth, received),
+        16 * MIB,
+    )
+    received = exchange(sent, "plan", far_groups)
+    sent, middle = call(
+        functools.partial(climb_body, low_bits),
+        (vectors(height), vectors(2 * (plan_bits - low_bits))),
+        (ops, smooth, received),
+        16 * MIB,
+    )
+    received = exchange(sent, "height")
     third = call(
         turn_body,
         field_shape,
-        (packed, received, low, second, owners),
+        (ops, smooth, received, low, middle, second, owners),
         16 * MIB,
-        [pltpu.VMEM((2 * (LEVELS - low_bits), SUB, NB), F32)],
+        [pltpu.VMEM((2 * (LEVELS - plan_bits), SUB, NB), F32)],
     )
     out = call(
         last_body, field_shape, (third, *halo(third), weights, links, source), 12 * MIB

time: 107 us -> 103 us (0.963)
  waiting for transfers between devices: 7.02 us -> 0.84 us
  blocking collectives: 43.5 us -> 49.2 us
  starting transfers between devices: 41.9 us -> 39.2 us
  local copies, waits for them, and re-layouts: 3.19 us -> 1.61 us
    ppermute x12, waiting for transfers between devices: 7.02 us -> 0.84 us  [the longest x6 0.82 us: swapped(): return lax.ppermute(value, 'plan', pairs)]
    all_to_all x2 -> x3, blocking collectives: 43.5 us -> 49.2 us  [exchange(): lax.all_to_all(value, axis, 0, 0, axis_index_groups=groups, tiled=True)]
    ppermute x12, starting transfers between devices: 41.9 us -> 39.2 us  [the longest x6 28.3 us: shifted(): return lax.ppermute(value, 'height', pairs)]
    unnamed x12, local copies, waits for them, and re-layouts: 3.19 us -> 1.61 us
    pallas_call x6 -> x8, Pallas kernels: 10.9 us -> 11.1 us  [call(): pl.pallas_call(body, out_shape=out_shape, in_specs=whole(len(inputs)), ou...]
  transfers between devices with their start and end apart: 12 -> 12, of which waited for: 3 -> 1; matrix products, arithmetic and copies ran while one was open for 0% -> 0% of each run, Pallas kernels for 2% -> 3%
where the time goes in v2:
time: 103 us; the launch traced here: 102 us
  blocking collectives  49.2 us (48%)
  starting transfers between devices  39.2 us (38%)
  Pallas kernels  11.1 us (11%)
  local copies, waits for them, and re-layouts  1.61 us (2%)
    all_to_all x3, blocking collectives, exchange(): lax.all_to_all(value, axis, 0, 0, axis_index_groups=groups, tiled=True)  49.2 us
    ppermute x6, starting transfers between devices, shifted(): return lax.ppermute(value, 'height', pairs)  28.3 us
    pallas_call x8, Pallas kernels, call(): pl.pallas_call(body, out_shape=out_shape, in_specs=whole(len(inputs)), ou...  11.1 us
    ppermute x6, starting transfers between devices, swapped(): return lax.ppermute(value, 'plan', pairs)  10.9 us
  transfers between devices with their start and end apart: 12, of which 1 were waited for; matrix products, arithmetic and copies ran while one was open for 0% of the time, Pallas kernels for 3%

profile of v2, /device:TPU:2, one launch (start us, length us, event | category | flops | bytes accessed | tf_op | source)
XLA Modules:
  0.0 102.2 jit_solution(4143893451441058533)
XLA Ops:
  0.0 0.0 copy-start
  0.0 3.6 %collective-permute-start.3 = (f32[64,128]{1,0:T(8,128)}, f32[64,128]{1,0:T(8,128)S(1)}, u32[]{:S(2)}, u32[]{:S(2)}) collective-permute-start(f32[64,128]{1,0:T(8,128)} %bitcast.12), channel_id=1, source_target_pairs={{0,1},{1,2},{2,3},{3,4},{4,5},{5,6},{6,7},{8,9},{9,10},{10,11},{11... | collective-permute-start | bytes 98312 | tf_op jit(solution)/shard_map/ppermute | solution.py:255
  3.7 13.0 %collective-permute-start.2 = (f32[64,128]{1,0:T(8,128)}, f32[64,128]{1,0:T(8,128)S(1)}, u32[]{:S(2)}, u32[]{:S(2)}) collective-permute-start(f32[64,128]{1,0:T(8,128)} %bitcast.13), channel_id=1, source_target_pairs={{1,0},{2,1},{3,2},{4,3},{5,4},{6,5},{7,6},{9,8},{10,9},{11,10},{12... | collective-permute-start | bytes 98312 | tf_op jit(solution)/shard_map/ppermute | solution.py:255
  16.7 0.7 collective-permute-start.1
  17.3 1.9 %collective-permute-start = (f32[64,128]{1,0:T(8,128)}, f32[64,128]{1,0:T(8,128)S(1)}, u32[]{:S(2)}, u32[]{:S(2)}) collective-permute-start(f32[64,128]{1,0:T(8,128)} %bitcast.15), channel_id=1, source_target_pairs={{0,8},{8,0},{16,24},{24,16},{32,40},{40,32},{48,56},{56,48},{64,72... | collective-permute-start | bytes 98312 | tf_op jit(solution)/shard_map/ppermute | solution.py:262
  19.3 0.0 copy-start.1
  19.3 1.6 %copy-done.1 = bf16[64,64,176]{2,1,0:T(8,128)(2,1)S(1)} copy-done((bf16[64,64,176]{2,1,0:T(8,128)(2,1)S(1)}, bf16[64,64,176]{2,1,0:T(8,128)(2,1)}, u32[]{:S(2)}) %copy-start.1) | copy-done | bytes 1441816
  20.8 0.0 copy-start.3
  20.8 0.0 copy-start.4
  20.8 1.4 %shard_map.64.smooth = f32[11,64,8,128]{3,2,1,0:T(8,128)S(1)} custom-call(bf16[8,8,64,176]{3,2,1,0:T(8,128)(2,1)S(1)} %bitcast.10), custom_call_target="tpu_custom_call" | custom-call | tf_op jit(solution)/shard_map/pallas_call | solution.py:27
  22.3 0.0 copy-start.2
  22.3 0.0 collective-permute-done.3.below
  22.3 0.0 collective-permute-done.2.above
  22.3 0.0 collective-permute-done.1.outer
  22.3 0.0 collective-permute-done.inner
  22.3 0.0 copy-done
  22.3 0.0 copy-done.3
  22.3 0.0 copy-done.4
  22.3 1.0 shard_map.65.field
  23.3 0.0 copy-start.5
  23.3 1.9 %collective-permute-start.7 = (f32[64,128]{1,0:T(8,128)S(1)}, f32[64,128]{1,0:T(8,128)S(1)}, u32[]{:S(2)}, u32[]{:S(2)}) collective-permute-start(f32[64,128]{1,0:T(8,128)S(1)} %shard_map.65.field), channel_id=1, source_target_pairs={{0,1},{1,2},{2,3},{3,4},{4,5},{5,6},{6,7},{8,9},{9,10},{10,11},{11... | collective-permute-start | bytes 98312 | tf_op jit(solution)/shard_map/ppermute | solution.py:255
  25.3 3.9 %collective-permute-start.6 = (f32[64,128]{1,0:T(8,128)S(1)}, f32[64,128]{1,0:T(8,128)S(1)}, u32[]{:S(2)}, u32[]{:S(2)}) collective-permute-start(f32[64,128]{1,0:T(8,128)S(1)} %shard_map.65.field), channel_id=1, source_target_pairs={{1,0},{2,1},{3,2},{4,3},{5,4},{6,5},{7,6},{9,8},{10,9},{11,10},{12... | collective-permute-start | bytes 98312 | tf_op jit(solution)/shard_map/ppermute | solution.py:255
  29.2 0.7 collective-permute-start.5
  29.9 3.1 %collective-permute-start.4 = (f32[64,128]{1,0:T(8,128)S(1)}, f32[64,128]{1,0:T(8,128)S(1)}, u32[]{:S(2)}, u32[]{:S(2)}) collective-permute-start(f32[64,128]{1,0:T(8,128)S(1)} %shard_map.65.field), channel_id=1, source_target_pairs={{0,8},{8,0},{16,24},{24,16},{32,40},{40,32},{48,56},{56,48},{64,72... | collective-permute-start | bytes 98312 | tf_op jit(solution)/shard_map/ppermute | solution.py:262
  33.0 0.0 copy-done.2
  33.0 1.4 %shard_map.66.ops = f32[10,64,8,128]{3,2,1,0:T(8,128)S(1)} custom-call(bf16[8,8,64,160]{3,2,1,0:T(8,128)(2,1)S(1)} %bitcast.11), custom_call_target="tpu_custom_call" | custom-call | tf_op jit(solution)/shard_map/pallas_call | solution.py:27
  34.4 0.0 collective-permute-done.7.below
  34.4 0.0 collective-permute-done.6.above
  34.4 0.0 collective-permute-done.5.outer
  34.4 0.0 collective-permute-done.4.inner
  34.4 0.0 copy-done.5
  34.4 1.2 %shard_map.67 = f32[16,8,128]{2,1,0:T(8,128)S(1)} custom-call(f32[64,128]{1,0:T(8,128)S(1)} %shard_map.65.field, f32[64,128]{1,0:T(8,128)S(1)} %collective-permute-done.4.inner, f32[64,128]{1,0:T(8,128)S(1)} %collective-permute-done.5.outer, f32[64,128]{1,0:T(8,128)S(1)} %collective-permute-done.6.above, f32[64,128]{1,0:T(8,128)S(1)} %collective-permute-done.7.below, ...), custom_call_target="tpu_custom_call" | custom-call | tf_op jit(solution)/shard_map/pallas_call | solution.py:27
  35.6 10.8 %all_to_all.15.received = f32[16,8,128]{2,1,0:T(8,128)S(1)} all-to-all(f32[16,8,128]{2,1,0:T(8,128)S(1)} %shard_map.67), channel_id=1, replica_groups={{0,8,16,24,32,40,48,56,64,72,80,88,96,104,112,120},{128,136,144,152,160..., dimensions={0} | all-to-all | bytes 131072 | tf_op jit(solution)/shard_map/all_to_all | solution.py:272
  46.4 1.0 %shard_map.68 = (f32[8,8,128]{2,1,0:T(8,128)S(1)}, f32[8,8,128]{2,1,0:T(8,128)S(1)}) custom-call(f32[10,64,8,128]{3,2,1,0:T(8,128)S(1)} %shard_map.66.ops, f32[11,64,8,128]{3,2,1,0:T(8,128)S(1)} %shard_map.64.smooth, f32[16,8,128]{2,1,0:T(8,128)S(1)} %all_to_all.15.received), custom_call_target="tpu_custom_call" | custom-call | tf_op jit(solution)/shard_map/pallas_call | solution.py:27
  47.5 22.3 %all_to_all.16.received = f32[8,8,128]{2,1,0:T(8,128)S(1)} all-to-all(f32[8,8,128]{2,1,0:T(8,128)S(1)} %get-tuple-element.21), channel_id=1, replica_groups={{0,128,256,384,512,640,768,896},{8,136,264,392,520,648,776,904},{16,144..., dimensions={0} | all-to-all | bytes 65536 | tf_op jit(solution)/shard_map/all_to_all | solution.py:272
  69.8 0.7 shard_map.69
  70.5 16.1 %all_to_all.17.received = f32[8,8,128]{2,1,0:T(8,128)S(1)} all-to-all(f32[8,8,128]{2,1,0:T(8,128)S(1)} %get-tuple-element.22), channel_id=1, replica_groups=mesh['plan'=128,'height'=8] {'height'}, dimensions={0} | all-to-all | bytes 65536 | tf_op jit(solution)/shard_map/all_to_all | solution.py:272
  86.6 2.8 %shard_map.70.field = f32[64,128]{1,0:T(8,128)S(1)} custom-call(f32[10,64,8,128]{3,2,1,0:T(8,128)S(1)} %shard_map.66.ops, f32[11,64,8,128]{3,2,1,0:T(8,128)S(1)} %shard_map.64.smooth, f32[8,8,128]{2,1,0:T(8,128)S(1)} %all_to_all.17.received, f32[8,8,128]{2,1,0:T(8,128)S(1)} %get-tuple-element.23.low, f32[6,8,128]{2,1,0:T(8,128)S(1)} %get-tuple-element.24.middle, ...), custom_call_target="tpu_custom_call" | custom-call | tf_op jit(solution)/shard_map/pallas_call | solution.py:27
  89.4 2.3 %collective-permute-start.11 = (f32[64,128]{1,0:T(8,128)S(1)}, f32[64,128]{1,0:T(8,128)S(1)}, u32[]{:S(2)}, u32[]{:S(2)}) collective-permute-start(f32[64,128]{1,0:T(8,128)S(1)} %shard_map.70.field), channel_id=1, source_target_pairs={{0,1},{1,2},{2,3},{3,4},{4,5},{5,6},{6,7},{8,9},{9,10},{10,11},{11... | collective-permute-start | bytes 98312 | tf_op jit(solution)/shard_map/ppermute | solution.py:255
  91.7 3.5 %collective-permute-start.10 = (f32[64,128]{1,0:T(8,128)S(1)}, f32[64,128]{1,0:T(8,128)S(1)}, u32[]{:S(2)}, u32[]{:S(2)}) collective-permute-start(f32[64,128]{1,0:T(8,128)S(1)} %shard_map.70.field), channel_id=1, source_target_pairs={{1,0},{2,1},{3,2},{4,3},{5,4},{6,5},{7,6},{9,8},{10,9},{11,10},{12... | collective-permute-start | bytes 98312 | tf_op jit(solution)/shard_map/ppermute | solution.py:255
  95.2 0.7 collective-permute-start.9
  95.9 3.9 %collective-permute-start.8 = (f32[64,128]{1,0:T(8,128)S(1)}, f32[64,128]{1,0:T(8,128)S(1)}, u32[]{:S(2)}, u32[]{:S(2)}) collective-permute-start(f32[64,128]{1,0:T(8,128)S(1)} %shard_map.70.field), channel_id=1, source_target_pairs={{0,8},{8,0},{16,24},{24,16},{32,40},{40,32},{48,56},{56,48},{64,72... | collective-permute-start | bytes 98312 | tf_op jit(solution)/shard_map/ppermute | solution.py:262
  99.8 0.0 collective-permute-done.11.below
  99.8 0.0 collective-permute-done.10.above
  99.8 0.0 collective-permute-done.9.outer
  99.8 0.8 collective-permute-done.8.inner
  100.6 1.6 %shard_map.71 = f32[64,128]{1,0:T(8,128)} custom-call(f32[64,128]{1,0:T(8,128)S(1)} %shard_map.70.field, f32[64,128]{1,0:T(8,128)S(1)} %collective-permute-done.8.inner, f32[64,128]{1,0:T(8,128)S(1)} %collective-permute-done.9.outer, f32[64,128]{1,0:T(8,128)S(1)} %collective-permute-done.10.above, f32[64,128]{1,0:T(8,128)S(1)} %collective-permute-done.11.below, ...), custom_call_target="tpu_custom_call" | custom-call | tf_op jit(solution)/shard_map/pallas_call | solution.py:27
Async XLA Ops:
  0.0 22.3 %copy-start = (bf16[1,1,3,64,64,128]{5,4,3,2,1,0:T(8,128)(2,1)S(1)}, bf16[1,1,3,64,64,128]{5,4,3,2,1,0:T(8,128)(2,1)}, u32[]{:S(2)}) copy-start(bf16[1,1,3,64,64,128]{5,4,3,2,1,0:T(8,128)(2,1)} %param.7) | copy-start | bytes 9437188
  0.0 22.3 %collective-permute-start.3 = (f32[64,128]{1,0:T(8,128)}, f32[64,128]{1,0:T(8,128)S(1)}, u32[]{:S(2)}, u32[]{:S(2)}) collective-permute-start(f32[64,128]{1,0:T(8,128)} %bitcast.12), channel_id=1, source_target_pairs={{0,1},{1,2},{2,3},{3,4},{4,5},{5,6},{6,7},{8,9},{9,10},{10,11},{11... | collective-permute-start | bytes 98312 | tf_op jit(solution)/shard_map/ppermute | solution.py:255
  3.7 18.6 %collective-permute-start.2 = (f32[64,128]{1,0:T(8,128)}, f32[64,128]{1,0:T(8,128)S(1)}, u32[]{:S(2)}, u32[]{:S(2)}) collective-permute-start(f32[64,128]{1,0:T(8,128)} %bitcast.13), channel_id=1, source_target_pairs={{1,0},{2,1},{3,2},{4,3},{5,4},{6,5},{7,6},{9,8},{10,9},{11,10},{12... | collective-permute-start | bytes 98312 | tf_op jit(solution)/shard_map/ppermute | solution.py:255
  16.7 5.6 %collective-permute-start.1 = (f32[64,128]{1,0:T(8,128)}, f32[64,128]{1,0:T(8,128)S(1)}, u32[]{:S(2)}, u32[]{:S(2)}) collective-permute-start(f32[64,128]{1,0:T(8,128)} %bitcast.14), channel_id=1, source_target_pairs={{8,16},{16,8},{24,32},{32,24},{40,48},{48,40},{56,64},{64,56},{72,... | collective-permute-start | bytes 98312 | tf_op jit(solution)/shard_map/ppermute | solution.py:262
  17.3 5.0 %collective-permute-start = (f32[64,128]{1,0:T(8,128)}, f32[64,128]{1,0:T(8,128)S(1)}, u32[]{:S(2)}, u32[]{:S(2)}) collective-permute-start(f32[64,128]{1,0:T(8,128)} %bitcast.15), channel_id=1, source_target_pairs={{0,8},{8,0},{16,24},{24,16},{32,40},{40,32},{48,56},{56,48},{64,72... | collective-permute-start | bytes 98312 | tf_op jit(solution)/shard_map/ppermute | solution.py:262
  19.3 1.6 %copy-start.1 = (bf16[64,64,176]{2,1,0:T(8,128)(2,1)S(1)}, bf16[64,64,176]{2,1,0:T(8,128)(2,1)}, u32[]{:S(2)}) copy-start(bf16[64,64,176]{2,1,0:T(8,128)(2,1)} %param.11) | copy-start | bytes 4325380
  20.8 1.5 %copy-start.3 = (f32[1,1,64,128]{3,2,1,0:T(8,128)S(1)}, f32[1,1,64,128]{3,2,1,0:T(8,128)}, u32[]{:S(2)}) copy-start(f32[1,1,64,128]{3,2,1,0:T(8,128)} %param.6) | copy-start | bytes 98308
  20.8 1.5 %copy-start.4 = (s32[1,1,3,128]{3,1,2,0:T(1,128)S(1)}, s32[1,1,3,128]{3,1,2,0:T(1,128)}, u32[]{:S(2)}) copy-start(s32[1,1,3,128]{3,1,2,0:T(1,128)} %param.8) | copy-start | bytes 4612
  22.3 10.7 %copy-start.2 = (bf16[64,64,160]{2,1,0:T(8,128)(2,1)S(1)}, bf16[64,64,160]{2,1,0:T(8,128)(2,1)}, u32[]{:S(2)}) copy-start(bf16[64,64,160]{2,1,0:T(8,128)(2,1)} %param.10) | copy-start | bytes 3932164
  23.3 11.1 %copy-start.5 = (s32[1,1,128]{2,1,0:T(1,128)S(1)}, s32[1,1,128]{2,1,0:T(1,128)}, u32[]{:S(2)}) copy-start(s32[1,1,128]{2,1,0:T(1,128)} %param.9) | copy-start | bytes 1540
  23.3 11.1 %collective-permute-start.7 = (f32[64,128]{1,0:T(8,128)S(1)}, f32[64,128]{1,0:T(8,128)S(1)}, u32[]{:S(2)}, u32[]{:S(2)}) collective-permute-start(f32[64,128]{1,0:T(8,128)S(1)} %shard_map.65.field), channel_id=1, source_target_pairs={{0,1},{1,2},{2,3},{3,4},{4,5},{5,6},{6,7},{8,9},{9,10},{10,11},{11... | collective-permute-start | bytes 98312 | tf_op jit(solution)/shard_map/ppermute | solution.py:255
  25.3 9.1 %collective-permute-start.6 = (f32[64,128]{1,0:T(8,128)S(1)}, f32[64,128]{1,0:T(8,128)S(1)}, u32[]{:S(2)}, u32[]{:S(2)}) collective-permute-start(f32[64,128]{1,0:T(8,128)S(1)} %shard_map.65.field), channel_id=1, source_target_pairs={{1,0},{2,1},{3,2},{4,3},{5,4},{6,5},{7,6},{9,8},{10,9},{11,10},{12... | collective-permute-start | bytes 98312 | tf_op jit(solution)/shard_map/ppermute | solution.py:255
  29.2 5.2 %collective-permute-start.5 = (f32[64,128]{1,0:T(8,128)S(1)}, f32[64,128]{1,0:T(8,128)S(1)}, u32[]{:S(2)}, u32[]{:S(2)}) collective-permute-start(f32[64,128]{1,0:T(8,128)S(1)} %shard_map.65.field), channel_id=1, source_target_pairs={{8,16},{16,8},{24,32},{32,24},{40,48},{48,40},{56,64},{64,56},{72,... | collective-permute-start | bytes 98312 | tf_op jit(solution)/shard_map/ppermute | solution.py:262
  29.9 4.6 %collective-permute-start.4 = (f32[64,128]{1,0:T(8,128)S(1)}, f32[64,128]{1,0:T(8,128)S(1)}, u32[]{:S(2)}, u32[]{:S(2)}) collective-permute-start(f32[64,128]{1,0:T(8,128)S(1)} %shard_map.65.field), channel_id=1, source_target_pairs={{0,8},{8,0},{16,24},{24,16},{32,40},{40,32},{48,56},{56,48},{64,72... | collective-permute-start | bytes 98312 | tf_op jit(solution)/shard_map/ppermute | solution.py:262
  89.4 10.4 %collective-permute-start.11 = (f32[64,128]{1,0:T(8,128)S(1)}, f32[64,128]{1,0:T(8,128)S(1)}, u32[]{:S(2)}, u32[]{:S(2)}) collective-permute-start(f32[64,128]{1,0:T(8,128)S(1)} %shard_map.70.field), channel_id=1, source_target_pairs={{0,1},{1,2},{2,3},{3,4},{4,5},{5,6},{6,7},{8,9},{9,10},{10,11},{11... | collective-permute-start | bytes 98312 | tf_op jit(solution)/shard_map/ppermute | solution.py:255
  91.7 8.1 %collective-permute-start.10 = (f32[64,128]{1,0:T(8,128)S(1)}, f32[64,128]{1,0:T(8,128)S(1)}, u32[]{:S(2)}, u32[]{:S(2)}) collective-permute-start(f32[64,128]{1,0:T(8,128)S(1)} %shard_map.70.field), channel_id=1, source_target_pairs={{1,0},{2,1},{3,2},{4,3},{5,4},{6,5},{7,6},{9,8},{10,9},{11,10},{12... | collective-permute-start | bytes 98312 | tf_op jit(solution)/shard_map/ppermute | solution.py:255
  95.2 4.6 %collective-permute-start.9 = (f32[64,128]{1,0:T(8,128)S(1)}, f32[64,128]{1,0:T(8,128)S(1)}, u32[]{:S(2)}, u32[]{:S(2)}) collective-permute-start(f32[64,128]{1,0:T(8,128)S(1)} %shard_map.70.field), channel_id=1, source_target_pairs={{8,16},{16,8},{24,32},{32,24},{40,48},{48,40},{56,64},{64,56},{72,... | collective-permute-start | bytes 98312 | tf_op jit(solution)/shard_map/ppermute | solution.py:262
  95.9 4.7 %collective-permute-start.8 = (f32[64,128]{1,0:T(8,128)S(1)}, f32[64,128]{1,0:T(8,128)S(1)}, u32[]{:S(2)}, u32[]{:S(2)}) collective-permute-start(f32[64,128]{1,0:T(8,128)S(1)} %shard_map.70.field), channel_id=1, source_target_pairs={{0,8},{8,0},{16,24},{24,16},{32,40},{40,32},{48,56},{56,48},{64,72... | collective-permute-start | bytes 98312 | tf_op jit(solution)/shard_map/ppermute | solution.py:262

commit v3 on v2

--- a/solution.py
+++ b/solution.py
@@ -16,6 +16,8 @@
 GROUPS = BS // SUB
 F32 = jnp.float32
 MIB = 1 << 20
+HALF_ROOT = 0.7071067811865476
+BATCH = 4
 
 
 def whole(count):
@@ -90,7 +92,7 @@
     lax.fori_loop(0, GROUPS, body, 0)
 
 
-def first_body(source, inner, outer, above, below, weights, links, second):
+def first_body(source, inner, outer, above, below, weights, links, owners, second):
     fields = [ref[...] for ref in (source, inner, outer, above, below)]
     picked = pick(fields, links)
 
@@ -100,10 +102,11 @@
         second[rows, :] = 0.5 * mine + 0.5 * (mine - applied)
 
     tiles(step)
+    second[BS:, :] = jnp.broadcast_to(owners[...].astype(F32), (SUB, NB))
 
 
 def second_body(field, inner, outer, above, below, weights, links, source, owners, sent, left):
-    fields = [ref[...] for ref in (field, inner, outer, above, below)]
+    fields = [ref[0:BS, :] for ref in (field, inner, outer, above, below)]
     picked = pick(fields, links)
 
     def step(tile, rows):
@@ -127,12 +130,18 @@
         sent[copy] = packed
 
 
-def last_body(field, inner, outer, above, below, weights, links, source, out):
-    fields = [ref[...] for ref in (field, inner, outer, above, below)]
+def last_body(field, inner, outer, above, below, errors, weights, links, source, out, third):
+    fields = []
+    for number, ref in enumerate((field, inner, outer, above, below)):
+        error = errors[number]
+        owner = ref[BS:, :].astype(jnp.int32)
+        added = [take_lanes(error, owner + group * NC) for group in range(GROUPS)]
+        fields.append(ref[0:BS, :] + jnp.concatenate(added, axis=0))
+    third[...] = fields[0]
     picked = pick(fields, links)
 
     def step(tile, rows):
-        mine = field[rows, :]
+        mine = third[rows, :]
         applied = mine + coupled(weights, picked, tile)
         out[rows, :] = mine + 0.5 * (source[rows, :] - applied)
 
@@ -188,6 +197,9 @@
 
 
 def block_product(packed, level, vectors, turned):
+    if len(vectors) > BATCH:
+        parts = [vectors[i : i + BATCH] for i in range(0, len(vectors), BATCH)]
+        return [out for part in parts for out in block_product(packed, level, part, turned)]
     lane = iota((SUB, NB), 1) & (NC - 1)
     totals = [[None] * SUB for _ in vectors]
     for column in range(GROUPS):
@@ -201,52 +213,134 @@
     return [fold(total) for total in totals]
 
 
-def climb(ops, smooth, first_level, received, me, kept):
-    count = received.shape[0].bit_length() - 1
-    columns = [received[me]]
-    for bits in range(1, count + 1):
-        start = (me >> bits) << bits
-        total = received[start]
-        for other in range(1, 2**bits):
-            total = total + received[start + other]
-        columns.append(total * 2.0 ** (-bits / 2))
-    for step in range(count):
-        level = first_level + step
-        smoothed = block_product(smooth, level, columns, max(level - 1, 0))
-        if level > 0:
-            columns = [pltpu.roll(v, NC, 1) for v in columns]
-        kept[2 * step] = columns[0]
-        kept[2 * step + 1] = smoothed[0]
-        removed = block_product(ops, level, smoothed[1:], level)
-        columns = [a - b for a, b in zip(columns[1:], removed)]
-    return columns[0]
-
-
-def climb_body(first_level, ops, smooth, received, sent, kept):
-    me = (lax.axis_index("plan") >> first_level) & (received.shape[0] - 1)
-    top = climb(ops, smooth, first_level, received, me, kept)
+def up_step(ops, smooth, level, lows, highs):
+    columns = lows + highs
+    smoothed = block_product(smooth, level, columns, max(level - 1, 0))
+    if level > 0:
+        columns = [pltpu.roll(v, NC, 1) for v in columns]
+    removed = block_product(ops, level, smoothed[len(lows) :], level)
+    saved = list(zip(columns, smoothed[: len(lows)]))
+    return saved, [a - b for a, b in zip(columns[len(lows) :], removed)]
+
+
+def down_step(ops, smooth, level, errors, saved):
+    totals = []
+    for number, error in enumerate(errors):
+        total = pltpu.roll(saved[number][1], NC, 1) if saved else error
+        totals.append(total if error is None or not saved else total + error)
+    applied = block_product(ops, level, totals, level + 1)
+    if saved:
+        applied = [a - g for a, (g, _) in zip(applied, saved)]
+    fixed = block_product(smooth, level, applied, level)
+    return [pltpu.roll(t, NB - NC, 1) - f for t, f in zip(totals, fixed)]
+
+
+def group_sum(load, member, bits):
+    start = (member >> bits) << bits
+    total = load(start)
+    for other in range(1, 2**bits):
+        total = total + load(start + other)
+    return total * 2.0 ** (-bits / 2)
+
+
+def near_body(ops, smooth, received, sent, kept):
+    count = received.shape[0]
+    bits = count.bit_length() - 1
+    me = lax.axis_index("plan") & (count - 1)
+    across = (((me - 1) ^ 1) + 1) & (count - 1)
+    load = lambda n: received[n]
+    lows = [load(me), load(me ^ 1), load(across)]
+    highs = []
+    for level in range(1, bits):
+        highs += [group_sum(load, me, level), group_sum(load, across, level)]
+    highs.append(group_sum(load, me, bits))
+    saved = []
+    for level in range(bits):
+        pairs, rest = up_step(ops, smooth, level, lows, highs)
+        saved.append(pairs)
+        lows, highs = rest[:2], rest[2:]
+    errors = [None, None]
+    for level in reversed(range(1, bits)):
+        errors = down_step(ops, smooth, level, errors, saved[level])
+    errors = down_step(ops, smooth, 0, [errors[0], errors[0], errors[1]], saved[0])
     for copy in range(sent.shape[0]):
-        sent[copy] = top
-
-
-def turn_body(ops, smooth, received, low, middle, field, owners, third, high):
-    levels = [
-        (saved, 2 * place)
-        for saved in (low, middle, high)
-        for place in range(saved.shape[0] // 2)
+        sent[copy, 0] = lows[0]
+        sent[copy, 1] = errors[2]
+    kept[0] = errors[0]
+    kept[1] = errors[1]
+
+
+def far_body(first, ops, smooth, received, near, sent, kept):
+    count = received.shape[0]
+    bits = count.bit_length() - 1
+    members = 2**first
+    place = lax.axis_index("plan")
+    me, inside = place >> first, place & (members - 1)
+    across = me - (inside == 0).astype(jnp.int32) + (inside == members - 1).astype(jnp.int32)
+    across = jnp.clip(across, 0, count - 1)
+    load = lambda n: received[n, 0]
+    lows = [load(me), load(across)]
+    highs = []
+    for level in range(1, bits):
+        highs += [group_sum(load, me, level), group_sum(load, across, level)]
+    highs.append(group_sum(load, me, bits))
+    saved = []
+    for level in range(bits):
+        pairs, rest = up_step(ops, smooth, first + level, lows, highs)
+        saved.append(pairs)
+        lows, highs = rest[:2], rest[2:]
+    errors = [None, None]
+    for level in reversed(range(bits)):
+        errors = down_step(ops, smooth, first + level, errors, saved[level])
+    for copy in range(sent.shape[0]):
+        sent[copy, 0] = lows[0]
+        sent[copy, 1] = near[0]
+        sent[copy, 2] = errors[0]
+    kept[0] = errors[1]
+    kept[1] = received[across, 1]
+
+
+def top_body(first, middle, ops, smooth, received, near, far, errors, tree):
+    count = received.shape[0]
+    bits = count.bit_length() - 1
+    me, place = lax.axis_index("height"), lax.axis_index("plan")
+    last = lax.axis_size("plan") - 1
+    targets = (me, jnp.minimum(me + 1, count - 1), jnp.maximum(me - 1, 0))
+    values = [received[n, 0] for n in range(count)]
+    starts = []
+    used = 0
+    for level in range(first, LEVELS):
+        pairs, _ = up_step(ops, smooth, level, values, [])
+        removed = block_product(ops, level, [z for _, z in pairs], level)
+        starts.append(used)
+        for g, z in pairs:
+            tree[used, 0] = g
+            tree[used, 1] = z
+            used += 1
+        rest = [g - r for (g, _), r in zip(pairs, removed)]
+        values = [(a + b) * HALF_ROOT for a, b in zip(rest[0::2], rest[1::2])]
+    (error,) = block_product(smooth, LEVELS, values, LEVELS - 1)
+    parts = [error] * len(targets)
+    for level in reversed(range(first, LEVELS)):
+        at = [starts[level - first] + (target >> (level - first)) for target in targets]
+        saved = [(tree[n, 0], tree[n, 1]) for n in at]
+        parts = down_step(ops, smooth, level, parts, saved)
+    for level in reversed(range(middle, first)):
+        parts = down_step(ops, smooth, level, parts, None)
+    parts = [
+        parts[0] + received[targets[0], 2],
+        parts[0] + far[0],
+        parts[1] + received[targets[1], 2],
+        parts[2] + received[targets[2], 2],
     ]
-    top = climb(ops, smooth, (low.shape[0] + middle.shape[0]) // 2, received, lax.axis_index("height"), high)
-    (error,) = block_product(smooth, LEVELS, [top], LEVELS - 1)
-    for level in reversed(range(LEVELS)):
-        saved, place = levels[level]
-        error = pltpu.roll(saved[place + 1], NC, 1) + error
-        (applied,) = block_product(ops, level, [error], level + 1)
-        (fixed,) = block_product(smooth, level, [saved[place] - applied], level)
-        error = pltpu.roll(error, NB - NC, 1) + fixed
-    owner = jnp.broadcast_to(owners[...], (SUB, NB))
-    for group in range(GROUPS):
-        rows = slice(group * SUB, (group + 1) * SUB)
-        third[rows, :] = field[rows, :] + take_lanes(error, owner + group * NC)
+    for level in reversed(range(middle)):
+        parts = down_step(ops, smooth, level, parts, None)
+    zero = jnp.zeros((SUB, NB), F32)
+    errors[0] = parts[0] + near[0]
+    errors[1] = parts[0] + near[1]
+    errors[2] = jnp.where((place > 0) & (place < last), parts[1] + far[1], zero)
+    errors[3] = jnp.where(me < count - 1, parts[2] + received[targets[1], 1], zero)
+    errors[4] = jnp.where(me > 0, parts[3] + received[targets[2], 1], zero)
 
 
 def shifted(value, step):
@@ -285,13 +379,18 @@
     far = plan // near
     field_shape = jax.ShapeDtypeStruct((BS, NB), F32)
 
-    def vectors(count):
-        return jax.ShapeDtypeStruct((count, SUB, NB), F32)
+    def vectors(*counts):
+        return jax.ShapeDtypeStruct((*counts, SUB, NB), F32)
 
     smooth = pack(coarse_smooth)
     around = halo(source)
     smooth, source = lax.optimization_barrier((smooth, source))
-    second = call(first_body, field_shape, (source, *around, weights, links), 12 * MIB)
+    second = call(
+        first_body,
+        jax.ShapeDtypeStruct((BS + SUB, NB), F32),
+        (source, *around, weights, links, owners),
+        12 * MIB,
+    )
     around = halo(second)
     second, coarse_ops = lax.optimization_barrier((second, coarse_ops))
     ops = pack(coarse_ops)
@@ -306,29 +405,30 @@
     near_groups = [[a * near + b for b in range(near)] for a in range(far)]
     far_groups = [[a * near + b for a in range(far)] for b in range(near)]
     received = exchange(sent, "plan", near_groups)
-    sent, low = call(
-        functools.partial(climb_body, 0),
-        (vectors(far), vectors(2 * low_bits)),
-        (ops, smooth, received),
+    sent, near_kept = call(
+        near_body, (vectors(far, 2), vectors(2)), (ops, smooth, received), 16 * MIB
+    )
+    received = exchange(sent, "plan", far_groups)
+    sent, far_kept = call(
+        functools.partial(far_body, low_bits),
+        (vectors(height, 3), vectors(2)),
+        (ops, smooth, received, near_kept),
         16 * MIB,
     )
-    received = exchange(sent, "plan", far_groups)
-    sent, middle = call(
-        functools.partial(climb_body, low_bits),
-        (vectors(height), vectors(2 * (plan_bits - low_bits))),
-        (ops, smooth, received),
+    received = exchange(sent, "height")
+    errors = call(
+        functools.partial(top_body, plan_bits, low_bits),
+        vectors(5),
+        (ops, smooth, received, near_kept, far_kept),
         16 * MIB,
-    )
-    received = exchange(sent, "height")
-    third = call(
-        turn_body,
+        [pltpu.VMEM((2 * height, 2, SUB, NB), F32)],
+    )
+    out = call(
+        last_body,
         field_shape,
-        (ops, smooth, received, low, middle, second, owners),
-        16 * MIB,
-        [pltpu.VMEM((2 * (LEVELS - plan_bits), SUB, NB), F32)],
-    )
-    out = call(
-        last_body, field_shape, (third, *halo(third), weights, links, source), 12 * MIB
+        (second, *around, errors, weights, links, source),
+        12 * MIB,
+        [pltpu.VMEM((BS, NB), F32)],
     )
     return out[None, None]
 

time: 103 us -> 95.6 us (0.928)
  starting transfers between devices: 39.2 us -> 28.8 us
  Pallas kernels: 11.1 us -> 14.2 us
    ppermute x6 -> x4, starting transfers between devices: 28.3 us -> 22.5 us  [shifted(): return lax.ppermute(value, 'height', pairs)]
    ppermute x6 -> x4, starting transfers between devices: 10.9 us -> 6.35 us  [swapped(): return lax.ppermute(value, 'plan', pairs)]
    pallas_call x8, Pallas kernels: 11.1 us -> 14.2 us  [call(): pl.pallas_call(body, out_shape=out_shape, in_specs=whole(len(inputs)), ou...]
    all_to_all x3, blocking collectives: 49.2 us -> 50.2 us  [exchange(): lax.all_to_all(value, axis, 0, 0, axis_index_groups=groups, tiled=True)]
  transfers between devices with their start and end apart: 12 -> 8, of which waited for: 1 -> 0; matrix products, arithmetic and copies ran while one was open for 0% -> 0% of each run, Pallas kernels for 3% -> 3%
where the time goes in v3:
time: 95.6 us; the launch traced here: 95.2 us
  blocking collectives  50.2 us (53%)
  starting transfers between devices  28.8 us (30%)
  Pallas kernels  14.2 us (15%)
  local copies, waits for them, and re-layouts  1.61 us (2%)
    all_to_all x3, blocking collectives, exchange(): lax.all_to_all(value, axis, 0, 0, axis_index_groups=groups, tiled=True)  50.2 us
    ppermute x4, starting transfers between devices, shifted(): return lax.ppermute(value, 'height', pairs)  22.5 us
    pallas_call x8, Pallas kernels, call(): pl.pallas_call(body, out_shape=out_shape, in_specs=whole(len(inputs)), ou...  14.2 us
    ppermute x4, starting transfers between devices, swapped(): return lax.ppermute(value, 'plan', pairs)  6.35 us
  transfers between devices with their start and end apart: 8, of which 0 were waited for; matrix products, arithmetic and copies ran while one was open for 0% of the time, Pallas kernels for 3%

profile of v3, /device:TPU:2, one launch (start us, length us, event | category | flops | bytes accessed | tf_op | source)
XLA Modules:
  0.0 95.2 jit_solution(7525118839488941956)
XLA Ops:
  0.0 0.0 copy-start
  0.0 3.6 %collective-permute-start.3 = (f32[64,128]{1,0:T(8,128)}, f32[64,128]{1,0:T(8,128)S(1)}, u32[]{:S(2)}, u32[]{:S(2)}) collective-permute-start(f32[64,128]{1,0:T(8,128)} %bitcast.12), channel_id=1, source_target_pairs={{0,1},{1,2},{2,3},{3,4},{4,5},{5,6},{6,7},{8,9},{9,10},{10,11},{11... | collective-permute-start | bytes 98312 | tf_op jit(solution)/shard_map/ppermute | solution.py:349
  3.7 13.0 %collective-permute-start.2 = (f32[64,128]{1,0:T(8,128)}, f32[64,128]{1,0:T(8,128)S(1)}, u32[]{:S(2)}, u32[]{:S(2)}) collective-permute-start(f32[64,128]{1,0:T(8,128)} %bitcast.13), channel_id=1, source_target_pairs={{1,0},{2,1},{3,2},{4,3},{5,4},{6,5},{7,6},{9,8},{10,9},{11,10},{12... | collective-permute-start | bytes 98312 | tf_op jit(solution)/shard_map/ppermute | solution.py:349
  16.7 0.7 collective-permute-start.1
  17.3 1.9 %collective-permute-start = (f32[64,128]{1,0:T(8,128)}, f32[64,128]{1,0:T(8,128)S(1)}, u32[]{:S(2)}, u32[]{:S(2)}) collective-permute-start(f32[64,128]{1,0:T(8,128)} %bitcast.15), channel_id=1, source_target_pairs={{0,8},{8,0},{16,24},{24,16},{32,40},{40,32},{48,56},{56,48},{64,72... | collective-permute-start | bytes 98312 | tf_op jit(solution)/shard_map/ppermute | solution.py:356
  19.3 0.0 copy-start.1
  19.3 1.6 %copy-done.1 = bf16[64,64,176]{2,1,0:T(8,128)(2,1)S(1)} copy-done((bf16[64,64,176]{2,1,0:T(8,128)(2,1)S(1)}, bf16[64,64,176]{2,1,0:T(8,128)(2,1)}, u32[]{:S(2)}) %copy-start.1) | copy-done | bytes 1441816
  20.8 0.0 copy-start.3
  20.8 0.0 copy-start.4
  20.8 0.0 copy-start.5
  20.9 1.4 %shard_map.64.smooth = f32[11,64,8,128]{3,2,1,0:T(8,128)S(1)} custom-call(bf16[8,8,64,176]{3,2,1,0:T(8,128)(2,1)S(1)} %bitcast.10), custom_call_target="tpu_custom_call" | custom-call | tf_op jit(solution)/shard_map/pallas_call | solution.py:29
  22.3 0.0 copy-start.2
  22.3 0.0 collective-permute-done.3.below
  22.3 0.0 collective-permute-done.2.above
  22.3 0.0 collective-permute-done.1.outer
  22.3 0.0 collective-permute-done.inner
  22.3 0.0 copy-done
  22.3 0.0 copy-done.3
  22.3 0.0 copy-done.4
  22.3 0.0 copy-done.5
  22.4 1.0 %shard_map.65.field = f32[72,128]{1,0:T(8,128)S(1)} custom-call(f32[64,128]{1,0:T(8,128)S(1)} %bitcast.16, f32[64,128]{1,0:T(8,128)S(1)} %collective-permute-done.inner, f32[64,128]{1,0:T(8,128)S(1)} %collective-permute-done.1.outer, f32[64,128]{1,0:T(8,128)S(1)} %collective-permute-done.2.above, f32[64,128]{1,0:T(8,128)S(1)} %collective-permute-done.3.below, ...), custom_call_target="tpu_custom_call" | custom-call | tf_op jit(solution)/shard_map/pallas_call | solution.py:29
  23.3 1.9 %collective-permute-start.7 = (f32[72,128]{1,0:T(8,128)S(1)}, f32[72,128]{1,0:T(8,128)S(1)}, u32[]{:S(2)}, u32[]{:S(2)}) collective-permute-start(f32[72,128]{1,0:T(8,128)S(1)} %shard_map.65.field), channel_id=1, source_target_pairs={{0,1},{1,2},{2,3},{3,4},{4,5},{5,6},{6,7},{8,9},{9,10},{10,11},{11... | collective-permute-start | bytes 110600 | tf_op jit(solution)/shard_map/ppermute | solution.py:349
  25.3 3.9 %collective-permute-start.6 = (f32[72,128]{1,0:T(8,128)S(1)}, f32[72,128]{1,0:T(8,128)S(1)}, u32[]{:S(2)}, u32[]{:S(2)}) collective-permute-start(f32[72,128]{1,0:T(8,128)S(1)} %shard_map.65.field), channel_id=1, source_target_pairs={{1,0},{2,1},{3,2},{4,3},{5,4},{6,5},{7,6},{9,8},{10,9},{11,10},{12... | collective-permute-start | bytes 110600 | tf_op jit(solution)/shard_map/ppermute | solution.py:349
  29.2 0.7 collective-permute-start.5
  29.9 3.1 %collective-permute-start.4 = (f32[72,128]{1,0:T(8,128)S(1)}, f32[72,128]{1,0:T(8,128)S(1)}, u32[]{:S(2)}, u32[]{:S(2)}) collective-permute-start(f32[72,128]{1,0:T(8,128)S(1)} %shard_map.65.field), channel_id=1, source_target_pairs={{0,8},{8,0},{16,24},{24,16},{32,40},{40,32},{48,56},{56,48},{64,72... | collective-permute-start | bytes 110600 | tf_op jit(solution)/shard_map/ppermute | solution.py:356
  33.0 0.0 copy-done.2
  33.0 1.4 %shard_map.66.ops = f32[10,64,8,128]{3,2,1,0:T(8,128)S(1)} custom-call(bf16[8,8,64,160]{3,2,1,0:T(8,128)(2,1)S(1)} %bitcast.11), custom_call_target="tpu_custom_call" | custom-call | tf_op jit(solution)/shard_map/pallas_call | solution.py:29
  34.4 0.0 collective-permute-done.7.below
  34.4 0.0 collective-permute-done.6.above
  34.4 0.0 collective-permute-done.5.outer
  34.4 0.0 collective-permute-done.4.inner
  34.4 1.2 %shard_map.67 = f32[16,8,128]{2,1,0:T(8,128)S(1)} custom-call(f32[72,128]{1,0:T(8,128)S(1)} %shard_map.65.field, f32[72,128]{1,0:T(8,128)S(1)} %collective-permute-done.4.inner, f32[72,128]{1,0:T(8,128)S(1)} %collective-permute-done.5.outer, f32[72,128]{1,0:T(8,128)S(1)} %collective-permute-done.6.above, f32[72,128]{1,0:T(8,128)S(1)} %collective-permute-done.7.below, ...), custom_call_target="tpu_custom_call" | custom-call | tf_op jit(solution)/shard_map/pallas_call | solution.py:29
  35.6 10.8 %all_to_all.15.received = f32[16,8,128]{2,1,0:T(8,128)S(1)} all-to-all(f32[16,8,128]{2,1,0:T(8,128)S(1)} %shard_map.67), channel_id=1, replica_groups={{0,8,16,24,32,40,48,56,64,72,80,88,96,104,112,120},{128,136,144,152,160..., dimensions={0} | all-to-all | bytes 131072 | tf_op jit(solution)/shard_map/all_to_all | solution.py:366
  46.4 2.1 %shard_map.68 = (f32[8,2,8,128]{3,2,1,0:T(8,128)S(1)}, f32[2,8,128]{2,1,0:T(8,128)S(1)}) custom-call(f32[10,64,8,128]{3,2,1,0:T(8,128)S(1)} %shard_map.66.ops, f32[11,64,8,128]{3,2,1,0:T(8,128)S(1)} %shard_map.64.smooth, f32[16,8,128]{2,1,0:T(8,128)S(1)} %all_to_all.15.received), custom_call_target="tpu_custom_call" | custom-call | tf_op jit(solution)/shard_map/pallas_call | solution.py:29
  48.5 22.7 %all_to_all.16.received = f32[8,2,8,128]{3,2,1,0:T(8,128)S(1)} all-to-all(f32[8,2,8,128]{3,2,1,0:T(8,128)S(1)} %get-tuple-element.21), channel_id=1, replica_groups={{0,128,256,384,512,640,768,896},{8,136,264,392,520,648,776,904},{16,144..., dimensions={0} | all-to-all | bytes 131072 | tf_op jit(solution)/shard_map/all_to_all | solution.py:366
  71.2 1.5 %shard_map.69 = (f32[8,3,8,128]{3,2,1,0:T(8,128)S(1)}, f32[2,8,128]{2,1,0:T(8,128)S(1)}) custom-call(f32[10,64,8,128]{3,2,1,0:T(8,128)S(1)} %shard_map.66.ops, f32[11,64,8,128]{3,2,1,0:T(8,128)S(1)} %shard_map.64.smooth, f32[8,2,8,128]{3,2,1,0:T(8,128)S(1)} %all_to_all.16.received, f32[2,8,128]{2,1,0:T(8,128)S(1)} %get-tuple-element.22.near), custom_call_target="tpu_custom_call" | custom-call | tf_op jit(solution)/shard_map/pallas_call | solution.py:29
  72.7 16.8 %all_to_all.17.received = f32[8,3,8,128]{3,2,1,0:T(8,128)S(1)} all-to-all(f32[8,3,8,128]{3,2,1,0:T(8,128)S(1)} %get-tuple-element.23), channel_id=1, replica_groups=mesh['plan'=128,'height'=8] {'height'}, dimensions={0} | all-to-all | bytes 196608 | tf_op jit(solution)/shard_map/all_to_all | solution.py:366
  89.5 3.9 %shard_map.70.errors = f32[5,8,128]{2,1,0:T(8,128)S(1)} custom-call(f32[10,64,8,128]{3,2,1,0:T(8,128)S(1)} %shard_map.66.ops, f32[11,64,8,128]{3,2,1,0:T(8,128)S(1)} %shard_map.64.smooth, f32[8,3,8,128]{3,2,1,0:T(8,128)S(1)} %all_to_all.17.received, f32[2,8,128]{2,1,0:T(8,128)S(1)} %get-tuple-element.22.near, f32[2,8,128]{2,1,0:T(8,128)S(1)} %get-tuple-element.24.far), custom_call_target="tpu_custom_call" | custom-call | tf_op jit(solution)/shard_map/pallas_call | solution.py:29
  93.4 1.7 %shard_map.71 = f32[64,128]{1,0:T(8,128)} custom-call(f32[72,128]{1,0:T(8,128)S(1)} %shard_map.65.field, f32[72,128]{1,0:T(8,128)S(1)} %collective-permute-done.4.inner, f32[72,128]{1,0:T(8,128)S(1)} %collective-permute-done.5.outer, f32[72,128]{1,0:T(8,128)S(1)} %collective-permute-done.6.above, f32[72,128]{1,0:T(8,128)S(1)} %collective-permute-done.7.below, ...), custom_call_target="tpu_custom_call" | custom-call | tf_op jit(solution)/shard_map/pallas_call | solution.py:29
Async XLA Ops:
  0.0 22.3 %copy-start = (bf16[1,1,3,64,64,128]{5,4,3,2,1,0:T(8,128)(2,1)S(1)}, bf16[1,1,3,64,64,128]{5,4,3,2,1,0:T(8,128)(2,1)}, u32[]{:S(2)}) copy-start(bf16[1,1,3,64,64,128]{5,4,3,2,1,0:T(8,128)(2,1)} %param.7) | copy-start | bytes 9437188
  0.0 22.3 %collective-permute-start.3 = (f32[64,128]{1,0:T(8,128)}, f32[64,128]{1,0:T(8,128)S(1)}, u32[]{:S(2)}, u32[]{:S(2)}) collective-permute-start(f32[64,128]{1,0:T(8,128)} %bitcast.12), channel_id=1, source_target_pairs={{0,1},{1,2},{2,3},{3,4},{4,5},{5,6},{6,7},{8,9},{9,10},{10,11},{11... | collective-permute-start | bytes 98312 | tf_op jit(solution)/shard_map/ppermute | solution.py:349
  3.7 18.6 %collective-permute-start.2 = (f32[64,128]{1,0:T(8,128)}, f32[64,128]{1,0:T(8,128)S(1)}, u32[]{:S(2)}, u32[]{:S(2)}) collective-permute-start(f32[64,128]{1,0:T(8,128)} %bitcast.13), channel_id=1, source_target_pairs={{1,0},{2,1},{3,2},{4,3},{5,4},{6,5},{7,6},{9,8},{10,9},{11,10},{12... | collective-permute-start | bytes 98312 | tf_op jit(solution)/shard_map/ppermute | solution.py:349
  16.7 5.6 %collective-permute-start.1 = (f32[64,128]{1,0:T(8,128)}, f32[64,128]{1,0:T(8,128)S(1)}, u32[]{:S(2)}, u32[]{:S(2)}) collective-permute-start(f32[64,128]{1,0:T(8,128)} %bitcast.14), channel_id=1, source_target_pairs={{8,16},{16,8},{24,32},{32,24},{40,48},{48,40},{56,64},{64,56},{72,... | collective-permute-start | bytes 98312 | tf_op jit(solution)/shard_map/ppermute | solution.py:356
  17.3 5.0 %collective-permute-start = (f32[64,128]{1,0:T(8,128)}, f32[64,128]{1,0:T(8,128)S(1)}, u32[]{:S(2)}, u32[]{:S(2)}) collective-permute-start(f32[64,128]{1,0:T(8,128)} %bitcast.15), channel_id=1, source_target_pairs={{0,8},{8,0},{16,24},{24,16},{32,40},{40,32},{48,56},{56,48},{64,72... | collective-permute-start | bytes 98312 | tf_op jit(solution)/shard_map/ppermute | solution.py:356
  19.3 1.6 %copy-start.1 = (bf16[64,64,176]{2,1,0:T(8,128)(2,1)S(1)}, bf16[64,64,176]{2,1,0:T(8,128)(2,1)}, u32[]{:S(2)}) copy-start(bf16[64,64,176]{2,1,0:T(8,128)(2,1)} %param.11) | copy-start | bytes 4325380
  20.8 1.5 %copy-start.3 = (f32[1,1,64,128]{3,2,1,0:T(8,128)S(1)}, f32[1,1,64,128]{3,2,1,0:T(8,128)}, u32[]{:S(2)}) copy-start(f32[1,1,64,128]{3,2,1,0:T(8,128)} %param.6) | copy-start | bytes 98308
  20.8 1.5 %copy-start.4 = (s32[1,1,3,128]{3,1,2,0:T(1,128)S(1)}, s32[1,1,3,128]{3,1,2,0:T(1,128)}, u32[]{:S(2)}) copy-start(s32[1,1,3,128]{3,1,2,0:T(1,128)} %param.8) | copy-start | bytes 4612
  20.8 1.5 %copy-start.5 = (s32[1,1,128]{2,1,0:T(1,128)S(1)}, s32[1,1,128]{2,1,0:T(1,128)}, u32[]{:S(2)}) copy-start(s32[1,1,128]{2,1,0:T(1,128)} %param.9) | copy-start | bytes 1540
  22.3 10.7 %copy-start.2 = (bf16[64,64,160]{2,1,0:T(8,128)(2,1)S(1)}, bf16[64,64,160]{2,1,0:T(8,128)(2,1)}, u32[]{:S(2)}) copy-start(bf16[64,64,160]{2,1,0:T(8,128)(2,1)} %param.10) | copy-start | bytes 3932164
  23.3 11.1 %collective-permute-start.7 = (f32[72,128]{1,0:T(8,128)S(1)}, f32[72,128]{1,0:T(8,128)S(1)}, u32[]{:S(2)}, u32[]{:S(2)}) collective-permute-start(f32[72,128]{1,0:T(8,128)S(1)} %shard_map.65.field), channel_id=1, source_target_pairs={{0,1},{1,2},{2,3},{3,4},{4,5},{5,6},{6,7},{8,9},{9,10},{10,11},{11... | collective-permute-start | bytes 110600 | tf_op jit(solution)/shard_map/ppermute | solution.py:349
  25.3 9.1 %collective-permute-start.6 = (f32[72,128]{1,0:T(8,128)S(1)}, f32[72,128]{1,0:T(8,128)S(1)}, u32[]{:S(2)}, u32[]{:S(2)}) collective-permute-start(f32[72,128]{1,0:T(8,128)S(1)} %shard_map.65.field), channel_id=1, source_target_pairs={{1,0},{2,1},{3,2},{4,3},{5,4},{6,5},{7,6},{9,8},{10,9},{11,10},{12... | collective-permute-start | bytes 110600 | tf_op jit(solution)/shard_map/ppermute | solution.py:349
  29.2 5.2 %collective-permute-start.5 = (f32[72,128]{1,0:T(8,128)S(1)}, f32[72,128]{1,0:T(8,128)S(1)}, u32[]{:S(2)}, u32[]{:S(2)}) collective-permute-start(f32[72,128]{1,0:T(8,128)S(1)} %shard_map.65.field), channel_id=1, source_target_pairs={{8,16},{16,8},{24,32},{32,24},{40,48},{48,40},{56,64},{64,56},{72,... | collective-permute-start | bytes 110600 | tf_op jit(solution)/shard_map/ppermute | solution.py:356
  29.9 4.6 %collective-permute-start.4 = (f32[72,128]{1,0:T(8,128)S(1)}, f32[72,128]{1,0:T(8,128)S(1)}, u32[]{:S(2)}, u32[]{:S(2)}) collective-permute-start(f32[72,128]{1,0:T(8,128)S(1)} %shard_map.65.field), channel_id=1, source_target_pairs={{0,8},{8,0},{16,24},{24,16},{32,40},{40,32},{48,56},{56,48},{64,72... | collective-permute-start | bytes 110600 | tf_op jit(solution)/shard_map/ppermute | solution.py:356

commit v4 on v3

--- a/solution.py
+++ b/solution.py
@@ -92,25 +92,51 @@
     lax.fori_loop(0, GROUPS, body, 0)
 
 
-def first_body(source, inner, outer, above, below, weights, links, owners, second):
-    fields = [ref[...] for ref in (source, inner, outer, above, below)]
-    picked = pick(fields, links)
+def first_body(
+    source, inner, outer, above, below, couplings, links, owners, blocks,
+    second, weights, packed, field, link, owner, high, held, sems,
+):
+    small = [
+        pltpu.make_async_copy(there, here, sems.at[2, number])
+        for number, (there, here) in enumerate(((source, field), (links, link), (owners, owner)))
+    ]
+
+    def tile_copies(tile):
+        rows = pl.ds(tile * SUB, SUB)
+        return (
+            pltpu.make_async_copy(couplings.at[:, rows], weights.at[:, rows], sems.at[0, tile]),
+            pltpu.make_async_copy(blocks.at[:, tile], held.at[tile], sems.at[1, tile]),
+        )
+
+    for copy in small:
+        copy.start()
+    for tile in range(GROUPS):
+        for copy in tile_copies(tile):
+            copy.start()
+    for copy in small:
+        copy.wait()
+    fields = [ref[...] for ref in (field, inner, outer, above, below)]
+    picked = pick(fields, link)
 
     def step(tile, rows):
-        mine = source[rows, :]
+        for copy in tile_copies(tile):
+            copy.wait()
+        mine = field[rows, :]
         applied = 0.5 * (mine + coupled(weights, picked, tile))
         second[rows, :] = 0.5 * mine + 0.5 * (mine - applied)
+        pack_rows(tile, lambda part, rows, lanes: held[tile, part, rows, lanes], high, packed)
 
     tiles(step)
-    second[BS:, :] = jnp.broadcast_to(owners[...].astype(F32), (SUB, NB))
-
-
-def second_body(field, inner, outer, above, below, weights, links, source, owners, sent, left):
+    second[BS:, :] = jnp.broadcast_to(owner[...].astype(F32), (SUB, NB))
+
+
+def second_body(field, inner, outer, above, below, weights, links, source, owners, blocks, sent, packed, left, high):
     fields = [ref[0:BS, :] for ref in (field, inner, outer, above, below)]
     picked = pick(fields, links)
 
     def step(tile, rows):
         left[rows, :] = source[rows, :] - (field[rows, :] + coupled(weights, picked, tile))
+        pack_rows(tile, lambda part, rows, lanes: blocks[part, tile, rows, lanes], high, packed)
 
     tiles(step)
     member = ((iota((NB, NB), 0) & (NC - 1)) == owners[...]).astype(F32)
@@ -122,15 +148,15 @@
         preferred_element_type=F32,
     )
     lane_group = iota((SUB, NB), 1) // NC
-    packed = spread[0:SUB]
+    joined = spread[0:SUB]
     for group in range(1, GROUPS):
-        packed = jnp.where(lane_group == group, spread[group * SUB : (group + 1) * SUB], packed)
-    packed = packed * math.sqrt(NC / NB)
+        joined = jnp.where(lane_group == group, spread[group * SUB : (group + 1) * SUB], joined)
+    joined = joined * math.sqrt(NC / NB)
     for copy in range(sent.shape[0]):
-        sent[copy] = packed
-
-
-def last_body(field, inner, outer, above, below, errors, weights, links, source, out, third):
+        sent[copy] = joined
+
+
+def last_body(field, inner, outer, above, below, errors, weights, links, source, out, third, stage, sems):
     fields = []
     for number, ref in enumerate((field, inner, outer, above, below)):
         error = errors[number]
@@ -143,9 +169,13 @@
     def step(tile, rows):
         mine = third[rows, :]
         applied = mine + coupled(weights, picked, tile)
-        out[rows, :] = mine + 0.5 * (source[rows, :] - applied)
+        stage[rows, :] = mine + 0.5 * (source[rows, :] - applied)
+        pltpu.make_async_copy(stage.at[rows], out.at[rows], sems.at[tile]).start()
 
     tiles(step)
+    for tile in range(GROUPS):
+        rows = pl.ds(tile * SUB, SUB)
+        pltpu.make_async_copy(stage.at[rows], out.at[rows], sems.at[tile]).wait()
 
 
 def skew(values, count):
@@ -164,36 +194,19 @@
     return [values[v] for v in wanted]
 
 
-def pack_body(source, packed, high):
+def pack_rows(inner, load, high, packed):
     count = packed.shape[0]
-    rest = (count - GROUPS) * NC
-
-    def body(inner, carry):
-        for part in range(GROUPS):
-            high[part, :, 0:rest] = source[part, inner, :, NB:].astype(F32)
-        for column in range(GROUPS):
-            rows = slice(column * SUB, (column + 1) * SUB)
-            place = column * SUB + inner
-            values = [source[part, inner, rows, 0:NB].astype(F32) for part in range(GROUPS)]
-            for level, value in enumerate(skew(values, GROUPS)):
-                packed[level, place] = value
-            values = [high[part, rows, :] for part in range(GROUPS)]
-            for level, value in enumerate(skew(values, count - GROUPS)):
-                packed[GROUPS + level, place] = value
-        return carry
-
-    lax.fori_loop(0, SUB, body, 0)
-
-
-def pack(blocks):
-    width = blocks.shape[2]
-    return call(
-        pack_body,
-        jax.ShapeDtypeStruct((width // NC, BS, SUB, NB), F32),
-        (blocks.reshape(GROUPS, SUB, BS, width),),
-        12 * MIB,
-        [pltpu.VMEM((GROUPS, BS, NB), F32)],
-    )
+    for part in range(GROUPS):
+        high[part, :, 0 : (count - GROUPS) * NC] = load(part, slice(None), slice(NB, None)).astype(F32)
+    for column in range(GROUPS):
+        rows = slice(column * SUB, (column + 1) * SUB)
+        place = column * SUB + inner
+        values = [load(part, rows, slice(0, NB)).astype(F32) for part in range(GROUPS)]
+        for level, value in enumerate(skew(values, GROUPS)):
+            packed[level, place] = value
+        values = [high[part, rows, :] for part in range(GROUPS)]
+        for level, value in enumerate(skew(values, count - GROUPS)):
+            packed[GROUPS + level, place] = value
 
 
 def block_product(packed, level, vectors, turned):
@@ -382,25 +395,44 @@
     def vectors(*counts):
         return jax.ShapeDtypeStruct((*counts, SUB, NB), F32)
 
-    smooth = pack(coarse_smooth)
-    around = halo(source)
-    smooth, source = lax.optimization_barrier((smooth, source))
-    second = call(
+    weights_type = jax.ShapeDtypeStruct(weights.shape, weights.dtype)
+    split = lambda blocks: blocks.reshape(GROUPS, SUB, BS, blocks.shape[2])
+    high = pltpu.VMEM((GROUPS, BS, NB), F32)
+    vmem, hbm = (pl.BlockSpec(memory_space=space) for space in (pltpu.VMEM, pltpu.HBM))
+    held = functools.partial(pltpu.with_memory_space_constraint, memory_space=pltpu.HBM)
+    second, weights, smooth = pl.pallas_call(
         first_body,
-        jax.ShapeDtypeStruct((BS + SUB, NB), F32),
-        (source, *around, weights, links, owners),
-        12 * MIB,
+        out_shape=(
+            jax.ShapeDtypeStruct((BS + SUB, NB), F32),
+            weights_type,
+            vectors(LEVELS + 1, BS),
+        ),
+        in_specs=[hbm] + [vmem] * 4 + [hbm] * 4,
+        out_specs=(vmem, vmem, vmem),
+        scratch_shapes=[
+            pltpu.VMEM((BS, NB), F32),
+            pltpu.VMEM(links.shape, links.dtype),
+            pltpu.VMEM(owners.shape, owners.dtype),
+            high,
+            pltpu.VMEM((SUB, GROUPS, BS, coarse_smooth.shape[2]), coarse_smooth.dtype),
+            pltpu.SemaphoreType.DMA((3, GROUPS)),
+        ],
+        compiler_params=pltpu.CompilerParams(vmem_limit_bytes=24 * MIB),
+    )(
+        held(source),
+        *halo(source),
+        held(weights),
+        held(links),
+        held(owners),
+        held(split(coarse_smooth)),
     )
     around = halo(second)
-    second, coarse_ops = lax.optimization_barrier((second, coarse_ops))
-    ops = pack(coarse_ops)
-    ops, source = lax.optimization_barrier((ops, source))
-    sent = call(
+    sent, ops = call(
         second_body,
-        vectors(near),
-        (second, *around, weights, links, source, owners),
-        12 * MIB,
-        [pltpu.VMEM((BS, NB), F32)],
+        (vectors(near), vectors(LEVELS, BS)),
+        (second, *around, weights, links, source, owners, split(coarse_ops)),
+        24 * MIB,
+        [pltpu.VMEM((BS, NB), F32), high],
     )
     near_groups = [[a * near + b for b in range(near)] for a in range(far)]
     far_groups = [[a * near + b for a in range(far)] for b in range(near)]
@@ -423,13 +455,18 @@
         16 * MIB,
         [pltpu.VMEM((2 * height, 2, SUB, NB), F32)],
     )
-    out = call(
+    out = pl.pallas_call(
         last_body,
-        field_shape,
-        (second, *around, errors, weights, links, source),
-        12 * MIB,
-        [pltpu.VMEM((BS, NB), F32)],
-    )
+        out_shape=field_shape,
+        in_specs=[vmem] * 9,
+        out_specs=hbm,
+        scratch_shapes=[
+            pltpu.VMEM((BS, NB), F32),
+            pltpu.VMEM((BS, NB), F32),
+            pltpu.SemaphoreType.DMA((GROUPS,)),
+        ],
+        compiler_params=pltpu.CompilerParams(vmem_limit_bytes=12 * MIB),
+    )(second, *around, errors, weights, links, source)
     return out[None, None]
 
 

time: 95.6 us -> 97.2 us (1.017)
  waiting for transfers between devices: 0.02 us -> 2.18 us
  local copies, waits for them, and re-layouts: 1.61 us -> 0.02 us
  blocking collectives: 50.2 us -> 51.3 us
    pallas_call x0 -> x2, Pallas kernels: none -> 4.98 us  [the longest x1 3.2 us: shards(): pl.pallas_call(first_body, out_shape=(jax.ShapeDtypeStruct((BS + SUB, NB)...]
    pallas_call x8 -> x4, Pallas kernels: 14.2 us -> 9.78 us  [call(): pl.pallas_call(body, out_shape=out_shape, in_specs=whole(len(inputs)), ou...]
    ppermute x4, waiting for transfers between devices: 0.01 us -> 2.17 us  [swapped(): return lax.ppermute(value, 'plan', pairs)]
    unnamed x12 -> x8, local copies, waits for them, and re-layouts: 1.61 us -> 0.02 us
    all_to_all x3, blocking collectives: 50.2 us -> 51.3 us  [exchange(): lax.all_to_all(value, axis, 0, 0, axis_index_groups=groups, tiled=True)]
  transfers between devices with their start and end apart: 8 -> 8, of which waited for: 0 -> 2; matrix products, arithmetic and copies ran while one was open for 0% -> 0% of each run, Pallas kernels for 3% -> 0%
where the time goes in v4:
time: 97.2 us; the launch traced here: 96.8 us
  blocking collectives  51.3 us (53%)
  starting transfers between devices  28.4 us (29%)
  Pallas kernels  14.8 us (15%)
  waiting for transfers between devices  2.18 us (2%)
    all_to_all x3, blocking collectives, exchange(): lax.all_to_all(value, axis, 0, 0, axis_index_groups=groups, tiled=True)  51.3 us
    ppermute x4, starting transfers between devices, shifted(): return lax.ppermute(value, 'height', pairs)  22.3 us
    pallas_call x4, Pallas kernels, call(): pl.pallas_call(body, out_shape=out_shape, in_specs=whole(len(inputs)), ou...  9.78 us
    ppermute x4, starting transfers between devices, swapped(): return lax.ppermute(value, 'plan', pairs)  6.01 us
    pallas_call x1, Pallas kernels, shards(): pl.pallas_call(first_body, out_shape=(jax.ShapeDtypeStruct((BS + SUB, NB)...  3.2 us
    ppermute x4, waiting for transfers between devices, swapped(): return lax.ppermute(value, 'plan', pairs)  2.17 us
  transfers between devices with their start and end apart: 8, of which 2 were waited for; matrix products, arithmetic and copies ran while one was open for 0% of the time, Pallas kernels for 0%

profile of v4, /device:TPU:2, one launch (start us, length us, event | category | flops | bytes accessed | tf_op | source)
XLA Modules:
  0.0 96.8 jit_solution(10991806985536687909)
XLA Ops:
  0.0 0.0 copy-start.1
  0.0 0.0 copy-start.3
  0.0 0.0 copy-start.2
  0.0 0.0 copy-start
  0.0 3.5 %collective-permute-start.3 = (f32[64,128]{1,0:T(8,128)}, f32[64,128]{1,0:T(8,128)S(1)}, u32[]{:S(2)}, u32[]{:S(2)}) collective-permute-start(f32[64,128]{1,0:T(8,128)} %bitcast.8), channel_id=1, source_target_pairs={{0,1},{1,2},{2,3},{3,4},{4,5},{5,6},{6,7},{8,9},{9,10},{10,11},{11... | collective-permute-start | bytes 98312 | tf_op jit(solution)/shard_map/ppermute | solution.py:362
  3.6 13.0 %collective-permute-start.2 = (f32[64,128]{1,0:T(8,128)}, f32[64,128]{1,0:T(8,128)S(1)}, u32[]{:S(2)}, u32[]{:S(2)}) collective-permute-start(f32[64,128]{1,0:T(8,128)} %bitcast.9), channel_id=1, source_target_pairs={{1,0},{2,1},{3,2},{4,3},{5,4},{6,5},{7,6},{9,8},{10,9},{11,10},{12... | collective-permute-start | bytes 98312 | tf_op jit(solution)/shard_map/ppermute | solution.py:362
  16.5 0.7 collective-permute-start.1
  17.2 1.9 %collective-permute-start = (f32[64,128]{1,0:T(8,128)}, f32[64,128]{1,0:T(8,128)S(1)}, u32[]{:S(2)}, u32[]{:S(2)}) collective-permute-start(f32[64,128]{1,0:T(8,128)} %bitcast.11), channel_id=1, source_target_pairs={{0,8},{8,0},{16,24},{24,16},{32,40},{40,32},{48,56},{56,48},{64,72... | collective-permute-start | bytes 98312 | tf_op jit(solution)/shard_map/ppermute | solution.py:369
  19.1 0.0 collective-permute-done.3.below
  19.1 0.0 collective-permute-done.2.above
  19.2 0.0 collective-permute-done.1.outer
  19.2 1.4 %collective-permute-done.inner = f32[64,128]{1,0:T(8,128)S(1)} collective-permute-done((f32[64,128]{1,0:T(8,128)}, f32[64,128]{1,0:T(8,128)S(1)}, u32[]{:S(2)}, u32[]{:S(2)}) %collective-permute-start) | collective-permute-done | bytes 32800 | tf_op jit(solution)/shard_map/ppermute | solution.py:369
  20.5 3.2 %shard_map.64 = (f32[72,128]{1,0:T(8,128)S(1)}, bf16[3,64,64,128]{3,2,1,0:T(8,128)(2,1)S(1)}, f32[11,64,8,128]{3,2,1,0:T(8,128)S(1)}) custom-call(f32[64,128]{1,0:T(8,128)} %bitcast.12, f32[64,128]{1,0:T(8,128)S(1)} %collective-permute-done.inner, f32[64,128]{1,0:T(8,128)S(1)} %collective-permute-done.1.outer, f32[64,128]{1,0:T(8,128)S(1)} %collective-permute-done.2.above, ...), custom_call_target="tpu_custom_call" | custom-call | tf_op jit(solution)/shard_map/pallas_call | solution.py:403
  23.7 1.9 %collective-permute-start.7 = (f32[72,128]{1,0:T(8,128)S(1)}, f32[72,128]{1,0:T(8,128)S(1)}, u32[]{:S(2)}, u32[]{:S(2)}) collective-permute-start(f32[72,128]{1,0:T(8,128)S(1)} %get-tuple-element.14.field), channel_id=1, source_target_pairs={{0,1},{1,2},{2,3},{3,4},{4,5},{5,6},{6,7},{8,9},{9,10},{10,11},{11... | collective-permute-start | bytes 110600 | tf_op jit(solution)/shard_map/ppermute | solution.py:362
  25.7 3.9 %collective-permute-start.6 = (f32[72,128]{1,0:T(8,128)S(1)}, f32[72,128]{1,0:T(8,128)S(1)}, u32[]{:S(2)}, u32[]{:S(2)}) collective-permute-start(f32[72,128]{1,0:T(8,128)S(1)} %get-tuple-element.14.field), channel_id=1, source_target_pairs={{1,0},{2,1},{3,2},{4,3},{5,4},{6,5},{7,6},{9,8},{10,9},{11,10},{12... | collective-permute-start | bytes 110600 | tf_op jit(solution)/shard_map/ppermute | solution.py:362
  29.6 0.7 collective-permute-start.5
  30.3 2.8 %collective-permute-start.4 = (f32[72,128]{1,0:T(8,128)S(1)}, f32[72,128]{1,0:T(8,128)S(1)}, u32[]{:S(2)}, u32[]{:S(2)}) collective-permute-start(f32[72,128]{1,0:T(8,128)S(1)} %get-tuple-element.14.field), channel_id=1, source_target_pairs={{0,8},{8,0},{16,24},{24,16},{32,40},{40,32},{48,56},{56,48},{64,72... | collective-permute-start | bytes 110600 | tf_op jit(solution)/shard_map/ppermute | solution.py:369
  33.0 0.0 collective-permute-done.7.below
  33.0 0.0 collective-permute-done.6.above
  33.1 0.0 collective-permute-done.5.outer
  33.1 0.8 collective-permute-done.4.inner
  33.9 0.0 copy-done.1
  33.9 0.0 copy-done.3
  33.9 0.0 copy-done.2
  33.9 0.0 copy-done
  33.9 2.1 %shard_map.65 = (f32[16,8,128]{2,1,0:T(8,128)S(1)}, f32[10,64,8,128]{3,2,1,0:T(8,128)S(1)}) custom-call(f32[72,128]{1,0:T(8,128)S(1)} %get-tuple-element.14.field, f32[72,128]{1,0:T(8,128)S(1)} %collective-permute-done.4.inner, f32[72,128]{1,0:T(8,128)S(1)} %collective-permute-done.5.outer, f32[72,128]{1,0:T(8,128)S(1)} %collective-permute-done.6.above, ...), custom_call_target="tpu_custom_call" | custom-call | tf_op jit(solution)/shard_map/pallas_call | solution.py:29
  36.0 11.0 %all_to_all.15.received = f32[16,8,128]{2,1,0:T(8,128)S(1)} all-to-all(f32[16,8,128]{2,1,0:T(8,128)S(1)} %get-tuple-element.18), channel_id=1, replica_groups={{0,8,16,24,32,40,48,56,64,72,80,88,96,104,112,120},{128,136,144,152,160..., dimensions={0} | all-to-all | bytes 131072 | tf_op jit(solution)/shard_map/all_to_all | solution.py:379
  47.0 2.2 %shard_map.66 = (f32[8,2,8,128]{3,2,1,0:T(8,128)S(1)}, f32[2,8,128]{2,1,0:T(8,128)S(1)}) custom-call(f32[10,64,8,128]{3,2,1,0:T(8,128)S(1)} %get-tuple-element.16.ops, f32[11,64,8,128]{3,2,1,0:T(8,128)S(1)} %get-tuple-element.17.smooth, f32[16,8,128]{2,1,0:T(8,128)S(1)} %all_to_all.15.received), custom_call_target="tpu_custom_call" | custom-call | tf_op jit(solution)/shard_map/pallas_call | solution.py:29
  49.2 23.5 %all_to_all.16.received = f32[8,2,8,128]{3,2,1,0:T(8,128)S(1)} all-to-all(f32[8,2,8,128]{3,2,1,0:T(8,128)S(1)} %get-tuple-element.19), channel_id=1, replica_groups={{0,128,256,384,512,640,768,896},{8,136,264,392,520,648,776,904},{16,144..., dimensions={0} | all-to-all | bytes 131072 | tf_op jit(solution)/shard_map/all_to_all | solution.py:379
  72.7 1.6 %shard_map.67 = (f32[8,3,8,128]{3,2,1,0:T(8,128)S(1)}, f32[2,8,128]{2,1,0:T(8,128)S(1)}) custom-call(f32[10,64,8,128]{3,2,1,0:T(8,128)S(1)} %get-tuple-element.16.ops, f32[11,64,8,128]{3,2,1,0:T(8,128)S(1)} %get-tuple-element.17.smooth, f32[8,2,8,128]{3,2,1,0:T(8,128)S(1)} %all_to_all.16.received, f32[2,8,128]{2,1,0:T(8,128)S(1)} %get-tuple-element.20.near), custom_call_target="tpu_custom_call" | custom-call | tf_op jit(solution)/shard_map/pallas_call | solution.py:29
  74.3 16.8 %all_to_all.17.received = f32[8,3,8,128]{3,2,1,0:T(8,128)S(1)} all-to-all(f32[8,3,8,128]{3,2,1,0:T(8,128)S(1)} %get-tuple-element.21), channel_id=1, replica_groups=mesh['plan'=128,'height'=8] {'height'}, dimensions={0} | all-to-all | bytes 196608 | tf_op jit(solution)/shard_map/all_to_all | solution.py:379
  91.1 3.9 %shard_map.68.errors = f32[5,8,128]{2,1,0:T(8,128)S(1)} custom-call(f32[10,64,8,128]{3,2,1,0:T(8,128)S(1)} %get-tuple-element.16.ops, f32[11,64,8,128]{3,2,1,0:T(8,128)S(1)} %get-tuple-element.17.smooth, f32[8,3,8,128]{3,2,1,0:T(8,128)S(1)} %all_to_all.17.received, f32[2,8,128]{2,1,0:T(8,128)S(1)} %get-tuple-element.20.near, ...), custom_call_target="tpu_custom_call" | custom-call | tf_op jit(solution)/shard_map/pallas_call | solution.py:29
  95.0 1.8 %shard_map.69 = f32[64,128]{1,0:T(8,128)} custom-call(f32[72,128]{1,0:T(8,128)S(1)} %get-tuple-element.14.field, f32[72,128]{1,0:T(8,128)S(1)} %collective-permute-done.4.inner, f32[72,128]{1,0:T(8,128)S(1)} %collective-permute-done.5.outer, f32[72,128]{1,0:T(8,128)S(1)} %collective-permute-done.6.above, f32[72,128]{1,0:T(8,128)S(1)} %collective-permute-done.7.below, ...), custom_call_target="tpu_custom_call" | custom-call | tf_op jit(solution)/shard_map/pallas_call | solution.py:458
Async XLA Ops:
  0.0 33.9 %copy-start.1 = (f32[1,1,64,128]{3,2,1,0:T(8,128)S(1)}, f32[1,1,64,128]{3,2,1,0:T(8,128)}, u32[]{:S(2)}) copy-start(f32[1,1,64,128]{3,2,1,0:T(8,128)} %param.6) | copy-start | bytes 98308
  0.0 33.9 %copy-start.3 = (s32[1,1,128]{2,1,0:T(1,128)S(1)}, s32[1,1,128]{2,1,0:T(1,128)}, u32[]{:S(2)}) copy-start(s32[1,1,128]{2,1,0:T(1,128)} %param.9) | copy-start | bytes 1540
  0.0 33.9 %copy-start.2 = (s32[1,1,3,128]{3,1,2,0:T(1,128)S(1)}, s32[1,1,3,128]{3,1,2,0:T(1,128)}, u32[]{:S(2)}) copy-start(s32[1,1,3,128]{3,1,2,0:T(1,128)} %param.8) | copy-start | bytes 4612
  0.0 33.9 %copy-start = (bf16[64,64,160]{2,1,0:T(8,128)(2,1)S(1)}, bf16[64,64,160]{2,1,0:T(8,128)(2,1)}, u32[]{:S(2)}) copy-start(bf16[64,64,160]{2,1,0:T(8,128)(2,1)} %param.10) | copy-start | bytes 3932164
  0.0 19.1 %collective-permute-start.3 = (f32[64,128]{1,0:T(8,128)}, f32[64,128]{1,0:T(8,128)S(1)}, u32[]{:S(2)}, u32[]{:S(2)}) collective-permute-start(f32[64,128]{1,0:T(8,128)} %bitcast.8), channel_id=1, source_target_pairs={{0,1},{1,2},{2,3},{3,4},{4,5},{5,6},{6,7},{8,9},{9,10},{10,11},{11... | collective-permute-start | bytes 98312 | tf_op jit(solution)/shard_map/ppermute | solution.py:362
  3.6 15.6 %collective-permute-start.2 = (f32[64,128]{1,0:T(8,128)}, f32[64,128]{1,0:T(8,128)S(1)}, u32[]{:S(2)}, u32[]{:S(2)}) collective-permute-start(f32[64,128]{1,0:T(8,128)} %bitcast.9), channel_id=1, source_target_pairs={{1,0},{2,1},{3,2},{4,3},{5,4},{6,5},{7,6},{9,8},{10,9},{11,10},{12... | collective-permute-start | bytes 98312 | tf_op jit(solution)/shard_map/ppermute | solution.py:362
  16.5 2.6 %collective-permute-start.1 = (f32[64,128]{1,0:T(8,128)}, f32[64,128]{1,0:T(8,128)S(1)}, u32[]{:S(2)}, u32[]{:S(2)}) collective-permute-start(f32[64,128]{1,0:T(8,128)} %bitcast.10), channel_id=1, source_target_pairs={{8,16},{16,8},{24,32},{32,24},{40,48},{48,40},{56,64},{64,56},{72,... | collective-permute-start | bytes 98312 | tf_op jit(solution)/shard_map/ppermute | solution.py:369
  17.2 3.3 %collective-permute-start = (f32[64,128]{1,0:T(8,128)}, f32[64,128]{1,0:T(8,128)S(1)}, u32[]{:S(2)}, u32[]{:S(2)}) collective-permute-start(f32[64,128]{1,0:T(8,128)} %bitcast.11), channel_id=1, source_target_pairs={{0,8},{8,0},{16,24},{24,16},{32,40},{40,32},{48,56},{56,48},{64,72... | collective-permute-start | bytes 98312 | tf_op jit(solution)/shard_map/ppermute | solution.py:369
  23.7 9.3 %collective-permute-start.7 = (f32[72,128]{1,0:T(8,128)S(1)}, f32[72,128]{1,0:T(8,128)S(1)}, u32[]{:S(2)}, u32[]{:S(2)}) collective-permute-start(f32[72,128]{1,0:T(8,128)S(1)} %get-tuple-element.14.field), channel_id=1, source_target_pairs={{0,1},{1,2},{2,3},{3,4},{4,5},{5,6},{6,7},{8,9},{9,10},{10,11},{11... | collective-permute-start | bytes 110600 | tf_op jit(solution)/shard_map/ppermute | solution.py:362
  25.7 7.4 %collective-permute-start.6 = (f32[72,128]{1,0:T(8,128)S(1)}, f32[72,128]{1,0:T(8,128)S(1)}, u32[]{:S(2)}, u32[]{:S(2)}) collective-permute-start(f32[72,128]{1,0:T(8,128)S(1)} %get-tuple-element.14.field), channel_id=1, source_target_pairs={{1,0},{2,1},{3,2},{4,3},{5,4},{6,5},{7,6},{9,8},{10,9},{11,10},{12... | collective-permute-start | bytes 110600 | tf_op jit(solution)/shard_map/ppermute | solution.py:362
  29.6 3.5 %collective-permute-start.5 = (f32[72,128]{1,0:T(8,128)S(1)}, f32[72,128]{1,0:T(8,128)S(1)}, u32[]{:S(2)}, u32[]{:S(2)}) collective-permute-start(f32[72,128]{1,0:T(8,128)S(1)} %get-tuple-element.14.field), channel_id=1, source_target_pairs={{8,16},{16,8},{24,32},{32,24},{40,48},{48,40},{56,64},{64,56},{72,... | collective-permute-start | bytes 110600 | tf_op jit(solution)/shard_map/ppermute | solution.py:369
  30.3 3.6 %collective-permute-start.4 = (f32[72,128]{1,0:T(8,128)S(1)}, f32[72,128]{1,0:T(8,128)S(1)}, u32[]{:S(2)}, u32[]{:S(2)}) collective-permute-start(f32[72,128]{1,0:T(8,128)S(1)} %get-tuple-element.14.field), channel_id=1, source_target_pairs={{0,8},{8,0},{16,24},{24,16},{32,40},{40,32},{48,56},{56,48},{64,72... | collective-permute-start | bytes 110600 | tf_op jit(solution)/shard_map/ppermute | solution.py:369

commit v5 on v3

--- a/solution.py
+++ b/solution.py
@@ -164,36 +164,62 @@
     return [values[v] for v in wanted]
 
 
+def pack_rows(inner, load, high, packed):
+    count = packed.shape[0]
+    for part in range(GROUPS):
+        high[part, :, 0 : (count - GROUPS) * NC] = load(part, slice(None), slice(NB, None)).astype(F32)
+    for column in range(GROUPS):
+        rows = slice(column * SUB, (column + 1) * SUB)
+        place = column * SUB + inner
+        values = [load(part, rows, slice(0, NB)).astype(F32) for part in range(GROUPS)]
+        for level, value in enumerate(skew(values, GROUPS)):
+            packed[level, place] = value
+        values = [high[part, rows, :] for part in range(GROUPS)]
+        for level, value in enumerate(skew(values, count - GROUPS)):
+            packed[GROUPS + level, place] = value
+
+
 def pack_body(source, packed, high):
-    count = packed.shape[0]
-    rest = (count - GROUPS) * NC
-
     def body(inner, carry):
-        for part in range(GROUPS):
-            high[part, :, 0:rest] = source[part, inner, :, NB:].astype(F32)
-        for column in range(GROUPS):
-            rows = slice(column * SUB, (column + 1) * SUB)
-            place = column * SUB + inner
-            values = [source[part, inner, rows, 0:NB].astype(F32) for part in range(GROUPS)]
-            for level, value in enumerate(skew(values, GROUPS)):
-                packed[level, place] = value
-            values = [high[part, rows, :] for part in range(GROUPS)]
-            for level, value in enumerate(skew(values, count - GROUPS)):
-                packed[GROUPS + level, place] = value
+        pack_rows(inner, lambda part, rows, lanes: source[part, inner, rows, lanes], high, packed)
         return carry
 
     lax.fori_loop(0, SUB, body, 0)
 
 
-def pack(blocks):
+def stream_body(source, packed, high, held, sems):
+    def copy(inner):
+        return pltpu.make_async_copy(source.at[:, inner], held.at[inner], sems.at[inner])
+
+    for inner in range(SUB):
+        copy(inner).start()
+
+    def body(inner, carry):
+        copy(inner).wait()
+        pack_rows(inner, lambda part, rows, lanes: held[inner, part, rows, lanes], high, packed)
+        return carry
+
+    lax.fori_loop(0, SUB, body, 0)
+
+
+def pack(blocks, streamed):
     width = blocks.shape[2]
-    return call(
-        pack_body,
-        jax.ShapeDtypeStruct((width // NC, BS, SUB, NB), F32),
-        (blocks.reshape(GROUPS, SUB, BS, width),),
-        12 * MIB,
-        [pltpu.VMEM((GROUPS, BS, NB), F32)],
-    )
+    blocks = blocks.reshape(GROUPS, SUB, BS, width)
+    scratch = [pltpu.VMEM((GROUPS, BS, NB), F32)]
+    if streamed:
+        blocks = pltpu.with_memory_space_constraint(blocks, pltpu.HBM)
+        scratch += [
+            pltpu.VMEM((SUB, GROUPS, BS, width), blocks.dtype),
+            pltpu.SemaphoreType.DMA((SUB,)),
+        ]
+    return pl.pallas_call(
+        stream_body if streamed else pack_body,
+        out_shape=jax.ShapeDtypeStruct((width // NC, BS, SUB, NB), F32),
+        in_specs=[pl.BlockSpec(memory_space=pltpu.HBM if streamed else pltpu.VMEM)],
+        out_specs=pl.BlockSpec(memory_space=pltpu.VMEM),
+        scratch_shapes=scratch,
+        compiler_params=pltpu.CompilerParams(vmem_limit_bytes=12 * MIB),
+    )(blocks)
 
 
 def block_product(packed, level, vectors, turned):
@@ -382,7 +408,7 @@
     def vectors(*counts):
         return jax.ShapeDtypeStruct((*counts, SUB, NB), F32)
 
-    smooth = pack(coarse_smooth)
+    smooth = pack(coarse_smooth, True)
     around = halo(source)
     smooth, source = lax.optimization_barrier((smooth, source))
     second = call(
@@ -393,7 +419,7 @@
     )
     around = halo(second)
     second, coarse_ops = lax.optimization_barrier((second, coarse_ops))
-    ops = pack(coarse_ops)
+    ops = pack(coarse_ops, False)
     ops, source = lax.optimization_barrier((ops, source))
     sent = call(
         second_body,

time: 95.6 us -> 95 us (level)
  local copies, waits for them, and re-layouts: 1.61 us -> 0.02 us
  Pallas kernels: 14.2 us -> 15.3 us
    pallas_call x0 -> x2, Pallas kernels: none -> 3.81 us  [pack(): pl.pallas_call(stream_body if streamed else pack_body, out_shape=jax.Shap...]
    pallas_call x8 -> x6, Pallas kernels: 14.2 us -> 11.4 us  [call(): pl.pallas_call(body, out_shape=out_shape, in_specs=whole(len(inputs)), ou...]
    unnamed x12 -> x10, local copies, waits for them, and re-layouts: 1.61 us -> 0.02 us
  transfers between devices with their start and end apart: 8 -> 8, of which waited for: 0 -> 0; matrix products, arithmetic and copies ran while one was open for 0% -> 0% of each run, Pallas kernels for 3% -> 4%
where the time goes in v5:
time: 95 us; the launch traced here: 94.6 us
  blocking collectives  50.2 us (53%)
  starting transfers between devices  28.8 us (30%)
  Pallas kernels  15.3 us (16%)
    all_to_all x3, blocking collectives, exchange(): lax.all_to_all(value, axis, 0, 0, axis_index_groups=groups, tiled=True)  50.2 us
    ppermute x4, starting transfers between devices, shifted(): return lax.ppermute(value, 'height', pairs)  22.5 us
    pallas_call x6, Pallas kernels, call(): pl.pallas_call(body, out_shape=out_shape, in_specs=whole(len(inputs)), ou...  11.4 us
    ppermute x4, starting transfers between devices, swapped(): return lax.ppermute(value, 'plan', pairs)  6.35 us
    pallas_call x2, Pallas kernels, pack(): pl.pallas_call(stream_body if streamed else pack_body, out_shape=jax.Shap...  3.81 us
  transfers between devices with their start and end apart: 8, of which 0 were waited for; matrix products, arithmetic and copies ran while one was open for 0% of the time, Pallas kernels for 4%

profile of v5, /device:TPU:2, one launch (start us, length us, event | category | flops | bytes accessed | tf_op | source)
XLA Modules:
  0.0 94.6 jit_solution(2533248419052639845)
XLA Ops:
  0.0 0.0 copy-start.2
  0.0 0.0 copy-start.4
  0.0 0.0 copy-start.3
  0.0 0.0 copy-start
  0.0 3.7 %collective-permute-start.3 = (f32[64,128]{1,0:T(8,128)}, f32[64,128]{1,0:T(8,128)S(1)}, u32[]{:S(2)}, u32[]{:S(2)}) collective-permute-start(f32[64,128]{1,0:T(8,128)} %bitcast.11), channel_id=1, source_target_pairs={{0,1},{1,2},{2,3},{3,4},{4,5},{5,6},{6,7},{8,9},{9,10},{10,11},{11... | collective-permute-start | bytes 98312 | tf_op jit(solution)/shard_map/ppermute | solution.py:375
  3.7 13.0 %collective-permute-start.2 = (f32[64,128]{1,0:T(8,128)}, f32[64,128]{1,0:T(8,128)S(1)}, u32[]{:S(2)}, u32[]{:S(2)}) collective-permute-start(f32[64,128]{1,0:T(8,128)} %bitcast.12), channel_id=1, source_target_pairs={{1,0},{2,1},{3,2},{4,3},{5,4},{6,5},{7,6},{9,8},{10,9},{11,10},{12... | collective-permute-start | bytes 98312 | tf_op jit(solution)/shard_map/ppermute | solution.py:375
  16.7 0.7 collective-permute-start.1
  17.3 1.9 %collective-permute-start = (f32[64,128]{1,0:T(8,128)}, f32[64,128]{1,0:T(8,128)S(1)}, u32[]{:S(2)}, u32[]{:S(2)}) collective-permute-start(f32[64,128]{1,0:T(8,128)} %bitcast.14), channel_id=1, source_target_pairs={{0,8},{8,0},{16,24},{24,16},{32,40},{40,32},{48,56},{56,48},{64,72... | collective-permute-start | bytes 98312 | tf_op jit(solution)/shard_map/ppermute | solution.py:382
  19.3 2.4 %shard_map.64.smooth = f32[11,64,8,128]{3,2,1,0:T(8,128)S(1)} custom-call(bf16[8,8,64,176]{3,2,1,0:T(8,128)(2,1)} %bitcast.23), custom_call_target="tpu_custom_call" | custom-call | tf_op jit(solution)/shard_map/pallas_call | solution.py:215
  21.7 0.0 copy-start.1
  21.7 0.0 collective-permute-done.3.below
  21.7 0.0 collective-permute-done.2.above
  21.7 0.0 collective-permute-done.1.outer
  21.7 0.0 collective-permute-done.inner
  21.7 0.0 copy-done.2
  21.8 0.0 copy-done.4
  21.8 0.0 copy-done.3
  21.8 0.0 copy-done
  21.8 1.0 %shard_map.65.field = f32[72,128]{1,0:T(8,128)S(1)} custom-call(f32[64,128]{1,0:T(8,128)S(1)} %bitcast.15, f32[64,128]{1,0:T(8,128)S(1)} %collective-permute-done.inner, f32[64,128]{1,0:T(8,128)S(1)} %collective-permute-done.1.outer, f32[64,128]{1,0:T(8,128)S(1)} %collective-permute-done.2.above, f32[64,128]{1,0:T(8,128)S(1)} %collective-permute-done.3.below, ...), custom_call_target="tpu_custom_call" | custom-call | tf_op jit(solution)/shard_map/pallas_call | solution.py:29
  22.8 1.9 %collective-permute-start.7 = (f32[72,128]{1,0:T(8,128)S(1)}, f32[72,128]{1,0:T(8,128)S(1)}, u32[]{:S(2)}, u32[]{:S(2)}) collective-permute-start(f32[72,128]{1,0:T(8,128)S(1)} %shard_map.65.field), channel_id=1, source_target_pairs={{0,1},{1,2},{2,3},{3,4},{4,5},{5,6},{6,7},{8,9},{9,10},{10,11},{11... | collective-permute-start | bytes 110600 | tf_op jit(solution)/shard_map/ppermute | solution.py:375
  24.7 3.9 %collective-permute-start.6 = (f32[72,128]{1,0:T(8,128)S(1)}, f32[72,128]{1,0:T(8,128)S(1)}, u32[]{:S(2)}, u32[]{:S(2)}) collective-permute-start(f32[72,128]{1,0:T(8,128)S(1)} %shard_map.65.field), channel_id=1, source_target_pairs={{1,0},{2,1},{3,2},{4,3},{5,4},{6,5},{7,6},{9,8},{10,9},{11,10},{12... | collective-permute-start | bytes 110600 | tf_op jit(solution)/shard_map/ppermute | solution.py:375
  28.6 0.7 collective-permute-start.5
  29.3 3.1 %collective-permute-start.4 = (f32[72,128]{1,0:T(8,128)S(1)}, f32[72,128]{1,0:T(8,128)S(1)}, u32[]{:S(2)}, u32[]{:S(2)}) collective-permute-start(f32[72,128]{1,0:T(8,128)S(1)} %shard_map.65.field), channel_id=1, source_target_pairs={{0,8},{8,0},{16,24},{24,16},{32,40},{40,32},{48,56},{56,48},{64,72... | collective-permute-start | bytes 110600 | tf_op jit(solution)/shard_map/ppermute | solution.py:382
  32.4 0.0 copy-done.1
  32.4 1.4 %shard_map.66.ops = f32[10,64,8,128]{3,2,1,0:T(8,128)S(1)} custom-call(bf16[8,8,64,160]{3,2,1,0:T(8,128)(2,1)S(1)} %bitcast.10), custom_call_target="tpu_custom_call" | custom-call | tf_op jit(solution)/shard_map/pallas_call | solution.py:215
  33.8 0.0 collective-permute-done.7.below
  33.8 0.0 collective-permute-done.6.above
  33.8 0.0 collective-permute-done.5.outer
  33.8 0.0 collective-permute-done.4.inner
  33.8 1.2 %shard_map.67 = f32[16,8,128]{2,1,0:T(8,128)S(1)} custom-call(f32[72,128]{1,0:T(8,128)S(1)} %shard_map.65.field, f32[72,128]{1,0:T(8,128)S(1)} %collective-permute-done.4.inner, f32[72,128]{1,0:T(8,128)S(1)} %collective-permute-done.5.outer, f32[72,128]{1,0:T(8,128)S(1)} %collective-permute-done.6.above, f32[72,128]{1,0:T(8,128)S(1)} %collective-permute-done.7.below, ...), custom_call_target="tpu_custom_call" | custom-call | tf_op jit(solution)/shard_map/pallas_call | solution.py:29
  35.0 10.8 %all_to_all.15.received = f32[16,8,128]{2,1,0:T(8,128)S(1)} all-to-all(f32[16,8,128]{2,1,0:T(8,128)S(1)} %shard_map.67), channel_id=1, replica_groups={{0,8,16,24,32,40,48,56,64,72,80,88,96,104,112,120},{128,136,144,152,160..., dimensions={0} | all-to-all | bytes 131072 | tf_op jit(solution)/shard_map/all_to_all | solution.py:392
  45.8 2.1 %shard_map.68 = (f32[8,2,8,128]{3,2,1,0:T(8,128)S(1)}, f32[2,8,128]{2,1,0:T(8,128)S(1)}) custom-call(f32[10,64,8,128]{3,2,1,0:T(8,128)S(1)} %shard_map.66.ops, f32[11,64,8,128]{3,2,1,0:T(8,128)S(1)} %shard_map.64.smooth, f32[16,8,128]{2,1,0:T(8,128)S(1)} %all_to_all.15.received), custom_call_target="tpu_custom_call" | custom-call | tf_op jit(solution)/shard_map/pallas_call | solution.py:29
  48.0 22.7 %all_to_all.16.received = f32[8,2,8,128]{3,2,1,0:T(8,128)S(1)} all-to-all(f32[8,2,8,128]{3,2,1,0:T(8,128)S(1)} %get-tuple-element.21), channel_id=1, replica_groups={{0,128,256,384,512,640,768,896},{8,136,264,392,520,648,776,904},{16,144..., dimensions={0} | all-to-all | bytes 131072 | tf_op jit(solution)/shard_map/all_to_all | solution.py:392
  70.6 1.5 %shard_map.69 = (f32[8,3,8,128]{3,2,1,0:T(8,128)S(1)}, f32[2,8,128]{2,1,0:T(8,128)S(1)}) custom-call(f32[10,64,8,128]{3,2,1,0:T(8,128)S(1)} %shard_map.66.ops, f32[11,64,8,128]{3,2,1,0:T(8,128)S(1)} %shard_map.64.smooth, f32[8,2,8,128]{3,2,1,0:T(8,128)S(1)} %all_to_all.16.received, f32[2,8,128]{2,1,0:T(8,128)S(1)} %get-tuple-element.22.near), custom_call_target="tpu_custom_call" | custom-call | tf_op jit(solution)/shard_map/pallas_call | solution.py:29
  72.2 16.8 %all_to_all.17.received = f32[8,3,8,128]{3,2,1,0:T(8,128)S(1)} all-to-all(f32[8,3,8,128]{3,2,1,0:T(8,128)S(1)} %get-tuple-element.23), channel_id=1, replica_groups=mesh['plan'=128,'height'=8] {'height'}, dimensions={0} | all-to-all | bytes 196608 | tf_op jit(solution)/shard_map/all_to_all | solution.py:392
  89.0 3.9 %shard_map.70.errors = f32[5,8,128]{2,1,0:T(8,128)S(1)} custom-call(f32[10,64,8,128]{3,2,1,0:T(8,128)S(1)} %shard_map.66.ops, f32[11,64,8,128]{3,2,1,0:T(8,128)S(1)} %shard_map.64.smooth, f32[8,3,8,128]{3,2,1,0:T(8,128)S(1)} %all_to_all.17.received, f32[2,8,128]{2,1,0:T(8,128)S(1)} %get-tuple-element.22.near, f32[2,8,128]{2,1,0:T(8,128)S(1)} %get-tuple-element.24.far), custom_call_target="tpu_custom_call" | custom-call | tf_op jit(solution)/shard_map/pallas_call | solution.py:29
  92.9 1.7 %shard_map.71 = f32[64,128]{1,0:T(8,128)} custom-call(f32[72,128]{1,0:T(8,128)S(1)} %shard_map.65.field, f32[72,128]{1,0:T(8,128)S(1)} %collective-permute-done.4.inner, f32[72,128]{1,0:T(8,128)S(1)} %collective-permute-done.5.outer, f32[72,128]{1,0:T(8,128)S(1)} %collective-permute-done.6.above, f32[72,128]{1,0:T(8,128)S(1)} %collective-permute-done.7.below, ...), custom_call_target="tpu_custom_call" | custom-call | tf_op jit(solution)/shard_map/pallas_call | solution.py:29
Async XLA Ops:
  0.0 21.7 %copy-start.2 = (f32[1,1,64,128]{3,2,1,0:T(8,128)S(1)}, f32[1,1,64,128]{3,2,1,0:T(8,128)}, u32[]{:S(2)}) copy-start(f32[1,1,64,128]{3,2,1,0:T(8,128)} %param.6) | copy-start | bytes 98308
  0.0 21.8 %copy-start.4 = (s32[1,1,128]{2,1,0:T(1,128)S(1)}, s32[1,1,128]{2,1,0:T(1,128)}, u32[]{:S(2)}) copy-start(s32[1,1,128]{2,1,0:T(1,128)} %param.9) | copy-start | bytes 1540
  0.0 21.8 %copy-start.3 = (s32[1,1,3,128]{3,1,2,0:T(1,128)S(1)}, s32[1,1,3,128]{3,1,2,0:T(1,128)}, u32[]{:S(2)}) copy-start(s32[1,1,3,128]{3,1,2,0:T(1,128)} %param.8) | copy-start | bytes 4612
  0.0 21.8 %copy-start = (bf16[1,1,3,64,64,128]{5,4,3,2,1,0:T(8,128)(2,1)S(1)}, bf16[1,1,3,64,64,128]{5,4,3,2,1,0:T(8,128)(2,1)}, u32[]{:S(2)}) copy-start(bf16[1,1,3,64,64,128]{5,4,3,2,1,0:T(8,128)(2,1)} %param.7) | copy-start | bytes 9437188
  0.0 21.7 %collective-permute-start.3 = (f32[64,128]{1,0:T(8,128)}, f32[64,128]{1,0:T(8,128)S(1)}, u32[]{:S(2)}, u32[]{:S(2)}) collective-permute-start(f32[64,128]{1,0:T(8,128)} %bitcast.11), channel_id=1, source_target_pairs={{0,1},{1,2},{2,3},{3,4},{4,5},{5,6},{6,7},{8,9},{9,10},{10,11},{11... | collective-permute-start | bytes 98312 | tf_op jit(solution)/shard_map/ppermute | solution.py:375
  3.7 18.0 %collective-permute-start.2 = (f32[64,128]{1,0:T(8,128)}, f32[64,128]{1,0:T(8,128)S(1)}, u32[]{:S(2)}, u32[]{:S(2)}) collective-permute-start(f32[64,128]{1,0:T(8,128)} %bitcast.12), channel_id=1, source_target_pairs={{1,0},{2,1},{3,2},{4,3},{5,4},{6,5},{7,6},{9,8},{10,9},{11,10},{12... | collective-permute-start | bytes 98312 | tf_op jit(solution)/shard_map/ppermute | solution.py:375
  16.7 5.1 %collective-permute-start.1 = (f32[64,128]{1,0:T(8,128)}, f32[64,128]{1,0:T(8,128)S(1)}, u32[]{:S(2)}, u32[]{:S(2)}) collective-permute-start(f32[64,128]{1,0:T(8,128)} %bitcast.13), channel_id=1, source_target_pairs={{8,16},{16,8},{24,32},{32,24},{40,48},{48,40},{56,64},{64,56},{72,... | collective-permute-start | bytes 98312 | tf_op jit(solution)/shard_map/ppermute | solution.py:382
  17.3 4.4 %collective-permute-start = (f32[64,128]{1,0:T(8,128)}, f32[64,128]{1,0:T(8,128)S(1)}, u32[]{:S(2)}, u32[]{:S(2)}) collective-permute-start(f32[64,128]{1,0:T(8,128)} %bitcast.14), channel_id=1, source_target_pairs={{0,8},{8,0},{16,24},{24,16},{32,40},{40,32},{48,56},{56,48},{64,72... | collective-permute-start | bytes 98312 | tf_op jit(solution)/shard_map/ppermute | solution.py:382
  21.7 10.7 %copy-start.1 = (bf16[64,64,160]{2,1,0:T(8,128)(2,1)S(1)}, bf16[64,64,160]{2,1,0:T(8,128)(2,1)}, u32[]{:S(2)}) copy-start(bf16[64,64,160]{2,1,0:T(8,128)(2,1)} %param.10) | copy-start | bytes 3932164
  22.8 11.1 %collective-permute-start.7 = (f32[72,128]{1,0:T(8,128)S(1)}, f32[72,128]{1,0:T(8,128)S(1)}, u32[]{:S(2)}, u32[]{:S(2)}) collective-permute-start(f32[72,128]{1,0:T(8,128)S(1)} %shard_map.65.field), channel_id=1, source_target_pairs={{0,1},{1,2},{2,3},{3,4},{4,5},{5,6},{6,7},{8,9},{9,10},{10,11},{11... | collective-permute-start | bytes 110600 | tf_op jit(solution)/shard_map/ppermute | solution.py:375
  24.7 9.1 %collective-permute-start.6 = (f32[72,128]{1,0:T(8,128)S(1)}, f32[72,128]{1,0:T(8,128)S(1)}, u32[]{:S(2)}, u32[]{:S(2)}) collective-permute-start(f32[72,128]{1,0:T(8,128)S(1)} %shard_map.65.field), channel_id=1, source_target_pairs={{1,0},{2,1},{3,2},{4,3},{5,4},{6,5},{7,6},{9,8},{10,9},{11,10},{12... | collective-permute-start | bytes 110600 | tf_op jit(solution)/shard_map/ppermute | solution.py:375
  28.6 5.2 %collective-permute-start.5 = (f32[72,128]{1,0:T(8,128)S(1)}, f32[72,128]{1,0:T(8,128)S(1)}, u32[]{:S(2)}, u32[]{:S(2)}) collective-permute-start(f32[72,128]{1,0:T(8,128)S(1)} %shard_map.65.field), channel_id=1, source_target_pairs={{8,16},{16,8},{24,32},{32,24},{40,48},{48,40},{56,64},{64,56},{72,... | collective-permute-start | bytes 110600 | tf_op jit(solution)/shard_map/ppermute | solution.py:382
  29.3 4.6 %collective-permute-start.4 = (f32[72,128]{1,0:T(8,128)S(1)}, f32[72,128]{1,0:T(8,128)S(1)}, u32[]{:S(2)}, u32[]{:S(2)}) collective-permute-start(f32[72,128]{1,0:T(8,128)S(1)} %shard_map.65.field), channel_id=1, source_target_pairs={{0,8},{8,0},{16,24},{24,16},{32,40},{40,32},{48,56},{56,48},{64,72... | collective-permute-start | bytes 110600 | tf_op jit(solution)/shard_map/ppermute | solution.py:382

commit v6 on v5

--- a/solution.py
+++ b/solution.py
@@ -239,6 +239,15 @@
     return [fold(total) for total in totals]
 
 
+def turn_step(ops, smooth, level, lows, highs):
+    columns = lows + highs
+    smoothed = block_product(smooth, level, columns, max(level - 1, 0))
+    columns = [pltpu.roll(v, NC, 1) for v in columns]
+    rest = [g - a for g, a in zip(columns, block_product(ops, level, smoothed, level))]
+    fixed = block_product(smooth, level, rest[: len(lows)], level)
+    return rest[len(lows) :], [z + f for z, f in zip(smoothed, fixed)]
+
+
 def up_step(ops, smooth, level, lows, highs):
     columns = lows + highs
     smoothed = block_product(smooth, level, columns, max(level - 1, 0))
@@ -250,10 +259,9 @@
 
 
 def down_step(ops, smooth, level, errors, saved):
-    totals = []
-    for number, error in enumerate(errors):
-        total = pltpu.roll(saved[number][1], NC, 1) if saved else error
-        totals.append(total if error is None or not saved else total + error)
+    totals = errors
+    if saved:
+        totals = [pltpu.roll(z, NC, 1) + e for e, (_, z) in zip(errors, saved)]
     applied = block_product(ops, level, totals, level + 1)
     if saved:
         applied = [a - g for a, (g, _) in zip(applied, saved)]
@@ -263,10 +271,10 @@
 
 def group_sum(load, member, bits):
     start = (member >> bits) << bits
-    total = load(start)
-    for other in range(1, 2**bits):
-        total = total + load(start + other)
-    return total * 2.0 ** (-bits / 2)
+    terms = [load(start + other) for other in range(2**bits)]
+    while len(terms) > 1:
+        terms = [a + b for a, b in zip(terms[0::2], terms[1::2])]
+    return terms[0] * 2.0 ** (-bits / 2)
 
 
 def near_body(ops, smooth, received, sent, kept):
@@ -281,12 +289,12 @@
         highs += [group_sum(load, me, level), group_sum(load, across, level)]
     highs.append(group_sum(load, me, bits))
     saved = []
-    for level in range(bits):
+    for level in range(bits - 1):
         pairs, rest = up_step(ops, smooth, level, lows, highs)
         saved.append(pairs)
         lows, highs = rest[:2], rest[2:]
-    errors = [None, None]
-    for level in reversed(range(1, bits)):
+    lows, errors = turn_step(ops, smooth, bits - 1, lows, highs)
+    for level in reversed(range(1, bits - 1)):
         errors = down_step(ops, smooth, level, errors, saved[level])
     errors = down_step(ops, smooth, 0, [errors[0], errors[0], errors[1]], saved[0])
     for copy in range(sent.shape[0]):
@@ -311,12 +319,12 @@
         highs += [group_sum(load, me, level), group_sum(load, across, level)]
     highs.append(group_sum(load, me, bits))
     saved = []
-    for level in range(bits):
+    for level in range(bits - 1):
         pairs, rest = up_step(ops, smooth, first + level, lows, highs)
         saved.append(pairs)
         lows, highs = rest[:2], rest[2:]
-    errors = [None, None]
-    for level in reversed(range(bits)):
+    lows, errors = turn_step(ops, smooth, first + bits - 1, lows, highs)
+    for level in reversed(range(bits - 1)):
         errors = down_step(ops, smooth, first + level, errors, saved[level])
     for copy in range(sent.shape[0]):
         sent[copy, 0] = lows[0]

time: 95 us -> 94.9 us (level)
  no operation moved by 1% of the time
where the time goes in v6:
time: 94.9 us; the launch traced here: 94.5 us
  blocking collectives  50.2 us (53%)
  starting transfers between devices  28.8 us (30%)
  Pallas kernels  15.1 us (16%)
    all_to_all x3, blocking collectives, exchange(): lax.all_to_all(value, axis, 0, 0, axis_index_groups=groups, tiled=True)  50.2 us
    ppermute x4, starting transfers between devices, shifted(): return lax.ppermute(value, 'height', pairs)  22.5 us
    pallas_call x6, Pallas kernels, call(): pl.pallas_call(body, out_shape=out_shape, in_specs=whole(len(inputs)), ou...  11.3 us
    ppermute x4, starting transfers between devices, swapped(): return lax.ppermute(value, 'plan', pairs)  6.35 us
    pallas_call x2, Pallas kernels, pack(): pl.pallas_call(stream_body if streamed else pack_body, out_shape=jax.Shap...  3.81 us
  transfers between devices with their start and end apart: 8, of which 0 were waited for; matrix products, arithmetic and copies ran while one was open for 0% of the time, Pallas kernels for 4%

profile of v6, /device:TPU:2, one launch (start us, length us, event | category | flops | bytes accessed | tf_op | source)
XLA Modules:
  0.0 94.5 jit_solution(16705518262586430917)
XLA Ops:
  0.0 0.0 copy-start.2
  0.0 0.0 copy-start.4
  0.0 0.0 copy-start.3
  0.0 0.0 copy-start
  0.0 3.7 %collective-permute-start.3 = (f32[64,128]{1,0:T(8,128)}, f32[64,128]{1,0:T(8,128)S(1)}, u32[]{:S(2)}, u32[]{:S(2)}) collective-permute-start(f32[64,128]{1,0:T(8,128)} %bitcast.11), channel_id=1, source_target_pairs={{0,1},{1,2},{2,3},{3,4},{4,5},{5,6},{6,7},{8,9},{9,10},{10,11},{11... | collective-permute-start | bytes 98312 | tf_op jit(solution)/shard_map/ppermute | solution.py:383
  3.7 13.0 %collective-permute-start.2 = (f32[64,128]{1,0:T(8,128)}, f32[64,128]{1,0:T(8,128)S(1)}, u32[]{:S(2)}, u32[]{:S(2)}) collective-permute-start(f32[64,128]{1,0:T(8,128)} %bitcast.12), channel_id=1, source_target_pairs={{1,0},{2,1},{3,2},{4,3},{5,4},{6,5},{7,6},{9,8},{10,9},{11,10},{12... | collective-permute-start | bytes 98312 | tf_op jit(solution)/shard_map/ppermute | solution.py:383
  16.7 0.7 collective-permute-start.1
  17.3 1.9 %collective-permute-start = (f32[64,128]{1,0:T(8,128)}, f32[64,128]{1,0:T(8,128)S(1)}, u32[]{:S(2)}, u32[]{:S(2)}) collective-permute-start(f32[64,128]{1,0:T(8,128)} %bitcast.14), channel_id=1, source_target_pairs={{0,8},{8,0},{16,24},{24,16},{32,40},{40,32},{48,56},{56,48},{64,72... | collective-permute-start | bytes 98312 | tf_op jit(solution)/shard_map/ppermute | solution.py:390
  19.3 2.4 %shard_map.64.smooth = f32[11,64,8,128]{3,2,1,0:T(8,128)S(1)} custom-call(bf16[8,8,64,176]{3,2,1,0:T(8,128)(2,1)} %bitcast.23), custom_call_target="tpu_custom_call" | custom-call | tf_op jit(solution)/shard_map/pallas_call | solution.py:215
  21.7 0.0 copy-start.1
  21.7 0.0 collective-permute-done.3.below
  21.7 0.0 collective-permute-done.2.above
  21.7 0.0 collective-permute-done.1.outer
  21.7 0.0 collective-permute-done.inner
  21.7 0.0 copy-done.2
  21.8 0.0 copy-done.4
  21.8 0.0 copy-done.3
  21.8 0.0 copy-done
  21.8 1.0 %shard_map.65.field = f32[72,128]{1,0:T(8,128)S(1)} custom-call(f32[64,128]{1,0:T(8,128)S(1)} %bitcast.15, f32[64,128]{1,0:T(8,128)S(1)} %collective-permute-done.inner, f32[64,128]{1,0:T(8,128)S(1)} %collective-permute-done.1.outer, f32[64,128]{1,0:T(8,128)S(1)} %collective-permute-done.2.above, f32[64,128]{1,0:T(8,128)S(1)} %collective-permute-done.3.below, ...), custom_call_target="tpu_custom_call" | custom-call | tf_op jit(solution)/shard_map/pallas_call | solution.py:29
  22.8 1.9 %collective-permute-start.7 = (f32[72,128]{1,0:T(8,128)S(1)}, f32[72,128]{1,0:T(8,128)S(1)}, u32[]{:S(2)}, u32[]{:S(2)}) collective-permute-start(f32[72,128]{1,0:T(8,128)S(1)} %shard_map.65.field), channel_id=1, source_target_pairs={{0,1},{1,2},{2,3},{3,4},{4,5},{5,6},{6,7},{8,9},{9,10},{10,11},{11... | collective-permute-start | bytes 110600 | tf_op jit(solution)/shard_map/ppermute | solution.py:383
  24.7 3.9 %collective-permute-start.6 = (f32[72,128]{1,0:T(8,128)S(1)}, f32[72,128]{1,0:T(8,128)S(1)}, u32[]{:S(2)}, u32[]{:S(2)}) collective-permute-start(f32[72,128]{1,0:T(8,128)S(1)} %shard_map.65.field), channel_id=1, source_target_pairs={{1,0},{2,1},{3,2},{4,3},{5,4},{6,5},{7,6},{9,8},{10,9},{11,10},{12... | collective-permute-start | bytes 110600 | tf_op jit(solution)/shard_map/ppermute | solution.py:383
  28.6 0.7 collective-permute-start.5
  29.3 3.1 %collective-permute-start.4 = (f32[72,128]{1,0:T(8,128)S(1)}, f32[72,128]{1,0:T(8,128)S(1)}, u32[]{:S(2)}, u32[]{:S(2)}) collective-permute-start(f32[72,128]{1,0:T(8,128)S(1)} %shard_map.65.field), channel_id=1, source_target_pairs={{0,8},{8,0},{16,24},{24,16},{32,40},{40,32},{48,56},{56,48},{64,72... | collective-permute-start | bytes 110600 | tf_op jit(solution)/shard_map/ppermute | solution.py:390
  32.4 0.0 copy-done.1
  32.4 1.4 %shard_map.66.ops = f32[10,64,8,128]{3,2,1,0:T(8,128)S(1)} custom-call(bf16[8,8,64,160]{3,2,1,0:T(8,128)(2,1)S(1)} %bitcast.10), custom_call_target="tpu_custom_call" | custom-call | tf_op jit(solution)/shard_map/pallas_call | solution.py:215
  33.8 0.0 collective-permute-done.7.below
  33.8 0.0 collective-permute-done.6.above
  33.8 0.0 collective-permute-done.5.outer
  33.8 0.0 collective-permute-done.4.inner
  33.8 1.2 %shard_map.67 = f32[16,8,128]{2,1,0:T(8,128)S(1)} custom-call(f32[72,128]{1,0:T(8,128)S(1)} %shard_map.65.field, f32[72,128]{1,0:T(8,128)S(1)} %collective-permute-done.4.inner, f32[72,128]{1,0:T(8,128)S(1)} %collective-permute-done.5.outer, f32[72,128]{1,0:T(8,128)S(1)} %collective-permute-done.6.above, f32[72,128]{1,0:T(8,128)S(1)} %collective-permute-done.7.below, ...), custom_call_target="tpu_custom_call" | custom-call | tf_op jit(solution)/shard_map/pallas_call | solution.py:29
  35.0 10.8 %all_to_all.15.received = f32[16,8,128]{2,1,0:T(8,128)S(1)} all-to-all(f32[16,8,128]{2,1,0:T(8,128)S(1)} %shard_map.67), channel_id=1, replica_groups={{0,8,16,24,32,40,48,56,64,72,80,88,96,104,112,120},{128,136,144,152,160..., dimensions={0} | all-to-all | bytes 131072 | tf_op jit(solution)/shard_map/all_to_all | solution.py:400
  45.8 2.1 %shard_map.68 = (f32[8,2,8,128]{3,2,1,0:T(8,128)S(1)}, f32[2,8,128]{2,1,0:T(8,128)S(1)}) custom-call(f32[10,64,8,128]{3,2,1,0:T(8,128)S(1)} %shard_map.66.ops, f32[11,64,8,128]{3,2,1,0:T(8,128)S(1)} %shard_map.64.smooth, f32[16,8,128]{2,1,0:T(8,128)S(1)} %all_to_all.15.received), custom_call_target="tpu_custom_call" | custom-call | tf_op jit(solution)/shard_map/pallas_call | solution.py:29
  47.9 22.7 %all_to_all.16.received = f32[8,2,8,128]{3,2,1,0:T(8,128)S(1)} all-to-all(f32[8,2,8,128]{3,2,1,0:T(8,128)S(1)} %get-tuple-element.21), channel_id=1, replica_groups={{0,128,256,384,512,640,768,896},{8,136,264,392,520,648,776,904},{16,144..., dimensions={0} | all-to-all | bytes 131072 | tf_op jit(solution)/shard_map/all_to_all | solution.py:400
  70.6 1.5 %shard_map.69 = (f32[8,3,8,128]{3,2,1,0:T(8,128)S(1)}, f32[2,8,128]{2,1,0:T(8,128)S(1)}) custom-call(f32[10,64,8,128]{3,2,1,0:T(8,128)S(1)} %shard_map.66.ops, f32[11,64,8,128]{3,2,1,0:T(8,128)S(1)} %shard_map.64.smooth, f32[8,2,8,128]{3,2,1,0:T(8,128)S(1)} %all_to_all.16.received, f32[2,8,128]{2,1,0:T(8,128)S(1)} %get-tuple-element.22.near), custom_call_target="tpu_custom_call" | custom-call | tf_op jit(solution)/shard_map/pallas_call | solution.py:29
  72.1 16.8 %all_to_all.17.received = f32[8,3,8,128]{3,2,1,0:T(8,128)S(1)} all-to-all(f32[8,3,8,128]{3,2,1,0:T(8,128)S(1)} %get-tuple-element.23), channel_id=1, replica_groups=mesh['plan'=128,'height'=8] {'height'}, dimensions={0} | all-to-all | bytes 196608 | tf_op jit(solution)/shard_map/all_to_all | solution.py:400
  88.8 3.9 %shard_map.70.errors = f32[5,8,128]{2,1,0:T(8,128)S(1)} custom-call(f32[10,64,8,128]{3,2,1,0:T(8,128)S(1)} %shard_map.66.ops, f32[11,64,8,128]{3,2,1,0:T(8,128)S(1)} %shard_map.64.smooth, f32[8,3,8,128]{3,2,1,0:T(8,128)S(1)} %all_to_all.17.received, f32[2,8,128]{2,1,0:T(8,128)S(1)} %get-tuple-element.22.near, f32[2,8,128]{2,1,0:T(8,128)S(1)} %get-tuple-element.24.far), custom_call_target="tpu_custom_call" | custom-call | tf_op jit(solution)/shard_map/pallas_call | solution.py:29
  92.8 1.7 %shard_map.71 = f32[64,128]{1,0:T(8,128)} custom-call(f32[72,128]{1,0:T(8,128)S(1)} %shard_map.65.field, f32[72,128]{1,0:T(8,128)S(1)} %collective-permute-done.4.inner, f32[72,128]{1,0:T(8,128)S(1)} %collective-permute-done.5.outer, f32[72,128]{1,0:T(8,128)S(1)} %collective-permute-done.6.above, f32[72,128]{1,0:T(8,128)S(1)} %collective-permute-done.7.below, ...), custom_call_target="tpu_custom_call" | custom-call | tf_op jit(solution)/shard_map/pallas_call | solution.py:29
Async XLA Ops:
  0.0 21.7 %copy-start.2 = (f32[1,1,64,128]{3,2,1,0:T(8,128)S(1)}, f32[1,1,64,128]{3,2,1,0:T(8,128)}, u32[]{:S(2)}) copy-start(f32[1,1,64,128]{3,2,1,0:T(8,128)} %param.6) | copy-start | bytes 98308
  0.0 21.8 %copy-start.4 = (s32[1,1,128]{2,1,0:T(1,128)S(1)}, s32[1,1,128]{2,1,0:T(1,128)}, u32[]{:S(2)}) copy-start(s32[1,1,128]{2,1,0:T(1,128)} %param.9) | copy-start | bytes 1540
  0.0 21.8 %copy-start.3 = (s32[1,1,3,128]{3,1,2,0:T(1,128)S(1)}, s32[1,1,3,128]{3,1,2,0:T(1,128)}, u32[]{:S(2)}) copy-start(s32[1,1,3,128]{3,1,2,0:T(1,128)} %param.8) | copy-start | bytes 4612
  0.0 21.8 %copy-start = (bf16[1,1,3,64,64,128]{5,4,3,2,1,0:T(8,128)(2,1)S(1)}, bf16[1,1,3,64,64,128]{5,4,3,2,1,0:T(8,128)(2,1)}, u32[]{:S(2)}) copy-start(bf16[1,1,3,64,64,128]{5,4,3,2,1,0:T(8,128)(2,1)} %param.7) | copy-start | bytes 9437188
  0.0 21.7 %collective-permute-start.3 = (f32[64,128]{1,0:T(8,128)}, f32[64,128]{1,0:T(8,128)S(1)}, u32[]{:S(2)}, u32[]{:S(2)}) collective-permute-start(f32[64,128]{1,0:T(8,128)} %bitcast.11), channel_id=1, source_target_pairs={{0,1},{1,2},{2,3},{3,4},{4,5},{5,6},{6,7},{8,9},{9,10},{10,11},{11... | collective-permute-start | bytes 98312 | tf_op jit(solution)/shard_map/ppermute | solution.py:383
  3.7 18.0 %collective-permute-start.2 = (f32[64,128]{1,0:T(8,128)}, f32[64,128]{1,0:T(8,128)S(1)}, u32[]{:S(2)}, u32[]{:S(2)}) collective-permute-start(f32[64,128]{1,0:T(8,128)} %bitcast.12), channel_id=1, source_target_pairs={{1,0},{2,1},{3,2},{4,3},{5,4},{6,5},{7,6},{9,8},{10,9},{11,10},{12... | collective-permute-start | bytes 98312 | tf_op jit(solution)/shard_map/ppermute | solution.py:383
  16.7 5.1 %collective-permute-start.1 = (f32[64,128]{1,0:T(8,128)}, f32[64,128]{1,0:T(8,128)S(1)}, u32[]{:S(2)}, u32[]{:S(2)}) collective-permute-start(f32[64,128]{1,0:T(8,128)} %bitcast.13), channel_id=1, source_target_pairs={{8,16},{16,8},{24,32},{32,24},{40,48},{48,40},{56,64},{64,56},{72,... | collective-permute-start | bytes 98312 | tf_op jit(solution)/shard_map/ppermute | solution.py:390
  17.3 4.4 %collective-permute-start = (f32[64,128]{1,0:T(8,128)}, f32[64,128]{1,0:T(8,128)S(1)}, u32[]{:S(2)}, u32[]{:S(2)}) collective-permute-start(f32[64,128]{1,0:T(8,128)} %bitcast.14), channel_id=1, source_target_pairs={{0,8},{8,0},{16,24},{24,16},{32,40},{40,32},{48,56},{56,48},{64,72... | collective-permute-start | bytes 98312 | tf_op jit(solution)/shard_map/ppermute | solution.py:390
  21.7 10.7 %copy-start.1 = (bf16[64,64,160]{2,1,0:T(8,128)(2,1)S(1)}, bf16[64,64,160]{2,1,0:T(8,128)(2,1)}, u32[]{:S(2)}) copy-start(bf16[64,64,160]{2,1,0:T(8,128)(2,1)} %param.10) | copy-start | bytes 3932164
  22.8 11.1 %collective-permute-start.7 = (f32[72,128]{1,0:T(8,128)S(1)}, f32[72,128]{1,0:T(8,128)S(1)}, u32[]{:S(2)}, u32[]{:S(2)}) collective-permute-start(f32[72,128]{1,0:T(8,128)S(1)} %shard_map.65.field), channel_id=1, source_target_pairs={{0,1},{1,2},{2,3},{3,4},{4,5},{5,6},{6,7},{8,9},{9,10},{10,11},{11... | collective-permute-start | bytes 110600 | tf_op jit(solution)/shard_map/ppermute | solution.py:383
  24.7 9.1 %collective-permute-start.6 = (f32[72,128]{1,0:T(8,128)S(1)}, f32[72,128]{1,0:T(8,128)S(1)}, u32[]{:S(2)}, u32[]{:S(2)}) collective-permute-start(f32[72,128]{1,0:T(8,128)S(1)} %shard_map.65.field), channel_id=1, source_target_pairs={{1,0},{2,1},{3,2},{4,3},{5,4},{6,5},{7,6},{9,8},{10,9},{11,10},{12... | collective-permute-start | bytes 110600 | tf_op jit(solution)/shard_map/ppermute | solution.py:383
  28.6 5.2 %collective-permute-start.5 = (f32[72,128]{1,0:T(8,128)S(1)}, f32[72,128]{1,0:T(8,128)S(1)}, u32[]{:S(2)}, u32[]{:S(2)}) collective-permute-start(f32[72,128]{1,0:T(8,128)S(1)} %shard_map.65.field), channel_id=1, source_target_pairs={{8,16},{16,8},{24,32},{32,24},{40,48},{48,40},{56,64},{64,56},{72,... | collective-permute-start | bytes 110600 | tf_op jit(solution)/shard_map/ppermute | solution.py:390
  29.3 4.6 %collective-permute-start.4 = (f32[72,128]{1,0:T(8,128)S(1)}, f32[72,128]{1,0:T(8,128)S(1)}, u32[]{:S(2)}, u32[]{:S(2)}) collective-permute-start(f32[72,128]{1,0:T(8,128)S(1)} %shard_map.65.field), channel_id=1, source_target_pairs={{0,8},{8,0},{16,24},{24,16},{32,40},{40,32},{48,56},{56,48},{64,72... | collective-permute-start | bytes 110600 | tf_op jit(solution)/shard_map/ppermute | solution.py:390

commit v7 on v5

--- a/solution.py
+++ b/solution.py
@@ -59,7 +59,7 @@
 
 def pick(fields, links_ref):
     odd = lax.axis_index("plan") & 1
-    numbers = (0, 4 - odd, 3 + odd, 2, 1)
+    numbers = (0, 4 - odd, 2, 3 + odd, 1)
     picked = []
     for which in range(3):
         link = jnp.broadcast_to(links_ref[which], (BS, NB))
@@ -92,8 +92,8 @@
     lax.fori_loop(0, GROUPS, body, 0)
 
 
-def first_body(source, inner, outer, above, below, weights, links, owners, second):
-    fields = [ref[...] for ref in (source, inner, outer, above, below)]
+def first_body(source, inner, above, outer, below, weights, links, owners, second):
+    fields = [ref[...] for ref in (source, inner, above, outer, below)]
     picked = pick(fields, links)
 
     def step(tile, rows):
@@ -105,8 +105,8 @@
     second[BS:, :] = jnp.broadcast_to(owners[...].astype(F32), (SUB, NB))
 
 
-def second_body(field, inner, outer, above, below, weights, links, source, owners, sent, left):
-    fields = [ref[0:BS, :] for ref in (field, inner, outer, above, below)]
+def second_body(field, inner, above, outer, below, weights, links, source, owners, sent, left):
+    fields = [ref[0:BS, :] for ref in (field, inner, above, outer, below)]
     picked = pick(fields, links)
 
     def step(tile, rows):
@@ -130,9 +130,9 @@
         sent[copy] = packed
 
 
-def last_body(field, inner, outer, above, below, errors, weights, links, source, out, third):
+def last_body(field, inner, above, outer, below, errors, weights, links, source, out, third):
     fields = []
-    for number, ref in enumerate((field, inner, outer, above, below)):
+    for number, ref in enumerate((field, inner, above, outer, below)):
         error = errors[number]
         owner = ref[BS:, :].astype(jnp.int32)
         added = [take_lanes(error, owner + group * NC) for group in range(GROUPS)]
@@ -364,8 +364,8 @@
     zero = jnp.zeros((SUB, NB), F32)
     errors[0] = parts[0] + near[0]
     errors[1] = parts[0] + near[1]
-    errors[2] = jnp.where((place > 0) & (place < last), parts[1] + far[1], zero)
-    errors[3] = jnp.where(me < count - 1, parts[2] + received[targets[1], 1], zero)
+    errors[3] = jnp.where((place > 0) & (place < last), parts[1] + far[1], zero)
+    errors[2] = jnp.where(me < count - 1, parts[2] + received[targets[1], 1], zero)
     errors[4] = jnp.where(me > 0, parts[3] + received[targets[2], 1], zero)
 
 
@@ -385,7 +385,7 @@
 def halo(value):
     inner, outer = swapped(value, 0), swapped(value, 1)
     above, below = shifted(value, -1), shifted(value, 1)
-    return inner, outer, above, below
+    return inner, above, outer, below
 
 
 def exchange(value, axis, groups=None):

time: 95 us -> 95 us (level)
  no operation moved by 1% of the time
where the time goes in v7:
time: 95 us; the launch traced here: 94.6 us
  blocking collectives  50.2 us (53%)
  starting transfers between devices  28.8 us (30%)
  Pallas kernels  15.3 us (16%)
    all_to_all x3, blocking collectives, exchange(): lax.all_to_all(value, axis, 0, 0, axis_index_groups=groups, tiled=True)  50.2 us
    ppermute x4, starting transfers between devices, shifted(): return lax.ppermute(value, 'height', pairs)  22.5 us
    pallas_call x6, Pallas kernels, call(): pl.pallas_call(body, out_shape=out_shape, in_specs=whole(len(inputs)), ou...  11.5 us
    ppermute x4, starting transfers between devices, swapped(): return lax.ppermute(value, 'plan', pairs)  6.35 us
    pallas_call x2, Pallas kernels, pack(): pl.pallas_call(stream_body if streamed else pack_body, out_shape=jax.Shap...  3.81 us
  transfers between devices with their start and end apart: 8, of which 0 were waited for; matrix products, arithmetic and copies ran while one was open for 0% of the time, Pallas kernels for 4%

profile of v7, /device:TPU:2, one launch (start us, length us, event | category | flops | bytes accessed | tf_op | source)
XLA Modules:
  0.0 94.6 jit_solution(18128635107272102084)
XLA Ops:
  0.0 0.0 copy-start.2
  0.0 0.0 copy-start.4
  0.0 0.0 copy-start.3
  0.0 0.0 copy-start
  0.0 3.7 %collective-permute-start.3 = (f32[64,128]{1,0:T(8,128)}, f32[64,128]{1,0:T(8,128)S(1)}, u32[]{:S(2)}, u32[]{:S(2)}) collective-permute-start(f32[64,128]{1,0:T(8,128)} %bitcast.11), channel_id=1, source_target_pairs={{0,1},{1,2},{2,3},{3,4},{4,5},{5,6},{6,7},{8,9},{9,10},{10,11},{11... | collective-permute-start | bytes 98312 | tf_op jit(solution)/shard_map/ppermute | solution.py:375
  3.7 0.7 collective-permute-start.2
  4.4 13.0 %collective-permute-start.1 = (f32[64,128]{1,0:T(8,128)}, f32[64,128]{1,0:T(8,128)S(1)}, u32[]{:S(2)}, u32[]{:S(2)}) collective-permute-start(f32[64,128]{1,0:T(8,128)} %bitcast.13), channel_id=1, source_target_pairs={{1,0},{2,1},{3,2},{4,3},{5,4},{6,5},{7,6},{9,8},{10,9},{11,10},{12... | collective-permute-start | bytes 98312 | tf_op jit(solution)/shard_map/ppermute | solution.py:375
  17.3 1.9 %collective-permute-start = (f32[64,128]{1,0:T(8,128)}, f32[64,128]{1,0:T(8,128)S(1)}, u32[]{:S(2)}, u32[]{:S(2)}) collective-permute-start(f32[64,128]{1,0:T(8,128)} %bitcast.14), channel_id=1, source_target_pairs={{0,8},{8,0},{16,24},{24,16},{32,40},{40,32},{48,56},{56,48},{64,72... | collective-permute-start | bytes 98312 | tf_op jit(solution)/shard_map/ppermute | solution.py:382
  19.3 2.4 %shard_map.64.smooth = f32[11,64,8,128]{3,2,1,0:T(8,128)S(1)} custom-call(bf16[8,8,64,176]{3,2,1,0:T(8,128)(2,1)} %bitcast.23), custom_call_target="tpu_custom_call" | custom-call | tf_op jit(solution)/shard_map/pallas_call | solution.py:215
  21.7 0.0 copy-start.1
  21.7 0.0 collective-permute-done.3.below
  21.7 0.0 collective-permute-done.2.outer
  21.7 0.0 collective-permute-done.1.above
  21.7 0.0 collective-permute-done.inner
  21.7 0.0 copy-done.2
  21.8 0.0 copy-done.4
  21.8 0.0 copy-done.3
  21.8 0.0 copy-done
  21.8 1.0 %shard_map.65.field = f32[72,128]{1,0:T(8,128)S(1)} custom-call(f32[64,128]{1,0:T(8,128)S(1)} %bitcast.15, f32[64,128]{1,0:T(8,128)S(1)} %collective-permute-done.inner, f32[64,128]{1,0:T(8,128)S(1)} %collective-permute-done.1.above, f32[64,128]{1,0:T(8,128)S(1)} %collective-permute-done.2.outer, f32[64,128]{1,0:T(8,128)S(1)} %collective-permute-done.3.below, ...), custom_call_target="tpu_custom_call" | custom-call | tf_op jit(solution)/shard_map/pallas_call | solution.py:29
  22.8 1.9 %collective-permute-start.7 = (f32[72,128]{1,0:T(8,128)S(1)}, f32[72,128]{1,0:T(8,128)S(1)}, u32[]{:S(2)}, u32[]{:S(2)}) collective-permute-start(f32[72,128]{1,0:T(8,128)S(1)} %shard_map.65.field), channel_id=1, source_target_pairs={{0,1},{1,2},{2,3},{3,4},{4,5},{5,6},{6,7},{8,9},{9,10},{10,11},{11... | collective-permute-start | bytes 110600 | tf_op jit(solution)/shard_map/ppermute | solution.py:375
  24.7 0.7 collective-permute-start.6
  25.4 3.9 %collective-permute-start.5 = (f32[72,128]{1,0:T(8,128)S(1)}, f32[72,128]{1,0:T(8,128)S(1)}, u32[]{:S(2)}, u32[]{:S(2)}) collective-permute-start(f32[72,128]{1,0:T(8,128)S(1)} %shard_map.65.field), channel_id=1, source_target_pairs={{1,0},{2,1},{3,2},{4,3},{5,4},{6,5},{7,6},{9,8},{10,9},{11,10},{12... | collective-permute-start | bytes 110600 | tf_op jit(solution)/shard_map/ppermute | solution.py:375
  29.3 3.1 %collective-permute-start.4 = (f32[72,128]{1,0:T(8,128)S(1)}, f32[72,128]{1,0:T(8,128)S(1)}, u32[]{:S(2)}, u32[]{:S(2)}) collective-permute-start(f32[72,128]{1,0:T(8,128)S(1)} %shard_map.65.field), channel_id=1, source_target_pairs={{0,8},{8,0},{16,24},{24,16},{32,40},{40,32},{48,56},{56,48},{64,72... | collective-permute-start | bytes 110600 | tf_op jit(solution)/shard_map/ppermute | solution.py:382
  32.4 0.0 copy-done.1
  32.4 1.4 %shard_map.66.ops = f32[10,64,8,128]{3,2,1,0:T(8,128)S(1)} custom-call(bf16[8,8,64,160]{3,2,1,0:T(8,128)(2,1)S(1)} %bitcast.10), custom_call_target="tpu_custom_call" | custom-call | tf_op jit(solution)/shard_map/pallas_call | solution.py:215
  33.8 0.0 collective-permute-done.7.below
  33.8 0.0 collective-permute-done.6.outer
  33.8 0.0 collective-permute-done.5.above
  33.8 0.0 collective-permute-done.4.inner
  33.8 1.2 %shard_map.67 = f32[16,8,128]{2,1,0:T(8,128)S(1)} custom-call(f32[72,128]{1,0:T(8,128)S(1)} %shard_map.65.field, f32[72,128]{1,0:T(8,128)S(1)} %collective-permute-done.4.inner, f32[72,128]{1,0:T(8,128)S(1)} %collective-permute-done.5.above, f32[72,128]{1,0:T(8,128)S(1)} %collective-permute-done.6.outer, f32[72,128]{1,0:T(8,128)S(1)} %collective-permute-done.7.below, ...), custom_call_target="tpu_custom_call" | custom-call | tf_op jit(solution)/shard_map/pallas_call | solution.py:29
  35.0 11.1 %all_to_all.15.received = f32[16,8,128]{2,1,0:T(8,128)S(1)} all-to-all(f32[16,8,128]{2,1,0:T(8,128)S(1)} %shard_map.67), channel_id=1, replica_groups={{0,8,16,24,32,40,48,56,64,72,80,88,96,104,112,120},{128,136,144,152,160..., dimensions={0} | all-to-all | bytes 131072 | tf_op jit(solution)/shard_map/all_to_all | solution.py:392
  46.1 2.1 %shard_map.68 = (f32[8,2,8,128]{3,2,1,0:T(8,128)S(1)}, f32[2,8,128]{2,1,0:T(8,128)S(1)}) custom-call(f32[10,64,8,128]{3,2,1,0:T(8,128)S(1)} %shard_map.66.ops, f32[11,64,8,128]{3,2,1,0:T(8,128)S(1)} %shard_map.64.smooth, f32[16,8,128]{2,1,0:T(8,128)S(1)} %all_to_all.15.received), custom_call_target="tpu_custom_call" | custom-call | tf_op jit(solution)/shard_map/pallas_call | solution.py:29
  48.2 22.8 %all_to_all.16.received = f32[8,2,8,128]{3,2,1,0:T(8,128)S(1)} all-to-all(f32[8,2,8,128]{3,2,1,0:T(8,128)S(1)} %get-tuple-element.21), channel_id=1, replica_groups={{0,128,256,384,512,640,768,896},{8,136,264,392,520,648,776,904},{16,144..., dimensions={0} | all-to-all | bytes 131072 | tf_op jit(solution)/shard_map/all_to_all | solution.py:392
  71.0 1.5 %shard_map.69 = (f32[8,3,8,128]{3,2,1,0:T(8,128)S(1)}, f32[2,8,128]{2,1,0:T(8,128)S(1)}) custom-call(f32[10,64,8,128]{3,2,1,0:T(8,128)S(1)} %shard_map.66.ops, f32[11,64,8,128]{3,2,1,0:T(8,128)S(1)} %shard_map.64.smooth, f32[8,2,8,128]{3,2,1,0:T(8,128)S(1)} %all_to_all.16.received, f32[2,8,128]{2,1,0:T(8,128)S(1)} %get-tuple-element.22.near), custom_call_target="tpu_custom_call" | custom-call | tf_op jit(solution)/shard_map/pallas_call | solution.py:29
  72.6 16.4 %all_to_all.17.received = f32[8,3,8,128]{3,2,1,0:T(8,128)S(1)} all-to-all(f32[8,3,8,128]{3,2,1,0:T(8,128)S(1)} %get-tuple-element.23), channel_id=1, replica_groups=mesh['plan'=128,'height'=8] {'height'}, dimensions={0} | all-to-all | bytes 196608 | tf_op jit(solution)/shard_map/all_to_all | solution.py:392
  89.0 3.9 %shard_map.70.errors = f32[5,8,128]{2,1,0:T(8,128)S(1)} custom-call(f32[10,64,8,128]{3,2,1,0:T(8,128)S(1)} %shard_map.66.ops, f32[11,64,8,128]{3,2,1,0:T(8,128)S(1)} %shard_map.64.smooth, f32[8,3,8,128]{3,2,1,0:T(8,128)S(1)} %all_to_all.17.received, f32[2,8,128]{2,1,0:T(8,128)S(1)} %get-tuple-element.22.near, f32[2,8,128]{2,1,0:T(8,128)S(1)} %get-tuple-element.24.far), custom_call_target="tpu_custom_call" | custom-call | tf_op jit(solution)/shard_map/pallas_call | solution.py:29
  92.9 1.7 %shard_map.71 = f32[64,128]{1,0:T(8,128)} custom-call(f32[72,128]{1,0:T(8,128)S(1)} %shard_map.65.field, f32[72,128]{1,0:T(8,128)S(1)} %collective-permute-done.4.inner, f32[72,128]{1,0:T(8,128)S(1)} %collective-permute-done.5.above, f32[72,128]{1,0:T(8,128)S(1)} %collective-permute-done.6.outer, f32[72,128]{1,0:T(8,128)S(1)} %collective-permute-done.7.below, ...), custom_call_target="tpu_custom_call" | custom-call | tf_op jit(solution)/shard_map/pallas_call | solution.py:29
Async XLA Ops:
  0.0 21.7 %copy-start.2 = (f32[1,1,64,128]{3,2,1,0:T(8,128)S(1)}, f32[1,1,64,128]{3,2,1,0:T(8,128)}, u32[]{:S(2)}) copy-start(f32[1,1,64,128]{3,2,1,0:T(8,128)} %param.6) | copy-start | bytes 98308
  0.0 21.8 %copy-start.4 = (s32[1,1,128]{2,1,0:T(1,128)S(1)}, s32[1,1,128]{2,1,0:T(1,128)}, u32[]{:S(2)}) copy-start(s32[1,1,128]{2,1,0:T(1,128)} %param.9) | copy-start | bytes 1540
  0.0 21.8 %copy-start.3 = (s32[1,1,3,128]{3,1,2,0:T(1,128)S(1)}, s32[1,1,3,128]{3,1,2,0:T(1,128)}, u32[]{:S(2)}) copy-start(s32[1,1,3,128]{3,1,2,0:T(1,128)} %param.8) | copy-start | bytes 4612
  0.0 21.8 %copy-start = (bf16[1,1,3,64,64,128]{5,4,3,2,1,0:T(8,128)(2,1)S(1)}, bf16[1,1,3,64,64,128]{5,4,3,2,1,0:T(8,128)(2,1)}, u32[]{:S(2)}) copy-start(bf16[1,1,3,64,64,128]{5,4,3,2,1,0:T(8,128)(2,1)} %param.7) | copy-start | bytes 9437188
  0.0 21.7 %collective-permute-start.3 = (f32[64,128]{1,0:T(8,128)}, f32[64,128]{1,0:T(8,128)S(1)}, u32[]{:S(2)}, u32[]{:S(2)}) collective-permute-start(f32[64,128]{1,0:T(8,128)} %bitcast.11), channel_id=1, source_target_pairs={{0,1},{1,2},{2,3},{3,4},{4,5},{5,6},{6,7},{8,9},{9,10},{10,11},{11... | collective-permute-start | bytes 98312 | tf_op jit(solution)/shard_map/ppermute | solution.py:375
  3.7 18.0 %collective-permute-start.2 = (f32[64,128]{1,0:T(8,128)}, f32[64,128]{1,0:T(8,128)S(1)}, u32[]{:S(2)}, u32[]{:S(2)}) collective-permute-start(f32[64,128]{1,0:T(8,128)} %bitcast.12), channel_id=1, source_target_pairs={{8,16},{16,8},{24,32},{32,24},{40,48},{48,40},{56,64},{64,56},{72,... | collective-permute-start | bytes 98312 | tf_op jit(solution)/shard_map/ppermute | solution.py:382
  4.4 17.4 %collective-permute-start.1 = (f32[64,128]{1,0:T(8,128)}, f32[64,128]{1,0:T(8,128)S(1)}, u32[]{:S(2)}, u32[]{:S(2)}) collective-permute-start(f32[64,128]{1,0:T(8,128)} %bitcast.13), channel_id=1, source_target_pairs={{1,0},{2,1},{3,2},{4,3},{5,4},{6,5},{7,6},{9,8},{10,9},{11,10},{12... | collective-permute-start | bytes 98312 | tf_op jit(solution)/shard_map/ppermute | solution.py:375
  17.3 4.4 %collective-permute-start = (f32[64,128]{1,0:T(8,128)}, f32[64,128]{1,0:T(8,128)S(1)}, u32[]{:S(2)}, u32[]{:S(2)}) collective-permute-start(f32[64,128]{1,0:T(8,128)} %bitcast.14), channel_id=1, source_target_pairs={{0,8},{8,0},{16,24},{24,16},{32,40},{40,32},{48,56},{56,48},{64,72... | collective-permute-start | bytes 98312 | tf_op jit(solution)/shard_map/ppermute | solution.py:382
  21.7 10.7 %copy-start.1 = (bf16[64,64,160]{2,1,0:T(8,128)(2,1)S(1)}, bf16[64,64,160]{2,1,0:T(8,128)(2,1)}, u32[]{:S(2)}) copy-start(bf16[64,64,160]{2,1,0:T(8,128)(2,1)} %param.10) | copy-start | bytes 3932164
  22.8 11.1 %collective-permute-start.7 = (f32[72,128]{1,0:T(8,128)S(1)}, f32[72,128]{1,0:T(8,128)S(1)}, u32[]{:S(2)}, u32[]{:S(2)}) collective-permute-start(f32[72,128]{1,0:T(8,128)S(1)} %shard_map.65.field), channel_id=1, source_target_pairs={{0,1},{1,2},{2,3},{3,4},{4,5},{5,6},{6,7},{8,9},{9,10},{10,11},{11... | collective-permute-start | bytes 110600 | tf_op jit(solution)/shard_map/ppermute | solution.py:375
  24.7 9.1 %collective-permute-start.6 = (f32[72,128]{1,0:T(8,128)S(1)}, f32[72,128]{1,0:T(8,128)S(1)}, u32[]{:S(2)}, u32[]{:S(2)}) collective-permute-start(f32[72,128]{1,0:T(8,128)S(1)} %shard_map.65.field), channel_id=1, source_target_pairs={{8,16},{16,8},{24,32},{32,24},{40,48},{48,40},{56,64},{64,56},{72,... | collective-permute-start | bytes 110600 | tf_op jit(solution)/shard_map/ppermute | solution.py:382
  25.4 8.5 %collective-permute-start.5 = (f32[72,128]{1,0:T(8,128)S(1)}, f32[72,128]{1,0:T(8,128)S(1)}, u32[]{:S(2)}, u32[]{:S(2)}) collective-permute-start(f32[72,128]{1,0:T(8,128)S(1)} %shard_map.65.field), channel_id=1, source_target_pairs={{1,0},{2,1},{3,2},{4,3},{5,4},{6,5},{7,6},{9,8},{10,9},{11,10},{12... | collective-permute-start | bytes 110600 | tf_op jit(solution)/shard_map/ppermute | solution.py:375
  29.3 4.6 %collective-permute-start.4 = (f32[72,128]{1,0:T(8,128)S(1)}, f32[72,128]{1,0:T(8,128)S(1)}, u32[]{:S(2)}, u32[]{:S(2)}) collective-permute-start(f32[72,128]{1,0:T(8,128)S(1)} %shard_map.65.field), channel_id=1, source_target_pairs={{0,8},{8,0},{16,24},{24,16},{32,40},{40,32},{48,56},{56,48},{64,72... | collective-permute-start | bytes 110600 | tf_op jit(solution)/shard_map/ppermute | solution.py:382

commit v8 on v6

--- a/solution.py
+++ b/solution.py
@@ -59,7 +59,7 @@
 
 def pick(fields, links_ref):
     odd = lax.axis_index("plan") & 1
-    numbers = (0, 4 - odd, 3 + odd, 2, 1)
+    numbers = (0, 4 - odd, 3 + odd, 1, 2)
     picked = []
     for which in range(3):
         link = jnp.broadcast_to(links_ref[which], (BS, NB))
@@ -92,8 +92,8 @@
     lax.fori_loop(0, GROUPS, body, 0)
 
 
-def first_body(source, inner, outer, above, below, weights, links, owners, second):
-    fields = [ref[...] for ref in (source, inner, outer, above, below)]
+def first_body(source, inner, outer, below, above, weights, links, owners, second):
+    fields = [ref[...] for ref in (source, inner, outer, below, above)]
     picked = pick(fields, links)
 
     def step(tile, rows):
@@ -105,8 +105,8 @@
     second[BS:, :] = jnp.broadcast_to(owners[...].astype(F32), (SUB, NB))
 
 
-def second_body(field, inner, outer, above, below, weights, links, source, owners, sent, left):
-    fields = [ref[0:BS, :] for ref in (field, inner, outer, above, below)]
+def second_body(field, inner, outer, below, above, weights, links, source, owners, sent, left):
+    fields = [ref[0:BS, :] for ref in (field, inner, outer, below, above)]
     picked = pick(fields, links)
 
     def step(tile, rows):
@@ -130,9 +130,9 @@
         sent[copy] = packed
 
 
-def last_body(field, inner, outer, above, below, errors, weights, links, source, out, third):
+def last_body(field, inner, outer, below, above, errors, weights, links, source, out, third):
     fields = []
-    for number, ref in enumerate((field, inner, outer, above, below)):
+    for number, ref in enumerate((field, inner, outer, below, above)):
         error = errors[number]
         owner = ref[BS:, :].astype(jnp.int32)
         added = [take_lanes(error, owner + group * NC) for group in range(GROUPS)]
@@ -373,8 +373,8 @@
     errors[0] = parts[0] + near[0]
     errors[1] = parts[0] + near[1]
     errors[2] = jnp.where((place > 0) & (place < last), parts[1] + far[1], zero)
-    errors[3] = jnp.where(me < count - 1, parts[2] + received[targets[1], 1], zero)
-    errors[4] = jnp.where(me > 0, parts[3] + received[targets[2], 1], zero)
+    errors[4] = jnp.where(me < count - 1, parts[2] + received[targets[1], 1], zero)
+    errors[3] = jnp.where(me > 0, parts[3] + received[targets[2], 1], zero)
 
 
 def shifted(value, step):
@@ -393,7 +393,7 @@
 def halo(value):
     inner, outer = swapped(value, 0), swapped(value, 1)
     above, below = shifted(value, -1), shifted(value, 1)
-    return inner, outer, above, below
+    return inner, outer, below, above
 
 
 def exchange(value, axis, groups=None):

time: 94.9 us -> 92.7 us (0.977)
  blocking collectives: 50.2 us -> 47.2 us
    all_to_all x3, blocking collectives: 50.2 us -> 47.2 us  [exchange(): lax.all_to_all(value, axis, 0, 0, axis_index_groups=groups, tiled=True)]
where the time goes in v8:
time: 92.7 us; the launch traced here: 92.3 us
  blocking collectives  47.2 us (51%)
  starting transfers between devices  29.7 us (32%)
  Pallas kernels  15.1 us (16%)
    all_to_all x3, blocking collectives, exchange(): lax.all_to_all(value, axis, 0, 0, axis_index_groups=groups, tiled=True)  47.2 us
    ppermute x4, starting transfers between devices, shifted(): return lax.ppermute(value, 'height', pairs)  23.1 us
    pallas_call x6, Pallas kernels, call(): pl.pallas_call(body, out_shape=out_shape, in_specs=whole(len(inputs)), ou...  11.3 us
    ppermute x4, starting transfers between devices, swapped(): return lax.ppermute(value, 'plan', pairs)  6.63 us
    pallas_call x2, Pallas kernels, pack(): pl.pallas_call(stream_body if streamed else pack_body, out_shape=jax.Shap...  3.81 us
  transfers between devices with their start and end apart: 8, of which 0 were waited for; matrix products, arithmetic and copies ran while one was open for 0% of the time, Pallas kernels for 4%

profile of v8, /device:TPU:2, one launch (start us, length us, event | category | flops | bytes accessed | tf_op | source)
XLA Modules:
  0.0 92.3 jit_solution(14173666383268528738)
XLA Ops:
  0.0 0.0 copy-start.2
  0.0 0.0 copy-start.4
  0.0 0.0 copy-start.3
  0.0 0.0 copy-start
  0.0 15.3 %collective-permute-start.3 = (f32[64,128]{1,0:T(8,128)}, f32[64,128]{1,0:T(8,128)S(1)}, u32[]{:S(2)}, u32[]{:S(2)}) collective-permute-start(f32[64,128]{1,0:T(8,128)} %bitcast.11), channel_id=1, source_target_pairs={{1,0},{2,1},{3,2},{4,3},{5,4},{6,5},{7,6},{9,8},{10,9},{11,10},{12... | collective-permute-start | bytes 98312 | tf_op jit(solution)/shard_map/ppermute | solution.py:383
  15.4 1.9 %collective-permute-start.2 = (f32[64,128]{1,0:T(8,128)}, f32[64,128]{1,0:T(8,128)S(1)}, u32[]{:S(2)}, u32[]{:S(2)}) collective-permute-start(f32[64,128]{1,0:T(8,128)} %bitcast.12), channel_id=1, source_target_pairs={{0,1},{1,2},{2,3},{3,4},{4,5},{5,6},{6,7},{8,9},{9,10},{10,11},{11... | collective-permute-start | bytes 98312 | tf_op jit(solution)/shard_map/ppermute | solution.py:383
  17.3 0.7 collective-permute-start.1
  18.0 1.9 %collective-permute-start = (f32[64,128]{1,0:T(8,128)}, f32[64,128]{1,0:T(8,128)S(1)}, u32[]{:S(2)}, u32[]{:S(2)}) collective-permute-start(f32[64,128]{1,0:T(8,128)} %bitcast.14), channel_id=1, source_target_pairs={{0,8},{8,0},{16,24},{24,16},{32,40},{40,32},{48,56},{56,48},{64,72... | collective-permute-start | bytes 98312 | tf_op jit(solution)/shard_map/ppermute | solution.py:390
  19.9 2.4 %shard_map.64.smooth = f32[11,64,8,128]{3,2,1,0:T(8,128)S(1)} custom-call(bf16[8,8,64,176]{3,2,1,0:T(8,128)(2,1)} %bitcast.23), custom_call_target="tpu_custom_call" | custom-call | tf_op jit(solution)/shard_map/pallas_call | solution.py:215
  22.3 0.0 copy-start.1
  22.3 0.0 collective-permute-done.3.above
  22.3 0.0 collective-permute-done.2.below
  22.4 0.0 collective-permute-done.1.outer
  22.4 0.0 collective-permute-done.inner
  22.4 0.0 copy-done.2
  22.4 0.0 copy-done.4
  22.4 0.0 copy-done.3
  22.4 0.0 copy-done
  22.4 1.0 %shard_map.65.field = f32[72,128]{1,0:T(8,128)S(1)} custom-call(f32[64,128]{1,0:T(8,128)S(1)} %bitcast.15, f32[64,128]{1,0:T(8,128)S(1)} %collective-permute-done.inner, f32[64,128]{1,0:T(8,128)S(1)} %collective-permute-done.1.outer, f32[64,128]{1,0:T(8,128)S(1)} %collective-permute-done.2.below, f32[64,128]{1,0:T(8,128)S(1)} %collective-permute-done.3.above, ...), custom_call_target="tpu_custom_call" | custom-call | tf_op jit(solution)/shard_map/pallas_call | solution.py:29
  23.4 3.9 %collective-permute-start.7 = (f32[72,128]{1,0:T(8,128)S(1)}, f32[72,128]{1,0:T(8,128)S(1)}, u32[]{:S(2)}, u32[]{:S(2)}) collective-permute-start(f32[72,128]{1,0:T(8,128)S(1)} %shard_map.65.field), channel_id=1, source_target_pairs={{1,0},{2,1},{3,2},{4,3},{5,4},{6,5},{7,6},{9,8},{10,9},{11,10},{12... | collective-permute-start | bytes 110600 | tf_op jit(solution)/shard_map/ppermute | solution.py:383
  27.3 1.9 %collective-permute-start.6 = (f32[72,128]{1,0:T(8,128)S(1)}, f32[72,128]{1,0:T(8,128)S(1)}, u32[]{:S(2)}, u32[]{:S(2)}) collective-permute-start(f32[72,128]{1,0:T(8,128)S(1)} %shard_map.65.field), channel_id=1, source_target_pairs={{0,1},{1,2},{2,3},{3,4},{4,5},{5,6},{6,7},{8,9},{9,10},{10,11},{11... | collective-permute-start | bytes 110600 | tf_op jit(solution)/shard_map/ppermute | solution.py:383
  29.2 0.7 collective-permute-start.5
  29.9 3.4 %collective-permute-start.4 = (f32[72,128]{1,0:T(8,128)S(1)}, f32[72,128]{1,0:T(8,128)S(1)}, u32[]{:S(2)}, u32[]{:S(2)}) collective-permute-start(f32[72,128]{1,0:T(8,128)S(1)} %shard_map.65.field), channel_id=1, source_target_pairs={{0,8},{8,0},{16,24},{24,16},{32,40},{40,32},{48,56},{56,48},{64,72... | collective-permute-start | bytes 110600 | tf_op jit(solution)/shard_map/ppermute | solution.py:390
  33.3 0.0 copy-done.1
  33.3 1.4 %shard_map.66.ops = f32[10,64,8,128]{3,2,1,0:T(8,128)S(1)} custom-call(bf16[8,8,64,160]{3,2,1,0:T(8,128)(2,1)S(1)} %bitcast.10), custom_call_target="tpu_custom_call" | custom-call | tf_op jit(solution)/shard_map/pallas_call | solution.py:215
  34.7 0.0 collective-permute-done.7.above
  34.7 0.0 collective-permute-done.6.below
  34.7 0.0 collective-permute-done.5.outer
  34.7 0.0 collective-permute-done.4.inner
  34.8 1.2 %shard_map.67 = f32[16,8,128]{2,1,0:T(8,128)S(1)} custom-call(f32[72,128]{1,0:T(8,128)S(1)} %shard_map.65.field, f32[72,128]{1,0:T(8,128)S(1)} %collective-permute-done.4.inner, f32[72,128]{1,0:T(8,128)S(1)} %collective-permute-done.5.outer, f32[72,128]{1,0:T(8,128)S(1)} %collective-permute-done.6.below, f32[72,128]{1,0:T(8,128)S(1)} %collective-permute-done.7.above, ...), custom_call_target="tpu_custom_call" | custom-call | tf_op jit(solution)/shard_map/pallas_call | solution.py:29
  35.9 10.8 %all_to_all.15.received = f32[16,8,128]{2,1,0:T(8,128)S(1)} all-to-all(f32[16,8,128]{2,1,0:T(8,128)S(1)} %shard_map.67), channel_id=1, replica_groups={{0,8,16,24,32,40,48,56,64,72,80,88,96,104,112,120},{128,136,144,152,160..., dimensions={0} | all-to-all | bytes 131072 | tf_op jit(solution)/shard_map/all_to_all | solution.py:400
  46.7 2.1 %shard_map.68 = (f32[8,2,8,128]{3,2,1,0:T(8,128)S(1)}, f32[2,8,128]{2,1,0:T(8,128)S(1)}) custom-call(f32[10,64,8,128]{3,2,1,0:T(8,128)S(1)} %shard_map.66.ops, f32[11,64,8,128]{3,2,1,0:T(8,128)S(1)} %shard_map.64.smooth, f32[16,8,128]{2,1,0:T(8,128)S(1)} %all_to_all.15.received), custom_call_target="tpu_custom_call" | custom-call | tf_op jit(solution)/shard_map/pallas_call | solution.py:29
  48.8 21.8 %all_to_all.16.received = f32[8,2,8,128]{3,2,1,0:T(8,128)S(1)} all-to-all(f32[8,2,8,128]{3,2,1,0:T(8,128)S(1)} %get-tuple-element.21), channel_id=1, replica_groups={{0,128,256,384,512,640,768,896},{8,136,264,392,520,648,776,904},{16,144..., dimensions={0} | all-to-all | bytes 131072 | tf_op jit(solution)/shard_map/all_to_all | solution.py:400
  70.6 1.5 %shard_map.69 = (f32[8,3,8,128]{3,2,1,0:T(8,128)S(1)}, f32[2,8,128]{2,1,0:T(8,128)S(1)}) custom-call(f32[10,64,8,128]{3,2,1,0:T(8,128)S(1)} %shard_map.66.ops, f32[11,64,8,128]{3,2,1,0:T(8,128)S(1)} %shard_map.64.smooth, f32[8,2,8,128]{3,2,1,0:T(8,128)S(1)} %all_to_all.16.received, f32[2,8,128]{2,1,0:T(8,128)S(1)} %get-tuple-element.22.near), custom_call_target="tpu_custom_call" | custom-call | tf_op jit(solution)/shard_map/pallas_call | solution.py:29
  72.1 14.6 %all_to_all.17.received = f32[8,3,8,128]{3,2,1,0:T(8,128)S(1)} all-to-all(f32[8,3,8,128]{3,2,1,0:T(8,128)S(1)} %get-tuple-element.23), channel_id=1, replica_groups=mesh['plan'=128,'height'=8] {'height'}, dimensions={0} | all-to-all | bytes 196608 | tf_op jit(solution)/shard_map/all_to_all | solution.py:400
  86.7 3.9 %shard_map.70.errors = f32[5,8,128]{2,1,0:T(8,128)S(1)} custom-call(f32[10,64,8,128]{3,2,1,0:T(8,128)S(1)} %shard_map.66.ops, f32[11,64,8,128]{3,2,1,0:T(8,128)S(1)} %shard_map.64.smooth, f32[8,3,8,128]{3,2,1,0:T(8,128)S(1)} %all_to_all.17.received, f32[2,8,128]{2,1,0:T(8,128)S(1)} %get-tuple-element.22.near, f32[2,8,128]{2,1,0:T(8,128)S(1)} %get-tuple-element.24.far), custom_call_target="tpu_custom_call" | custom-call | tf_op jit(solution)/shard_map/pallas_call | solution.py:29
  90.6 1.7 %shard_map.71 = f32[64,128]{1,0:T(8,128)} custom-call(f32[72,128]{1,0:T(8,128)S(1)} %shard_map.65.field, f32[72,128]{1,0:T(8,128)S(1)} %collective-permute-done.4.inner, f32[72,128]{1,0:T(8,128)S(1)} %collective-permute-done.5.outer, f32[72,128]{1,0:T(8,128)S(1)} %collective-permute-done.6.below, f32[72,128]{1,0:T(8,128)S(1)} %collective-permute-done.7.above, ...), custom_call_target="tpu_custom_call" | custom-call | tf_op jit(solution)/shard_map/pallas_call | solution.py:29
Async XLA Ops:
  0.0 22.4 %copy-start.2 = (f32[1,1,64,128]{3,2,1,0:T(8,128)S(1)}, f32[1,1,64,128]{3,2,1,0:T(8,128)}, u32[]{:S(2)}) copy-start(f32[1,1,64,128]{3,2,1,0:T(8,128)} %param.6) | copy-start | bytes 98308
  0.0 22.4 %copy-start.4 = (s32[1,1,128]{2,1,0:T(1,128)S(1)}, s32[1,1,128]{2,1,0:T(1,128)}, u32[]{:S(2)}) copy-start(s32[1,1,128]{2,1,0:T(1,128)} %param.9) | copy-start | bytes 1540
  0.0 22.4 %copy-start.3 = (s32[1,1,3,128]{3,1,2,0:T(1,128)S(1)}, s32[1,1,3,128]{3,1,2,0:T(1,128)}, u32[]{:S(2)}) copy-start(s32[1,1,3,128]{3,1,2,0:T(1,128)} %param.8) | copy-start | bytes 4612
  0.0 22.4 %copy-start = (bf16[1,1,3,64,64,128]{5,4,3,2,1,0:T(8,128)(2,1)S(1)}, bf16[1,1,3,64,64,128]{5,4,3,2,1,0:T(8,128)(2,1)}, u32[]{:S(2)}) copy-start(bf16[1,1,3,64,64,128]{5,4,3,2,1,0:T(8,128)(2,1)} %param.7) | copy-start | bytes 9437188
  0.0 22.3 %collective-permute-start.3 = (f32[64,128]{1,0:T(8,128)}, f32[64,128]{1,0:T(8,128)S(1)}, u32[]{:S(2)}, u32[]{:S(2)}) collective-permute-start(f32[64,128]{1,0:T(8,128)} %bitcast.11), channel_id=1, source_target_pairs={{1,0},{2,1},{3,2},{4,3},{5,4},{6,5},{7,6},{9,8},{10,9},{11,10},{12... | collective-permute-start | bytes 98312 | tf_op jit(solution)/shard_map/ppermute | solution.py:383
  15.4 7.0 %collective-permute-start.2 = (f32[64,128]{1,0:T(8,128)}, f32[64,128]{1,0:T(8,128)S(1)}, u32[]{:S(2)}, u32[]{:S(2)}) collective-permute-start(f32[64,128]{1,0:T(8,128)} %bitcast.12), channel_id=1, source_target_pairs={{0,1},{1,2},{2,3},{3,4},{4,5},{5,6},{6,7},{8,9},{9,10},{10,11},{11... | collective-permute-start | bytes 98312 | tf_op jit(solution)/shard_map/ppermute | solution.py:383
  17.3 5.1 %collective-permute-start.1 = (f32[64,128]{1,0:T(8,128)}, f32[64,128]{1,0:T(8,128)S(1)}, u32[]{:S(2)}, u32[]{:S(2)}) collective-permute-start(f32[64,128]{1,0:T(8,128)} %bitcast.13), channel_id=1, source_target_pairs={{8,16},{16,8},{24,32},{32,24},{40,48},{48,40},{56,64},{64,56},{72,... | collective-permute-start | bytes 98312 | tf_op jit(solution)/shard_map/ppermute | solution.py:390
  18.0 4.4 %collective-permute-start = (f32[64,128]{1,0:T(8,128)}, f32[64,128]{1,0:T(8,128)S(1)}, u32[]{:S(2)}, u32[]{:S(2)}) collective-permute-start(f32[64,128]{1,0:T(8,128)} %bitcast.14), channel_id=1, source_target_pairs={{0,8},{8,0},{16,24},{24,16},{32,40},{40,32},{48,56},{56,48},{64,72... | collective-permute-start | bytes 98312 | tf_op jit(solution)/shard_map/ppermute | solution.py:390
  22.3 11.0 %copy-start.1 = (bf16[64,64,160]{2,1,0:T(8,128)(2,1)S(1)}, bf16[64,64,160]{2,1,0:T(8,128)(2,1)}, u32[]{:S(2)}) copy-start(bf16[64,64,160]{2,1,0:T(8,128)(2,1)} %param.10) | copy-start | bytes 3932164
  23.4 11.3 %collective-permute-start.7 = (f32[72,128]{1,0:T(8,128)S(1)}, f32[72,128]{1,0:T(8,128)S(1)}, u32[]{:S(2)}, u32[]{:S(2)}) collective-permute-start(f32[72,128]{1,0:T(8,128)S(1)} %shard_map.65.field), channel_id=1, source_target_pairs={{1,0},{2,1},{3,2},{4,3},{5,4},{6,5},{7,6},{9,8},{10,9},{11,10},{12... | collective-permute-start | bytes 110600 | tf_op jit(solution)/shard_map/ppermute | solution.py:383
  27.3 7.4 %collective-permute-start.6 = (f32[72,128]{1,0:T(8,128)S(1)}, f32[72,128]{1,0:T(8,128)S(1)}, u32[]{:S(2)}, u32[]{:S(2)}) collective-permute-start(f32[72,128]{1,0:T(8,128)S(1)} %shard_map.65.field), channel_id=1, source_target_pairs={{0,1},{1,2},{2,3},{3,4},{4,5},{5,6},{6,7},{8,9},{9,10},{10,11},{11... | collective-permute-start | bytes 110600 | tf_op jit(solution)/shard_map/ppermute | solution.py:383
  29.2 5.5 %collective-permute-start.5 = (f32[72,128]{1,0:T(8,128)S(1)}, f32[72,128]{1,0:T(8,128)S(1)}, u32[]{:S(2)}, u32[]{:S(2)}) collective-permute-start(f32[72,128]{1,0:T(8,128)S(1)} %shard_map.65.field), channel_id=1, source_target_pairs={{8,16},{16,8},{24,32},{32,24},{40,48},{48,40},{56,64},{64,56},{72,... | collective-permute-start | bytes 110600 | tf_op jit(solution)/shard_map/ppermute | solution.py:390
  29.9 4.8 %collective-permute-start.4 = (f32[72,128]{1,0:T(8,128)S(1)}, f32[72,128]{1,0:T(8,128)S(1)}, u32[]{:S(2)}, u32[]{:S(2)}) collective-permute-start(f32[72,128]{1,0:T(8,128)S(1)} %shard_map.65.field), channel_id=1, source_target_pairs={{0,8},{8,0},{16,24},{24,16},{32,40},{40,32},{48,56},{56,48},{64,72... | collective-permute-start | bytes 110600 | tf_op jit(solution)/shard_map/ppermute | solution.py:390
